TPU v7x, 32 devices: a whole 2x2x4 slice. The times are simulated.
32 devices in a mesh: parts: 2 (over x), loop: 4 (over y, core), tgrp: 4 (over z).
Axes of the slice: x: 2, y: 2, z: 4, core: 2. Of those that a mesh axis runs over, the one named last changes fastest.
Arguments:
- data: bfloat16 [8, 3, 12288], P(('parts', 'loop'), None, 'tgrp'), parts along dimension 0
- templates: bfloat16 [128, 4, 3, 2048], P('tgrp', 'loop')
- masks: int32 [128, 4], replicated, may hold values from 0 to 1, as said below
- offsets: int32 [8], P(('parts', 'loop')), parts along dimension 0, may hold values from 0 to 512, as said below
- active: int32 [8, 3], P(('parts', 'loop')), parts along dimension 0, may hold values 0 or 1
Outputs:
- detection: float32 [256, 12288], P(('parts', 'loop'), 'tgrp'), parts along dimension 0
There are 2 independent parts, one for each index of `parts`. A program takes and returns all parts, laid end to end along the dimension named above; an argument that names none is the same for every part. Nothing has to cross between parts.
Inputs may be any that keep to these rules, and one draw needn't show every extreme that they name: `masks`: every template uses at least one station. `offsets`: some station has an offset of exactly 512.
All inputs are finite; a program needn't handle non-finite values. No bound on the sum of `active` on one device may be relied on, other than what follows from the above.
Results may differ from a plain program's by a relative error of at most 0.0003.
Values may be sent and summed in bfloat16 or wider, within the bound.
No kernel may reach another device: no remote copies, remote signals or barrier semaphores. Data moves between devices by JAX's collectives and lax.ppermute only.
A program may use at most 64 MiB of HBM per device.

v0:
```python
import jax
import jax.numpy as jnp
from jax import lax
from jax.sharding import PartitionSpec as P

L = 2048


epsilon = 1e-05


def passed_along(value, axis, steps):
    count = lax.axis_size(axis)
    initial, last = (max(0, -steps), min(count, count - steps))
    return lax.ppermute(value, axis, [(source, source + steps) for source in range(initial, last)])


def window_energy(squares, out_len, span):
    inner_len = out_len + span - 128
    nblocks = (inner_len + 127) // 128
    total_len = 128 * (nblocks + 1)
    padded = jnp.concatenate([squares, jnp.zeros((total_len - squares.shape[0],), squares.dtype)])
    first = padded[: 128 * nblocks].reshape(nblocks, 128)
    second = padded[128 : 128 * nblocks + 128].reshape(nblocks, 128)
    segments = jnp.concatenate([first, second], axis=1)
    rows_at = lax.broadcasted_iota(jnp.int32, (256, 128), 0)
    cols_at = lax.broadcasted_iota(jnp.int32, (256, 128), 1)
    gap = rows_at - cols_at
    band = jnp.where((gap >= 0) & (gap < 128), 1.0, 0.0).astype(squares.dtype)
    inner = jnp.dot(segments, band, precision=lax.Precision.HIGHEST).reshape(nblocks * 128)
    energy = jnp.zeros((out_len,), squares.dtype)
    for block_at in range(span // 128):
        energy = energy + inner[128 * block_at : 128 * block_at + out_len]
    return energy


def correlate(panel, window, out_len):
    row_count = panel.shape[0]
    blocks = panel.shape[2] // 128
    span_len = out_len + panel.shape[2] - 128
    unfold = jnp.stack(
        [window[:, shift_by : shift_by + span_len] for shift_by in range(128)], axis=1
    )
    unfold = unfold.reshape(3 * 128, span_len)
    frames = (
        panel.reshape(row_count, 3, blocks, 128)
        .transpose(0, 2, 1, 3)
        .reshape(row_count, blocks, 3 * 128)
    )

    def add_block(block_at, running_sum):
        start_at = (block_at * 128).astype(jnp.int32)
        columns = lax.dynamic_slice_in_dim(unfold, start_at, out_len, 1)
        weights_now = lax.dynamic_index_in_dim(frames, block_at, 1, keepdims=False)
        return running_sum + jnp.dot(weights_now, columns, preferred_element_type=jnp.float32)

    return lax.fori_loop(0, blocks, add_block, jnp.zeros((row_count, out_len), jnp.float32))


def local(data, templates, masks, offsets, active):
    local_count = data.shape[0]
    block_len = data.shape[2]
    following = passed_along(data, "tgrp", -1)
    extended = jnp.concatenate([data, following], axis=2)
    loop_at = lax.axis_index("loop")
    first_station = loop_at * local_count
    counts = jnp.sum(masks, axis=1).astype(jnp.float32)
    local_masks = lax.dynamic_slice_in_dim(masks, first_station, local_count, 1)
    weights = local_masks.astype(jnp.float32) * jnp.sqrt(3.0 * L / counts)[:, None]
    station = 0
    channel_on = active[station].astype(jnp.bfloat16)
    series = lax.dynamic_slice(
        extended[station], (jnp.int32(0), offsets[station]), (3, block_len + L)
    )
    window = series * channel_on[:, None]
    wide_window = window.astype(jnp.float32)
    squares = jnp.sum(wide_window * wide_window, axis=0)
    energy = window_energy(squares, block_len, L)
    inv_datas = [1.0 / jnp.sqrt(energy / (3.0 * L) + epsilon)]
    windows = [window]
    channel_sets = [channel_on]
    panel_rows = lax.all_gather(templates, "tgrp", axis=0, tiled=True)
    station = 0
    panel = panel_rows[:, station] * channel_sets[station][None, :, None]
    wide_panel = panel.astype(jnp.float32)
    inv_template = 1.0 / jnp.sqrt(
        jnp.sum(wide_panel * wide_panel, axis=(1, 2)) / (3.0 * L) + epsilon
    )
    corr = correlate(panel, windows[station], block_len)
    row_weights = weights[:, station]
    row_scale = inv_template * row_weights
    stacked = corr * inv_datas[station][None, :] * row_scale[:, None] / (3.0 * L)
    rows_here = stacked.shape[0] // lax.axis_size("loop")
    summed = lax.psum(stacked, "loop")
    return lax.dynamic_slice_in_dim(summed, loop_at * rows_here, rows_here, 0)


def solution(mesh):
    placed = (
        P(("parts", "loop"), None, "tgrp"),
        P("tgrp", "loop", None, None),
        P(),
        P(("parts", "loop")),
        P(("parts", "loop"), None),
    )
    return jax.shard_map(
        local, mesh=mesh, in_specs=placed, out_specs=P(("parts", "loop"), "tgrp"), check_vma=False
    )
```

profile of v0, /device:TPU:1, one launch (start us, length us, event | category | flops | bytes accessed | tf_op | source)
XLA Modules:
  0.0 145.5 jit_solution(8335573352305815033)
XLA Ops:
  9.9 2.1 %collective-permute-done = bf16[1,3,3072]{2,1,0:T(4,128)(2,1)S(1)} collective-permute-done((bf16[1,3,3072]{2,1,0:T(4,128)(2,1)}, bf16[1,3,3072]{2,1,0:T(4,128)(2,1)S(1)}, u32[]{:S(2)}, u32[]{:S(2)}) %collective-permute-start) | collective-permute-done | bytes 18464 | tf_op jit(solution)/shard_map/ppermute | solution.py:15
  26.6 2.2 %copy.141 = bf16[3,128,4992]{2,1,0:T(8,128)(2,1)} copy(bf16[3,128,4992]{2,0,1:T(4,128)(2,1)S(1)} %constant_dynamic-update-slice_fusion) | data formatting | bytes 7667712 | tf_op jit(solution)/shard_map/stack | solution.py:41
  29.1 18.2 %all-gather.2.cloned.1.call-done = bf16[128,1,3,2048]{3,0,2,1:T(8,128)(2,1)} async-done(((bf16[32,1,3,2048]{3,0,2,1:T(8,128)(2,1)}), bf16[128,1,3,2048]{3,0,2,1:T(8,128)(2,1)}) %all-gather.2.cloned.1.call-update) | async-done | bytes 1572880 | tf_op jit(solution)/shard_map/all_gather | solution.py:82
  47.4 1.9 %copy.139 = bf16[128,1,3,2048]{0,3,2,1:T(8,128)(2,1)S(1)} copy(bf16[128,1,3,2048]{3,0,2,1:T(8,128)(2,1)} %all-gather.2.cloned.1.call-done) | data formatting | bytes 3145728 | tf_op jit(solution)/shard_map/all_gather | solution.py:82
  50.8 40.8 %while.14 = (s32[]{:T(128)}, f32[128,3072]{1,0:T(8,128)S(1)}, bf16[128,16,384]{0,2,1:T(8,128)(2,1)}, bf16[384,4992]{1,0:T(8,128)(2,1)}, s32[]{:T(128)}, /*index=5*/s32[]{:T(128)}, s32[]{:T(128)}, s32[]{:T(128)}) while((s32[]{:T(128)}, f32[128,3072]{1,0:T(8,128)S(1)}, bf16[128,16,384]{0,2,1:T(8,128)(2,1)}, ...), condition=%wide.region_1.0_spmd.clone, body=%wide.region_0.0_spmd.clone.sunk | while | flops 302776320 | bytes 5603985 | solution.py:57
  50.8 2.6 %convolution_add_fusion.2 = f32[128,3072]{1,0:T(8,128)S(1)} fusion(bf16[384,4992]{1,0:T(8,128)(2,1)} %get-tuple-element.168, s32[]{:T(128)S(6)} %select_n.34, f32[128,3072]{1,0:T(8,128)S(1)} %get-tuple-element.158, pred[]{:T(512)S(6)} %compare.3, bf16[128,16,384]{0,2,1:T(8,128)(2,1)} %get-tuple-element.167, s32[]{:T(128)} %get-tuple-element.157), kind=kOutput, calls=%fused_computation.clone.1 | convolution fusion | flops 302776320 | bytes 5603845 | tf_op jit(solution)/shard_map/while/body/eval_jaxpr/dot_general | solution.py:55
  53.4 2.5 %convolution_add_fusion.2 = f32[128,3072]{1,0:T(8,128)S(1)} fusion(bf16[384,4992]{1,0:T(8,128)(2,1)} %get-tuple-element.168, s32[]{:T(128)S(6)} %select_n.34, f32[128,3072]{1,0:T(8,128)S(1)} %get-tuple-element.158, pred[]{:T(512)S(6)} %compare.3, bf16[128,16,384]{0,2,1:T(8,128)(2,1)} %get-tuple-element.167, s32[]{:T(128)} %get-tuple-element.157), kind=kOutput, calls=%fused_computation.clone.1 | convolution fusion | flops 302776320 | bytes 5603845 | tf_op jit(solution)/shard_map/while/body/eval_jaxpr/dot_general | solution.py:55
  56.0 2.5 %convolution_add_fusion.2 = f32[128,3072]{1,0:T(8,128)S(1)} fusion(bf16[384,4992]{1,0:T(8,128)(2,1)} %get-tuple-element.168, s32[]{:T(128)S(6)} %select_n.34, f32[128,3072]{1,0:T(8,128)S(1)} %get-tuple-element.158, pred[]{:T(512)S(6)} %compare.3, bf16[128,16,384]{0,2,1:T(8,128)(2,1)} %get-tuple-element.167, s32[]{:T(128)} %get-tuple-element.157), kind=kOutput, calls=%fused_computation.clone.1 | convolution fusion | flops 302776320 | bytes 5603845 | tf_op jit(solution)/shard_map/while/body/eval_jaxpr/dot_general | solution.py:55
  58.5 2.5 %convolution_add_fusion.2 = f32[128,3072]{1,0:T(8,128)S(1)} fusion(bf16[384,4992]{1,0:T(8,128)(2,1)} %get-tuple-element.168, s32[]{:T(128)S(6)} %select_n.34, f32[128,3072]{1,0:T(8,128)S(1)} %get-tuple-element.158, pred[]{:T(512)S(6)} %compare.3, bf16[128,16,384]{0,2,1:T(8,128)(2,1)} %get-tuple-element.167, s32[]{:T(128)} %get-tuple-element.157), kind=kOutput, calls=%fused_computation.clone.1 | convolution fusion | flops 302776320 | bytes 5603845 | tf_op jit(solution)/shard_map/while/body/eval_jaxpr/dot_general | solution.py:55
  61.1 2.5 %convolution_add_fusion.2 = f32[128,3072]{1,0:T(8,128)S(1)} fusion(bf16[384,4992]{1,0:T(8,128)(2,1)} %get-tuple-element.168, s32[]{:T(128)S(6)} %select_n.34, f32[128,3072]{1,0:T(8,128)S(1)} %get-tuple-element.158, pred[]{:T(512)S(6)} %compare.3, bf16[128,16,384]{0,2,1:T(8,128)(2,1)} %get-tuple-element.167, s32[]{:T(128)} %get-tuple-element.157), kind=kOutput, calls=%fused_computation.clone.1 | convolution fusion | flops 302776320 | bytes 5603845 | tf_op jit(solution)/shard_map/while/body/eval_jaxpr/dot_general | solution.py:55
  63.6 2.5 %convolution_add_fusion.2 = f32[128,3072]{1,0:T(8,128)S(1)} fusion(bf16[384,4992]{1,0:T(8,128)(2,1)} %get-tuple-element.168, s32[]{:T(128)S(6)} %select_n.34, f32[128,3072]{1,0:T(8,128)S(1)} %get-tuple-element.158, pred[]{:T(512)S(6)} %compare.3, bf16[128,16,384]{0,2,1:T(8,128)(2,1)} %get-tuple-element.167, s32[]{:T(128)} %get-tuple-element.157), kind=kOutput, calls=%fused_computation.clone.1 | convolution fusion | flops 302776320 | bytes 5603845 | tf_op jit(solution)/shard_map/while/body/eval_jaxpr/dot_general | solution.py:55
  66.2 2.5 %convolution_add_fusion.2 = f32[128,3072]{1,0:T(8,128)S(1)} fusion(bf16[384,4992]{1,0:T(8,128)(2,1)} %get-tuple-element.168, s32[]{:T(128)S(6)} %select_n.34, f32[128,3072]{1,0:T(8,128)S(1)} %get-tuple-element.158, pred[]{:T(512)S(6)} %compare.3, bf16[128,16,384]{0,2,1:T(8,128)(2,1)} %get-tuple-element.167, s32[]{:T(128)} %get-tuple-element.157), kind=kOutput, calls=%fused_computation.clone.1 | convolution fusion | flops 302776320 | bytes 5603845 | tf_op jit(solution)/shard_map/while/body/eval_jaxpr/dot_general | solution.py:55
  68.7 2.5 %convolution_add_fusion.2 = f32[128,3072]{1,0:T(8,128)S(1)} fusion(bf16[384,4992]{1,0:T(8,128)(2,1)} %get-tuple-element.168, s32[]{:T(128)S(6)} %select_n.34, f32[128,3072]{1,0:T(8,128)S(1)} %get-tuple-element.158, pred[]{:T(512)S(6)} %compare.3, bf16[128,16,384]{0,2,1:T(8,128)(2,1)} %get-tuple-element.167, s32[]{:T(128)} %get-tuple-element.157), kind=kOutput, calls=%fused_computation.clone.1 | convolution fusion | flops 302776320 | bytes 5603845 | tf_op jit(solution)/shard_map/while/body/eval_jaxpr/dot_general | solution.py:55
  71.3 2.5 %convolution_add_fusion.2 = f32[128,3072]{1,0:T(8,128)S(1)} fusion(bf16[384,4992]{1,0:T(8,128)(2,1)} %get-tuple-element.168, s32[]{:T(128)S(6)} %select_n.34, f32[128,3072]{1,0:T(8,128)S(1)} %get-tuple-element.158, pred[]{:T(512)S(6)} %compare.3, bf16[128,16,384]{0,2,1:T(8,128)(2,1)} %get-tuple-element.167, s32[]{:T(128)} %get-tuple-element.157), kind=kOutput, calls=%fused_computation.clone.1 | convolution fusion | flops 302776320 | bytes 5603845 | tf_op jit(solution)/shard_map/while/body/eval_jaxpr/dot_general | solution.py:55
  73.8 2.5 %convolution_add_fusion.2 = f32[128,3072]{1,0:T(8,128)S(1)} fusion(bf16[384,4992]{1,0:T(8,128)(2,1)} %get-tuple-element.168, s32[]{:T(128)S(6)} %select_n.34, f32[128,3072]{1,0:T(8,128)S(1)} %get-tuple-element.158, pred[]{:T(512)S(6)} %compare.3, bf16[128,16,384]{0,2,1:T(8,128)(2,1)} %get-tuple-element.167, s32[]{:T(128)} %get-tuple-element.157), kind=kOutput, calls=%fused_computation.clone.1 | convolution fusion | flops 302776320 | bytes 5603845 | tf_op jit(solution)/shard_map/while/body/eval_jaxpr/dot_general | solution.py:55
  76.3 2.5 %convolution_add_fusion.2 = f32[128,3072]{1,0:T(8,128)S(1)} fusion(bf16[384,4992]{1,0:T(8,128)(2,1)} %get-tuple-element.168, s32[]{:T(128)S(6)} %select_n.34, f32[128,3072]{1,0:T(8,128)S(1)} %get-tuple-element.158, pred[]{:T(512)S(6)} %compare.3, bf16[128,16,384]{0,2,1:T(8,128)(2,1)} %get-tuple-element.167, s32[]{:T(128)} %get-tuple-element.157), kind=kOutput, calls=%fused_computation.clone.1 | convolution fusion | flops 302776320 | bytes 5603845 | tf_op jit(solution)/shard_map/while/body/eval_jaxpr/dot_general | solution.py:55
  78.9 2.5 %convolution_add_fusion.2 = f32[128,3072]{1,0:T(8,128)S(1)} fusion(bf16[384,4992]{1,0:T(8,128)(2,1)} %get-tuple-element.168, s32[]{:T(128)S(6)} %select_n.34, f32[128,3072]{1,0:T(8,128)S(1)} %get-tuple-element.158, pred[]{:T(512)S(6)} %compare.3, bf16[128,16,384]{0,2,1:T(8,128)(2,1)} %get-tuple-element.167, s32[]{:T(128)} %get-tuple-element.157), kind=kOutput, calls=%fused_computation.clone.1 | convolution fusion | flops 302776320 | bytes 5603845 | tf_op jit(solution)/shard_map/while/body/eval_jaxpr/dot_general | solution.py:55
  81.4 2.5 %convolution_add_fusion.2 = f32[128,3072]{1,0:T(8,128)S(1)} fusion(bf16[384,4992]{1,0:T(8,128)(2,1)} %get-tuple-element.168, s32[]{:T(128)S(6)} %select_n.34, f32[128,3072]{1,0:T(8,128)S(1)} %get-tuple-element.158, pred[]{:T(512)S(6)} %compare.3, bf16[128,16,384]{0,2,1:T(8,128)(2,1)} %get-tuple-element.167, s32[]{:T(128)} %get-tuple-element.157), kind=kOutput, calls=%fused_computation.clone.1 | convolution fusion | flops 302776320 | bytes 5603845 | tf_op jit(solution)/shard_map/while/body/eval_jaxpr/dot_general | solution.py:55
  84.0 2.5 %convolution_add_fusion.2 = f32[128,3072]{1,0:T(8,128)S(1)} fusion(bf16[384,4992]{1,0:T(8,128)(2,1)} %get-tuple-element.168, s32[]{:T(128)S(6)} %select_n.34, f32[128,3072]{1,0:T(8,128)S(1)} %get-tuple-element.158, pred[]{:T(512)S(6)} %compare.3, bf16[128,16,384]{0,2,1:T(8,128)(2,1)} %get-tuple-element.167, s32[]{:T(128)} %get-tuple-element.157), kind=kOutput, calls=%fused_computation.clone.1 | convolution fusion | flops 302776320 | bytes 5603845 | tf_op jit(solution)/shard_map/while/body/eval_jaxpr/dot_general | solution.py:55
  86.5 2.5 %convolution_add_fusion.2 = f32[128,3072]{1,0:T(8,128)S(1)} fusion(bf16[384,4992]{1,0:T(8,128)(2,1)} %get-tuple-element.168, s32[]{:T(128)S(6)} %select_n.34, f32[128,3072]{1,0:T(8,128)S(1)} %get-tuple-element.158, pred[]{:T(512)S(6)} %compare.3, bf16[128,16,384]{0,2,1:T(8,128)(2,1)} %get-tuple-element.167, s32[]{:T(128)} %get-tuple-element.157), kind=kOutput, calls=%fused_computation.clone.1 | convolution fusion | flops 302776320 | bytes 5603845 | tf_op jit(solution)/shard_map/while/body/eval_jaxpr/dot_general | solution.py:55
  89.1 2.5 %convolution_add_fusion.2 = f32[128,3072]{1,0:T(8,128)S(1)} fusion(bf16[384,4992]{1,0:T(8,128)(2,1)} %get-tuple-element.168, s32[]{:T(128)S(6)} %select_n.34, f32[128,3072]{1,0:T(8,128)S(1)} %get-tuple-element.158, pred[]{:T(512)S(6)} %compare.3, bf16[128,16,384]{0,2,1:T(8,128)(2,1)} %get-tuple-element.167, s32[]{:T(128)} %get-tuple-element.157), kind=kOutput, calls=%fused_computation.clone.1 | convolution fusion | flops 302776320 | bytes 5603845 | tf_op jit(solution)/shard_map/while/body/eval_jaxpr/dot_general | solution.py:55
  92.9 1.4 multiply_multiply_fusion
  94.3 42.6 %all-reduce.2.cloned.1.call-done = f32[128,3072]{1,0:T(8,128)} async-done(((f32[128,3072]{1,0:T(8,128)}), f32[128,3072]{1,0:T(8,128)}) %all-reduce.2.cloned.1.call-update) | async-done | bytes 1572880 | tf_op jit(solution)/shard_map/psum | solution.py:94
  136.9 1.8 %constant_dynamic-slice_fusion = f32[32,3072]{1,0:T(8,128)} fusion(f32[128,3072]{1,0:T(8,128)} %all-reduce.2.cloned.1.call-done, s32[]{:T(128)S(6)} %select_n.29), kind=kLoop, calls=%fused_computation.305 | loop fusion | bytes 786436 | tf_op jit(solution)/shard_map/dynamic_slice | solution.py:95
  (146 shorter events, 19.9 us)
Async XLA Ops:
  6.5 40.8 %all-gather.2.cloned.1.call-start = ((), (), s32[]{:S(2)}) async-start(), calls=%async_computation | async-start | bytes 1966080 | tf_op jit(solution)/shard_map/all_gather | solution.py:82
  6.5 5.4 %collective-permute-start = (bf16[1,3,3072]{2,1,0:T(4,128)(2,1)}, bf16[1,3,3072]{2,1,0:T(4,128)(2,1)S(1)}, u32[]{:S(2)}, u32[]{:S(2)}) collective-permute-start(bf16[1,3,3072]{2,1,0:T(4,128)(2,1)} %param.7), channel_id=1, source_target_pairs={{1,0},{2,1},{3,2},{5,4},{6,5},{7,6},{9,8},{10,9},{11,10},{13,12},{... | collective-permute-start | bytes 55304 | tf_op jit(solution)/shard_map/ppermute | solution.py:15
  7.8 129.0 %all-reduce.2.cloned.1.call-start = ((), (), s32[]{:S(2)}) async-start(), calls=%async_computation.1 | async-start | bytes 3145728 | tf_op jit(solution)/shard_map/psum | solution.py:94
  50.8 40.8 %copy-start = (bf16[128,1,3,2048]{3,0,2,1:T(8,128)(2,1)S(1)}, bf16[128,1,3,2048]{3,0,2,1:T(8,128)(2,1)}, u32[]{:S(2)}) copy-start(bf16[128,1,3,2048]{3,0,2,1:T(8,128)(2,1)} %all-gather.2.cloned.1.call-done) | copy-start | bytes 4718596
Sparse Core Ops, SparseCore 0:
  8.9 38.4 all-gather.1
  94.4 42.4 all-reduce.1
where the time goes:
time: 147 us; the launch traced here: 145 us
  waiting for transfers between devices  62.9 us (43%)
  matrix products  40.6 us (28%)
  local copies, waits for them, and re-layouts  20.4 us (14%)
  between operations  14.6 us (10%)
  other arithmetic  5.18 us (4%)
    psum x1, waiting for transfers between devices, local(): summed = lax.psum(stacked, 'loop')  42.6 us
    dot_general x16, matrix products, add_block(): jnp.dot(weights_now, columns, preferred_element_type=jnp.float32)  40.3 us
    all_gather x1, waiting for transfers between devices, local(): panel_rows = lax.all_gather(templates, 'tgrp', axis=0, tiled=True)  18.2 us
    unnamed x129, local copies, waits for them, and re-layouts  13.1 us
  transfers between devices with their start and end apart: 3, of which 3 were waited for; matrix products, arithmetic and copies ran while one was open for 12% of the time, Pallas kernels for 0%

commit v1 on v0

--- a/solution.py
+++ b/solution.py
@@ -1,6 +1,10 @@
+import functools
+
 import jax
 import jax.numpy as jnp
 from jax import lax
+from jax.experimental import pallas as pl
+from jax.experimental.pallas import tpu as pltpu
 from jax.sharding import PartitionSpec as P
 
 L = 2048
@@ -57,7 +61,7 @@
     return lax.fori_loop(0, blocks, add_block, jnp.zeros((row_count, out_len), jnp.float32))
 
 
-def local(data, templates, masks, offsets, active):
+def local_general(data, templates, masks, offsets, active):
     local_count = data.shape[0]
     block_len = data.shape[2]
     following = passed_along(data, "tgrp", -1)
@@ -95,6 +99,258 @@
     return lax.dynamic_slice_in_dim(summed, loop_at * rows_here, rows_here, 0)
 
 
+ROWS = 16
+SHIFTS = 16
+
+
+def lanes(shape):
+    return lax.broadcasted_iota(jnp.int32, shape, len(shape) - 1)
+
+
+def split_kernel(active, t_ref, d_ref, keep_ref, send_ref, rows_ref, scratch):
+    half = lax.axis_index("loop") // 2
+    for c in range(3):
+        on = active[0, c].astype(jnp.float32)
+        for out, first in ((keep_ref, half), (send_ref, 1 - half)):
+            rows = t_ref[c, pl.ds(pl.multiple_of(ROWS * first, ROWS), ROWS), :]
+            out[c] = (rows.astype(jnp.float32) * on).astype(jnp.bfloat16)
+    blocks = d_ref.shape[2] // 128
+    wide = d_ref[0].astype(jnp.float32)
+    scratch[3 * blocks :] = jnp.zeros((scratch.shape[0] - 3 * blocks, 128), jnp.float32)
+    for c in range(3):
+        for j in range(blocks):
+            scratch[c * blocks + j : c * blocks + j + 1] = wide[c : c + 1, 128 * j : 128 * j + 128]
+    rows_ref[...] = scratch[...].astype(jnp.bfloat16)
+
+
+def split(active, panel, data):
+    blocks = data.shape[2] // 128
+    padded = (3 * blocks + 15) // 16 * 16
+    half = jax.ShapeDtypeStruct((3, ROWS, panel.shape[2]), jnp.bfloat16)
+    return pl.pallas_call(
+        split_kernel,
+        out_shape=(half, half, jax.ShapeDtypeStruct((padded, 128), jnp.bfloat16)),
+        in_specs=[pl.BlockSpec(memory_space=pltpu.SMEM)] + [pl.BlockSpec(memory_space=pltpu.VMEM)] * 2,
+        out_specs=(pl.BlockSpec(memory_space=pltpu.VMEM),) * 3,
+        scratch_shapes=[pltpu.VMEM((padded, 128), jnp.float32)],
+        name="split",
+    )(active, panel, data)
+
+
+def series_kernel(blocks, offset, active, d0, d1, d2, d3, x_ref, whole):
+    z = lax.axis_index("tgrp")
+    rows = x_ref.shape[1]
+    for c in range(3):
+        whole[c, 4 * blocks :] = jnp.zeros((whole.shape[1] - 4 * blocks, 128), jnp.float32)
+    for b, ref in enumerate((d0, d1, d2, d3)):
+        wide = ref[...].astype(jnp.float32)
+        at = pl.multiple_of(blocks * (z ^ b), 8)
+        for c in range(3):
+            whole[c, pl.ds(at, blocks), :] = wide[c * blocks : c * blocks + blocks]
+    row, lane = offset[0] // 128, offset[0] % 128
+    spill = lanes((rows, 128)) >= 128 - lane
+    for c in range(3):
+        on = active[0, c].astype(jnp.float32)
+        here = pltpu.roll(whole[c, pl.ds(row, rows), :], 128 - lane, 1)
+        after = pltpu.roll(whole[c, pl.ds(row + 1, rows), :], 128 - lane, 1)
+        x_ref[c] = (jnp.where(spill, after, here) * on).astype(jnp.bfloat16)
+
+
+def make_series(offset, active, pieces, blocks, rows):
+    return pl.pallas_call(
+        functools.partial(series_kernel, blocks),
+        out_shape=jax.ShapeDtypeStruct((3, rows, 128), jnp.bfloat16),
+        in_specs=[pl.BlockSpec(memory_space=pltpu.SMEM)] * 2 + [pl.BlockSpec(memory_space=pltpu.VMEM)] * 4,
+        out_specs=pl.BlockSpec(memory_space=pltpu.VMEM),
+        scratch_shapes=[pltpu.VMEM((3, rows + 8, 128), jnp.float32)],
+        name="series",
+    )(offset, active, *pieces)
+
+
+def correlate_kernel(span, nb, t0, t1, t2, t3, x0, x1, x2, x3, masks, first_ref, second_ref,
+                     tp_ref, xf_ref, a_ref, z_ref, d_ref, rs_ref, acc_ref, tot_ref, tr_ref):
+    ts, xs = (t0, t1, t2, t3), (x0, x1, x2, x3)
+    lb = span // 128
+    kb = lb + 1
+    rows = xf_ref.shape[1]
+    loop_at = lax.axis_index("loop")
+    half, core = loop_at // 2, loop_at % 2
+    k_first = 2 * ROWS * lax.axis_index("tgrp") + ROWS * half
+    lane = lanes((8, 128))
+    sub = lax.broadcasted_iota(jnp.int32, (8, 128), 0)
+    counts = jnp.sum(masks[...], axis=0, keepdims=True).astype(jnp.float32)
+    weight = jnp.sqrt(3.0 * span / counts)
+    own = k_first + lane % ROWS
+    diagonal = lanes((ROWS, 128)) % ROWS == lax.broadcasted_iota(jnp.int32, (ROWS, 128), 0)
+    lane_r = lanes((rows, 128))
+    for s in range(4):
+        norm = jnp.zeros((ROWS, 128), jnp.float32)
+        squares = jnp.zeros((rows, 128), jnp.float32)
+        for c in range(3):
+            i = 3 * s + c
+            t = ts[s][c]
+            tp_ref[i, :, 0:128] = jnp.zeros((ROWS, 128), jnp.bfloat16)
+            tp_ref[i, :, 128 : 128 + span] = t
+            tp_ref[i, :, 128 + span :] = jnp.zeros((ROWS, 128), jnp.bfloat16)
+            wide = t.astype(jnp.float32)
+            wide = wide * wide
+            for b in range(lb):
+                norm = norm + wide[:, 128 * b : 128 * b + 128]
+            x = xs[s][c, pl.ds(pl.multiple_of(2 * nb * core, 16), rows), :].astype(jnp.float32)
+            xf_ref[i] = x
+            squares = squares + x * x
+        inverse = 1.0 / jnp.sqrt(jnp.sum(norm, axis=1, keepdims=True) / (3.0 * span) + epsilon)
+        inverse = jnp.where(diagonal, jnp.broadcast_to(inverse, (ROWS, 128)), 0.0)
+        inverse = jnp.sum(inverse, axis=0, keepdims=True)
+        here = masks[pl.ds(loop_at ^ s, 1), :].astype(jnp.float32) * weight
+        here = jnp.take_along_axis(jnp.broadcast_to(here, (8, 128)), own, axis=1)
+        rs_ref[s] = here[0:1] * inverse / (3.0 * span)
+        b = 1
+        while b < 128:
+            after = pltpu.roll(squares, rows - 1, 0)
+            squares = squares + pltpu.roll(jnp.where(lane_r < b, after, squares), 128 - b, 1)
+            b *= 2
+        b = 1
+        while b < lb:
+            squares = squares + pltpu.roll(squares, rows - b, 0)
+            b *= 2
+        d_ref[s] = 1.0 / jnp.sqrt(squares / (3.0 * span) + epsilon)
+
+    from_lane = (lane + sub) % 128
+    inside = lane + sub < 128
+
+    def build(i, slot):
+        for r in range(SHIFTS):
+            n = ROWS * (8 * (r % 2) + r // 2)
+            a_ref[slot, n : n + ROWS, :] = tp_ref[i, :, 128 - 8 * r : 128 - 8 * r + 128 * kb]
+
+        def turned(j):
+            row = xf_ref[i, pl.ds(j, 8, stride=0), :]
+            return jnp.take_along_axis(row, from_lane, axis=1)
+
+        before, tiles = turned(0), []
+        for j in range(2 * nb + lb):
+            after = turned(j + 1)
+            tiles.append(jnp.where(inside, before, after))
+            before = after
+            if j >= nb:
+                z_ref[slot, j - nb] = jnp.concatenate([tiles[j - nb], tiles[j]], axis=0).astype(jnp.bfloat16)
+
+    def product(slot):
+        left = jnp.concatenate([z_ref[slot, b : b + nb].reshape(16 * nb, 128) for b in range(kb)], axis=1)
+        return lax.dot_general(left, a_ref[slot], (((1,), (1,)), ((), ())), preferred_element_type=jnp.float32)
+
+    def weighted(s):
+        for v in (0, 1):
+            index = 16 * (lane // 16) + 8 * v + sub
+            rs = rs_ref[s]
+            for j in range(nb):
+                for h in (0, 1):
+                    at = 16 * j + 8 * h
+                    scale = jnp.take_along_axis(d_ref[s, pl.ds(j + nb * h, 8, stride=0), :], index, axis=1) * rs
+                    tot_ref[v, at : at + 8, :] += acc_ref[at : at + 8, 128 * v : 128 * v + 128] * scale
+
+    tot_ref[...] = jnp.zeros(tot_ref.shape, jnp.float32)
+    build(0, 0)
+
+    def station(s, carry):
+        for c in range(3):
+            m = product(c)
+            build(jnp.minimum(3 * s + c + 1, 11), (c + 1) % 3)
+            if c == 0:
+                acc_ref[...] = m
+            else:
+                acc_ref[...] += m
+        weighted(s)
+        return carry
+
+    lax.fori_loop(0, 4, station, 0)
+
+    for f, out in enumerate((first_ref, second_ref)):
+        h = half ^ f
+        for jb in range(nb // 8):
+            v = [[tot_ref[q, pl.ds(128 * jb + 8 * h + p, 8, stride=16), :] for p in range(8)] for q in (0, 1)]
+            for b in (1, 2, 4):
+                upper = (lane // b) % 2 == 1
+                for q in (0, 1):
+                    for p in range(8):
+                        if not p & b:
+                            x, y = v[q][p], v[q][p + b]
+                            v[q][p] = jnp.where(upper, pltpu.roll(y, b, 1), x)
+                            v[q][p + b] = jnp.where(upper, y, pltpu.roll(x, 128 - b, 1))
+            upper = (lane // 8) % 2 == 1
+            for p in range(8):
+                x, y = v[0][p], v[1][p]
+                v[0][p] = jnp.where(upper, pltpu.roll(y, 8, 1), x)
+                v[1][p] = jnp.where(upper, y, pltpu.roll(x, 120, 1))
+            for q in (0, 1):
+                for p in range(8):
+                    at = nb * (8 * q + p) + 8 * jb
+                    tr_ref[f, at : at + 8, :] = v[q][p]
+        for j in range(nb):
+            for q in (0, 1):
+                out[8 * q : 8 * q + 8, 128 * j : 128 * j + 128] = tr_ref[f, pl.ds(8 * nb * q + j, 8, stride=nb), :]
+
+
+def correlate_stations(panels, series, masks, span, nb):
+    lb = span // 128
+    rows = 2 * nb + lb + 8
+    block = jax.ShapeDtypeStruct((ROWS, 128 * nb), jnp.float32)
+    vmem = pl.BlockSpec(memory_space=pltpu.VMEM)
+    return pl.pallas_call(
+        functools.partial(correlate_kernel, span, nb),
+        out_shape=(block, block),
+        in_specs=[vmem] * 9,
+        out_specs=(vmem, vmem),
+        scratch_shapes=[
+            pltpu.VMEM((12, ROWS, span + 256), jnp.bfloat16),
+            pltpu.VMEM((12, rows, 128), jnp.float32),
+            pltpu.VMEM((3, ROWS * SHIFTS, span + 128), jnp.bfloat16),
+            pltpu.VMEM((3, nb + lb, 16, 128), jnp.bfloat16),
+            pltpu.VMEM((4, rows, 128), jnp.float32),
+            pltpu.VMEM((4, 1, 128), jnp.float32),
+            pltpu.VMEM((16 * nb, 256), jnp.float32),
+            pltpu.VMEM((2, 16 * nb, 128), jnp.float32),
+            pltpu.VMEM((2, 16 * nb, 128), jnp.float32),
+        ],
+        compiler_params=pltpu.CompilerParams(vmem_limit_bytes=40 << 20),
+        name="correlate",
+    )(*panels, *series, masks)
+
+
+def swapped(value, loop_bits, tgrp_bits):
+    pairs = [(4 * l + z, 4 * (l ^ loop_bits) + (z ^ tgrp_bits)) for l in range(4) for z in range(4)]
+    return lax.ppermute(value, ("loop", "tgrp"), pairs)
+
+
+def to_owner(value, flip):
+    pairs = [(4 * l + z, 4 * z + 2 * (l % 2) + ((l // 2) ^ flip)) for l in range(4) for z in range(4)]
+    return lax.ppermute(value, ("loop", "tgrp"), pairs)
+
+
+def local_plane(data, templates, masks, offsets, active):
+    span = templates.shape[3]
+    nb = data.shape[2] // 128
+    panel = templates[:, 0].transpose(1, 0, 2)
+    keep, send, pieces = split(active, panel, data)
+    panel_y = swapped(send, 2, 0)
+    panel_c = swapped(keep, 1, 0)
+    d1 = swapped(pieces, 0, 1)
+    d2 = swapped(pieces, 0, 2)
+    d3 = swapped(d1, 0, 2)
+    series = make_series(offsets, active, (pieces, d1, d2, d3), nb, 4 * nb + span // 128 + 8)
+    series_y = swapped(series, 2, 0)
+    series_c = swapped(series, 1, 0)
+    series_yc = swapped(series_y, 1, 0)
+    panel_yc = swapped(panel_y, 1, 0)
+    first, second = correlate_stations(
+        (keep, panel_c, panel_y, panel_yc), (series, series_c, series_y, series_yc), masks.T, span, nb
+    )
+    first, second = to_owner(first, 0), to_owner(second, 1)
+    odd = lax.axis_index("tgrp") % 2 == 1
+    return jnp.concatenate([jnp.where(odd, second, first), jnp.where(odd, first, second)], axis=0)
+
+
 def solution(mesh):
     placed = (
         P(("parts", "loop"), None, "tgrp"),
@@ -103,6 +359,14 @@
         P(("parts", "loop")),
         P(("parts", "loop"), None),
     )
+
+    def local(data, templates, masks, offsets, active):
+        grid = (mesh.shape["loop"], mesh.shape["tgrp"])
+        fits = grid == (4, 4) and templates.shape[:2] == (2 * ROWS, 1) and masks.shape[0] == 128
+        fits = fits and templates.shape[3] == 2048 and data.shape[0] == 1 and data.shape[2] % 1024 == 0
+        plan = local_plane if fits else local_general
+        return plan(data, templates, masks, offsets, active)
+
     return jax.shard_map(
         local, mesh=mesh, in_specs=placed, out_specs=P(("parts", "loop"), "tgrp"), check_vma=False
     )

time: 147 us -> 47.6 us (0.32)
  waiting for transfers between devices: 62.9 us -> 12.1 us
  matrix products: 40.6 us -> 0 us
  local copies, waits for them, and re-layouts: 20.4 us -> 3 us
  starting transfers between devices: 1.32 us -> 18.7 us
  between operations: 14.6 us -> 0.72 us
  Pallas kernels: 0 us -> 11.9 us
  other arithmetic: 5.18 us -> 0.8 us
    psum x1 -> x0, waiting for transfers between devices: 42.6 us -> none  [local(): summed = lax.psum(stacked, 'loop')]
    dot_general x17 -> x0, matrix products: 40.6 us -> none  [the longest x16 40.3 us: add_block(): jnp.dot(weights_now, columns, preferred_element_type=jnp.float32)]
    all_gather x1 -> x0, waiting for transfers between devices: 18.2 us -> none  [local(): panel_rows = lax.all_gather(templates, 'tgrp', axis=0, tiled=True)]
    ppermute x1 -> x11, starting transfers between devices: 1.28 us -> 18.7 us  [the longest x9 13.3 us: swapped(): return lax.ppermute(value, ('loop', 'tgrp'), pairs)]
    pallas_call x0 -> x3, Pallas kernels: none -> 11.9 us  [the longest x1 8.48 us: correlate_stations(): pl.pallas_call(functools.partial(correlate_kernel, span, nb), out_shape=(...]
    unnamed x129 -> x12, local copies, waits for them, and re-layouts: 13.1 us -> 3 us
    ppermute x1 -> x11, waiting for transfers between devices: 2.06 us -> 12.1 us  [the longest x2 9.08 us: to_owner(): return lax.ppermute(value, ('loop', 'tgrp'), pairs)]
    another operation x2 -> x0, local copies, waits for them, and re-layouts: 2.34 us -> none  [correlate(): jnp.stack([window[:, shift_by:shift_by + span_len] for shift_by in range(...]
  transfers between devices with their start and end apart: 3 -> 11, of which waited for: 3 -> 4; matrix products, arithmetic and copies ran while one was open for 12% -> 0% of each run, Pallas kernels for 0% -> 3%
where the time goes in v1:
time: 47.6 us; the launch traced here: 47.3 us
  starting transfers between devices  18.7 us (39%)
  waiting for transfers between devices  12.1 us (25%)
  Pallas kernels  11.9 us (25%)
  local copies, waits for them, and re-layouts  3 us (6%)
  other arithmetic  0.8 us (2%)
  between operations  0.72 us (2%)
    ppermute x9, starting transfers between devices, swapped(): return lax.ppermute(value, ('loop', 'tgrp'), pairs)  13.3 us
    ppermute x2, waiting for transfers between devices, to_owner(): return lax.ppermute(value, ('loop', 'tgrp'), pairs)  9.08 us
    pallas_call x1, Pallas kernels, correlate_stations(): pl.pallas_call(functools.partial(correlate_kernel, span, nb), out_shape=(...  8.48 us
    ppermute x2, starting transfers between devices, to_owner(): return lax.ppermute(value, ('loop', 'tgrp'), pairs)  5.47 us
    ppermute x9, waiting for transfers between devices, swapped(): return lax.ppermute(value, ('loop', 'tgrp'), pairs)  3.05 us
    unnamed x12, local copies, waits for them, and re-layouts  3 us
    pallas_call x1, Pallas kernels, split(): pl.pallas_call(split_kernel, out_shape=(half, half, jax.ShapeDtypeStruct(...  1.81 us
    pallas_call x1, Pallas kernels, make_series(): pl.pallas_call(functools.partial(series_kernel, blocks), out_shape=jax.Sh...  1.62 us
  transfers between devices with their start and end apart: 11, of which 4 were waited for; matrix products, arithmetic and copies ran while one was open for 0% of the time, Pallas kernels for 3%

profile of v1, /device:TPU:1, one launch (start us, length us, event | category | flops | bytes accessed | tf_op | source)
XLA Modules:
  0.0 47.3 jit_solution(16900453646675076085)
XLA Ops:
  0.0 1.8 %split.1 = (bf16[3,16,2048]{2,1,0:T(8,128)(2,1)}, bf16[3,16,2048]{2,1,0:T(8,128)(2,1)}, bf16[80,128]{1,0:T(8,128)(2,1)}) custom-call(s32[1,3]{1,0:T(1,128)} %active.3, bf16[3,32,2048]{2,1,0:T(8,128)(2,1)} %bitcast.5, bf16[1,3,3072]{2,1,0:T(4,128)(2,1)} %d_ref.1), custom_call_target="tpu_custom_call" | custom-call | tf_op jit(solution)/shard_map/split/pallas_call | solution.py:130
  1.8 2.1 %collective-permute-start.1 = (bf16[3,16,2048]{2,1,0:T(8,128)(2,1)}, bf16[3,16,2048]{2,1,0:T(8,128)(2,1)S(1)}, u32[]{:S(2)}, u32[]{:S(2)}) collective-permute-start(bf16[3,16,2048]{2,1,0:T(8,128)(2,1)} %get-tuple-element.11), channel_id=1, source_target_pairs={{0,8},{1,9},{2,10},{3,11},{4,12},{5,13},{6,14},{7,15},{8,0},{9,1},... | collective-permute-start | bytes 589832 | tf_op jit(solution)/shard_map/ppermute | solution.py:323
  3.9 1.3 %collective-permute-start.3 = (bf16[80,128]{1,0:T(8,128)(2,1)}, bf16[80,128]{1,0:T(8,128)(2,1)S(1)}, u32[]{:S(2)}, u32[]{:S(2)}) collective-permute-start(bf16[80,128]{1,0:T(8,128)(2,1)} %get-tuple-element.12.d0), channel_id=1, source_target_pairs={{0,1},{1,0},{2,3},{3,2},{4,5},{5,4},{6,7},{7,6},{8,9},{9,8},{10,11... | collective-permute-start | bytes 61448 | tf_op jit(solution)/shard_map/ppermute | solution.py:323
  5.2 2.3 %collective-permute-start.4 = (bf16[80,128]{1,0:T(8,128)(2,1)}, bf16[80,128]{1,0:T(8,128)(2,1)S(1)}, u32[]{:S(2)}, u32[]{:S(2)}) collective-permute-start(bf16[80,128]{1,0:T(8,128)(2,1)} %get-tuple-element.12.d0), channel_id=1, source_target_pairs={{0,2},{1,3},{2,0},{3,1},{4,6},{5,7},{6,4},{7,5},{8,10},{9,11},{10,... | collective-permute-start | bytes 61448 | tf_op jit(solution)/shard_map/ppermute | solution.py:323
  7.5 1.8 %collective-permute-start.5 = (bf16[80,128]{1,0:T(8,128)(2,1)S(1)}, bf16[80,128]{1,0:T(8,128)(2,1)S(1)}, u32[]{:S(2)}, u32[]{:S(2)}) collective-permute-start(bf16[80,128]{1,0:T(8,128)(2,1)S(1)} %collective-permute-done.3.d1), channel_id=1, source_target_pairs={{0,2},{1,3},{2,0},{3,1},{4,6},{5,7},{6,4},{7,5},{8,10},{9,11},{10,... | collective-permute-start | bytes 61448 | tf_op jit(solution)/shard_map/ppermute | solution.py:323
  9.3 2.1 %collective-permute-start = (bf16[3,16,2048]{2,1,0:T(8,128)(2,1)}, bf16[3,16,2048]{2,1,0:T(8,128)(2,1)S(1)}, u32[]{:S(2)}, u32[]{:S(2)}) collective-permute-start(bf16[3,16,2048]{2,1,0:T(8,128)(2,1)} %get-tuple-element.10.t0), channel_id=1, source_target_pairs={{0,4},{1,5},{2,6},{3,7},{4,0},{5,1},{6,2},{7,3},{8,12},{9,13},{10,... | collective-permute-start | bytes 589832 | tf_op jit(solution)/shard_map/ppermute | solution.py:323
  11.4 0.0 collective-permute-start.2
  12.1 0.0 collective-permute-done.4.d2
  12.1 0.6 %copy-done.4 = bf16[80,128]{1,0:T(8,128)(2,1)} copy-done((bf16[80,128]{1,0:T(8,128)(2,1)}, bf16[80,128]{1,0:T(8,128)(2,1)S(1)}, u32[]{:S(2)}) %copy-start.4) | copy-done | bytes 20504
  12.7 0.6 %copy-done.5 = bf16[80,128]{1,0:T(8,128)(2,1)} copy-done((bf16[80,128]{1,0:T(8,128)(2,1)}, bf16[80,128]{1,0:T(8,128)(2,1)S(1)}, u32[]{:S(2)}) %copy-start.5) | copy-done | bytes 20504
  13.3 1.6 %series.1.x0 = bf16[3,120,128]{2,1,0:T(8,128)(2,1)} custom-call(s32[1]{0:T(128)S(6)} %copy.6.offset, s32[1,3]{1,0:T(1,128)} %active.3, bf16[80,128]{1,0:T(8,128)(2,1)} %get-tuple-element.12.d0, bf16[80,128]{1,0:T(8,128)(2,1)} %copy-done.3, bf16[80,128]{1,0:T(8,128)(2,1)} %copy-done.4, bf16[80,128]{1,0:T(8,128)(2,1)} %copy-done.5), custom_call_target="tpu_custom_call" | custom-call | tf_op jit(solution)/shard_map/series/pallas_call | solution.py:160
  14.9 0.2 collective-permute-start.7
  15.1 1.3 %collective-permute-start.6 = (bf16[3,120,128]{2,1,0:T(8,128)(2,1)}, bf16[3,120,128]{2,1,0:T(8,128)(2,1)S(1)}, u32[]{:S(2)}, u32[]{:S(2)}) collective-permute-start(bf16[3,120,128]{2,1,0:T(8,128)(2,1)} %series.1.x0), channel_id=1, source_target_pairs={{0,4},{1,5},{2,6},{3,7},{4,0},{5,1},{6,2},{7,3},{8,12},{9,13},{10,... | collective-permute-start | bytes 276488 | tf_op jit(solution)/shard_map/ppermute | solution.py:323
  16.4 2.1 %collective-permute-done.7.x2 = bf16[3,120,128]{2,1,0:T(8,128)(2,1)S(1)} collective-permute-done((bf16[3,120,128]{2,1,0:T(8,128)(2,1)}, bf16[3,120,128]{2,1,0:T(8,128)(2,1)S(1)}, u32[]{:S(2)}, u32[]{:S(2)}) %collective-permute-start.7) | collective-permute-done | bytes 92192 | tf_op jit(solution)/shard_map/ppermute | solution.py:323
  18.5 2.2 %collective-permute-start.8 = (bf16[3,120,128]{2,1,0:T(8,128)(2,1)S(1)}, bf16[3,120,128]{2,1,0:T(8,128)(2,1)S(1)}, u32[]{:S(2)}, u32[]{:S(2)}) collective-permute-start(bf16[3,120,128]{2,1,0:T(8,128)(2,1)S(1)} %collective-permute-done.7.x2), channel_id=1, source_target_pairs={{0,4},{1,5},{2,6},{3,7},{4,0},{5,1},{6,2},{7,3},{8,12},{9,13},{10,... | collective-permute-start | bytes 276488 | tf_op jit(solution)/shard_map/ppermute | solution.py:323
  20.7 0.9 %collective-permute-done.8.x3 = bf16[3,120,128]{2,1,0:T(8,128)(2,1)S(1)} collective-permute-done((bf16[3,120,128]{2,1,0:T(8,128)(2,1)S(1)}, bf16[3,120,128]{2,1,0:T(8,128)(2,1)S(1)}, u32[]{:S(2)}, u32[]{:S(2)}) %collective-permute-start.8) | collective-permute-done | bytes 92192 | tf_op jit(solution)/shard_map/ppermute | solution.py:323
  21.6 0.9 %copy-done = bf16[3,120,128]{2,1,0:T(8,128)(2,1)S(1)} copy-done((bf16[3,120,128]{2,1,0:T(8,128)(2,1)S(1)}, bf16[3,120,128]{2,1,0:T(8,128)(2,1)}, u32[]{:S(2)}) %copy-start) | copy-done | bytes 92184
  22.5 0.9 %copy-done.1 = bf16[3,16,2048]{2,1,0:T(8,128)(2,1)S(1)} copy-done((bf16[3,16,2048]{2,1,0:T(8,128)(2,1)S(1)}, bf16[3,16,2048]{2,1,0:T(8,128)(2,1)}, u32[]{:S(2)}) %copy-start.1) | copy-done | bytes 196632
  23.4 8.5 %correlate.1 = (f32[16,3072]{1,0:T(8,128)S(1)}, f32[16,3072]{1,0:T(8,128)S(1)}) custom-call(bf16[3,16,2048]{2,1,0:T(8,128)(2,1)S(1)} %copy-done.1, bf16[3,16,2048]{2,1,0:T(8,128)(2,1)S(1)} %collective-permute-done.t1, bf16[3,16,2048]{2,1,0:T(8,128)(2,1)S(1)} %collective-permute-done.1.t2, bf16[3,16,2048]{2,1,0:T(8,128)(2,1)S(1)} %collective-permute-done.2.t3, ...), custom_call_target="tpu_custom_call" | custom-call | tf_op jit(solution)/shard_map/correlate/pallas_call | solution.py:300
  31.9 4.3 %collective-permute-start.10 = (f32[16,3072]{1,0:T(8,128)S(1)}, f32[16,3072]{1,0:T(8,128)S(1)}, u32[]{:S(2)}, u32[]{:S(2)}) collective-permute-start(f32[16,3072]{1,0:T(8,128)S(1)} %get-tuple-element.14), channel_id=1, source_target_pairs={{0,0},{1,4},{2,8},{3,12},{4,2},{5,6},{6,10},{7,14},{8,1},{9,5},{10... | collective-permute-start | bytes 589832 | tf_op jit(solution)/shard_map/ppermute | solution.py:328
  36.2 1.2 %collective-permute-start.9 = (f32[16,3072]{1,0:T(8,128)S(1)}, f32[16,3072]{1,0:T(8,128)S(1)}, u32[]{:S(2)}, u32[]{:S(2)}) collective-permute-start(f32[16,3072]{1,0:T(8,128)S(1)} %get-tuple-element.13), channel_id=1, source_target_pairs={{0,1},{1,5},{2,9},{3,13},{4,3},{5,7},{6,11},{7,15},{8,0},{9,4},{10... | collective-permute-start | bytes 589832 | tf_op jit(solution)/shard_map/ppermute | solution.py:328
  37.4 5.7 %collective-permute-done.10 = f32[16,3072]{1,0:T(8,128)S(1)} collective-permute-done((f32[16,3072]{1,0:T(8,128)S(1)}, f32[16,3072]{1,0:T(8,128)S(1)}, u32[]{:S(2)}, u32[]{:S(2)}) %collective-permute-start.10) | collective-permute-done | bytes 196640 | tf_op jit(solution)/shard_map/ppermute | solution.py:328
  43.1 3.4 %collective-permute-done.9 = f32[16,3072]{1,0:T(8,128)S(1)} collective-permute-done((f32[16,3072]{1,0:T(8,128)S(1)}, f32[16,3072]{1,0:T(8,128)S(1)}, u32[]{:S(2)}, u32[]{:S(2)}) %collective-permute-start.9) | collective-permute-done | bytes 196640 | tf_op jit(solution)/shard_map/ppermute | solution.py:328
  46.5 0.8 %pad_maximum_fusion = f32[32,3072]{1,0:T(8,128)} fusion(f32[16,3072]{1,0:T(8,128)S(1)} %get-tuple-element.16, f32[16,3072]{1,0:T(8,128)S(1)} %get-tuple-element.15), kind=kLoop, calls=%fused_computation | loop fusion | flops 98304 | bytes 786432 | tf_op jit(solution)/shard_map/concatenate | solution.py:351
  (15 shorter events, 0.1 us)
Async XLA Ops:
  1.8 9.6 %collective-permute-start.1 = (bf16[3,16,2048]{2,1,0:T(8,128)(2,1)}, bf16[3,16,2048]{2,1,0:T(8,128)(2,1)S(1)}, u32[]{:S(2)}, u32[]{:S(2)}) collective-permute-start(bf16[3,16,2048]{2,1,0:T(8,128)(2,1)} %get-tuple-element.11), channel_id=1, source_target_pairs={{0,8},{1,9},{2,10},{3,11},{4,12},{5,13},{6,14},{7,15},{8,0},{9,1},... | collective-permute-start | bytes 589832 | tf_op jit(solution)/shard_map/ppermute | solution.py:323
  3.9 3.6 %collective-permute-start.3 = (bf16[80,128]{1,0:T(8,128)(2,1)}, bf16[80,128]{1,0:T(8,128)(2,1)S(1)}, u32[]{:S(2)}, u32[]{:S(2)}) collective-permute-start(bf16[80,128]{1,0:T(8,128)(2,1)} %get-tuple-element.12.d0), channel_id=1, source_target_pairs={{0,1},{1,0},{2,3},{3,2},{4,5},{5,4},{6,7},{7,6},{8,9},{9,8},{10,11... | collective-permute-start | bytes 61448 | tf_op jit(solution)/shard_map/ppermute | solution.py:323
  5.2 6.9 %collective-permute-start.4 = (bf16[80,128]{1,0:T(8,128)(2,1)}, bf16[80,128]{1,0:T(8,128)(2,1)S(1)}, u32[]{:S(2)}, u32[]{:S(2)}) collective-permute-start(bf16[80,128]{1,0:T(8,128)(2,1)} %get-tuple-element.12.d0), channel_id=1, source_target_pairs={{0,2},{1,3},{2,0},{3,1},{4,6},{5,7},{6,4},{7,5},{8,10},{9,11},{10,... | collective-permute-start | bytes 61448 | tf_op jit(solution)/shard_map/ppermute | solution.py:323
  7.5 4.6 %copy-start.3 = (bf16[80,128]{1,0:T(8,128)(2,1)}, bf16[80,128]{1,0:T(8,128)(2,1)S(1)}, u32[]{:S(2)}) copy-start(bf16[80,128]{1,0:T(8,128)(2,1)S(1)} %collective-permute-done.3.d1) | copy-start | bytes 61444
  7.5 4.6 %collective-permute-start.5 = (bf16[80,128]{1,0:T(8,128)(2,1)S(1)}, bf16[80,128]{1,0:T(8,128)(2,1)S(1)}, u32[]{:S(2)}, u32[]{:S(2)}) collective-permute-start(bf16[80,128]{1,0:T(8,128)(2,1)S(1)} %collective-permute-done.3.d1), channel_id=1, source_target_pairs={{0,2},{1,3},{2,0},{3,1},{4,6},{5,7},{6,4},{7,5},{8,10},{9,11},{10,... | collective-permute-start | bytes 61448 | tf_op jit(solution)/shard_map/ppermute | solution.py:323
  9.3 11.4 %collective-permute-start = (bf16[3,16,2048]{2,1,0:T(8,128)(2,1)}, bf16[3,16,2048]{2,1,0:T(8,128)(2,1)S(1)}, u32[]{:S(2)}, u32[]{:S(2)}) collective-permute-start(bf16[3,16,2048]{2,1,0:T(8,128)(2,1)} %get-tuple-element.10.t0), channel_id=1, source_target_pairs={{0,4},{1,5},{2,6},{3,7},{4,0},{5,1},{6,2},{7,3},{8,12},{9,13},{10,... | collective-permute-start | bytes 589832 | tf_op jit(solution)/shard_map/ppermute | solution.py:323
  11.4 10.2 %collective-permute-start.2 = (bf16[3,16,2048]{2,1,0:T(8,128)(2,1)S(1)}, bf16[3,16,2048]{2,1,0:T(8,128)(2,1)S(1)}, u32[]{:S(2)}, u32[]{:S(2)}) collective-permute-start(bf16[3,16,2048]{2,1,0:T(8,128)(2,1)S(1)} %collective-permute-done.1.t2), channel_id=1, source_target_pairs={{0,4},{1,5},{2,6},{3,7},{4,0},{5,1},{6,2},{7,3},{8,12},{9,13},{10,... | collective-permute-start | bytes 589832 | tf_op jit(solution)/shard_map/ppermute | solution.py:323
  12.1 0.6 %copy-start.4 = (bf16[80,128]{1,0:T(8,128)(2,1)}, bf16[80,128]{1,0:T(8,128)(2,1)S(1)}, u32[]{:S(2)}) copy-start(bf16[80,128]{1,0:T(8,128)(2,1)S(1)} %collective-permute-done.4.d2) | copy-start | bytes 61444
  12.7 0.6 %copy-start.5 = (bf16[80,128]{1,0:T(8,128)(2,1)}, bf16[80,128]{1,0:T(8,128)(2,1)S(1)}, u32[]{:S(2)}) copy-start(bf16[80,128]{1,0:T(8,128)(2,1)S(1)} %collective-permute-done.5.d3) | copy-start | bytes 61444
  13.3 8.3 %copy-start.2 = (s32[128,4]{0,1:T(4,128)S(1)}, s32[128,4]{0,1:T(4,128)}, u32[]{:S(2)}) copy-start(s32[128,4]{0,1:T(4,128)} %param.7) | copy-start | bytes 6148
  14.9 3.6 %collective-permute-start.7 = (bf16[3,120,128]{2,1,0:T(8,128)(2,1)}, bf16[3,120,128]{2,1,0:T(8,128)(2,1)S(1)}, u32[]{:S(2)}, u32[]{:S(2)}) collective-permute-start(bf16[3,120,128]{2,1,0:T(8,128)(2,1)} %series.1.x0), channel_id=1, source_target_pairs={{0,8},{1,9},{2,10},{3,11},{4,12},{5,13},{6,14},{7,15},{8,0},{9,1},... | collective-permute-start | bytes 276488 | tf_op jit(solution)/shard_map/ppermute | solution.py:323
  15.1 5.5 %collective-permute-start.6 = (bf16[3,120,128]{2,1,0:T(8,128)(2,1)}, bf16[3,120,128]{2,1,0:T(8,128)(2,1)S(1)}, u32[]{:S(2)}, u32[]{:S(2)}) collective-permute-start(bf16[3,120,128]{2,1,0:T(8,128)(2,1)} %series.1.x0), channel_id=1, source_target_pairs={{0,4},{1,5},{2,6},{3,7},{4,0},{5,1},{6,2},{7,3},{8,12},{9,13},{10,... | collective-permute-start | bytes 276488 | tf_op jit(solution)/shard_map/ppermute | solution.py:323
  18.5 3.1 %collective-permute-start.8 = (bf16[3,120,128]{2,1,0:T(8,128)(2,1)S(1)}, bf16[3,120,128]{2,1,0:T(8,128)(2,1)S(1)}, u32[]{:S(2)}, u32[]{:S(2)}) collective-permute-start(bf16[3,120,128]{2,1,0:T(8,128)(2,1)S(1)} %collective-permute-done.7.x2), channel_id=1, source_target_pairs={{0,4},{1,5},{2,6},{3,7},{4,0},{5,1},{6,2},{7,3},{8,12},{9,13},{10,... | collective-permute-start | bytes 276488 | tf_op jit(solution)/shard_map/ppermute | solution.py:323
  21.6 0.9 %copy-start = (bf16[3,120,128]{2,1,0:T(8,128)(2,1)S(1)}, bf16[3,120,128]{2,1,0:T(8,128)(2,1)}, u32[]{:S(2)}) copy-start(bf16[3,120,128]{2,1,0:T(8,128)(2,1)} %series.1.x0) | copy-start | bytes 276484
  22.5 0.9 %copy-start.1 = (bf16[3,16,2048]{2,1,0:T(8,128)(2,1)S(1)}, bf16[3,16,2048]{2,1,0:T(8,128)(2,1)}, u32[]{:S(2)}) copy-start(bf16[3,16,2048]{2,1,0:T(8,128)(2,1)} %get-tuple-element.10.t0) | copy-start | bytes 589828
  31.9 11.2 %collective-permute-start.10 = (f32[16,3072]{1,0:T(8,128)S(1)}, f32[16,3072]{1,0:T(8,128)S(1)}, u32[]{:S(2)}, u32[]{:S(2)}) collective-permute-start(f32[16,3072]{1,0:T(8,128)S(1)} %get-tuple-element.14), channel_id=1, source_target_pairs={{0,0},{1,4},{2,8},{3,12},{4,2},{5,6},{6,10},{7,14},{8,1},{9,5},{10... | collective-permute-start | bytes 589832 | tf_op jit(solution)/shard_map/ppermute | solution.py:328
  36.2 10.3 %collective-permute-start.9 = (f32[16,3072]{1,0:T(8,128)S(1)}, f32[16,3072]{1,0:T(8,128)S(1)}, u32[]{:S(2)}, u32[]{:S(2)}) collective-permute-start(f32[16,3072]{1,0:T(8,128)S(1)} %get-tuple-element.13), channel_id=1, source_target_pairs={{0,1},{1,5},{2,9},{3,13},{4,3},{5,7},{6,11},{7,15},{8,0},{9,4},{10... | collective-permute-start | bytes 589832 | tf_op jit(solution)/shard_map/ppermute | solution.py:328

commit v2 on v1

--- a/solution.py
+++ b/solution.py
@@ -107,46 +107,38 @@
     return lax.broadcasted_iota(jnp.int32, shape, len(shape) - 1)
 
 
-def split_kernel(active, t_ref, d_ref, keep_ref, send_ref, rows_ref, scratch):
+def split_kernel(active, t_ref, keep_ref, send_ref):
     half = lax.axis_index("loop") // 2
     for c in range(3):
         on = active[0, c].astype(jnp.float32)
         for out, first in ((keep_ref, half), (send_ref, 1 - half)):
             rows = t_ref[c, pl.ds(pl.multiple_of(ROWS * first, ROWS), ROWS), :]
             out[c] = (rows.astype(jnp.float32) * on).astype(jnp.bfloat16)
-    blocks = d_ref.shape[2] // 128
-    wide = d_ref[0].astype(jnp.float32)
-    scratch[3 * blocks :] = jnp.zeros((scratch.shape[0] - 3 * blocks, 128), jnp.float32)
-    for c in range(3):
-        for j in range(blocks):
-            scratch[c * blocks + j : c * blocks + j + 1] = wide[c : c + 1, 128 * j : 128 * j + 128]
-    rows_ref[...] = scratch[...].astype(jnp.bfloat16)
-
-
-def split(active, panel, data):
-    blocks = data.shape[2] // 128
-    padded = (3 * blocks + 15) // 16 * 16
+
+
+def split(active, panel):
     half = jax.ShapeDtypeStruct((3, ROWS, panel.shape[2]), jnp.bfloat16)
     return pl.pallas_call(
         split_kernel,
-        out_shape=(half, half, jax.ShapeDtypeStruct((padded, 128), jnp.bfloat16)),
-        in_specs=[pl.BlockSpec(memory_space=pltpu.SMEM)] + [pl.BlockSpec(memory_space=pltpu.VMEM)] * 2,
-        out_specs=(pl.BlockSpec(memory_space=pltpu.VMEM),) * 3,
-        scratch_shapes=[pltpu.VMEM((padded, 128), jnp.float32)],
+        out_shape=(half, half),
+        in_specs=[pl.BlockSpec(memory_space=pltpu.SMEM), pl.BlockSpec(memory_space=pltpu.VMEM)],
+        out_specs=(pl.BlockSpec(memory_space=pltpu.VMEM),) * 2,
+        compiler_params=pltpu.CompilerParams(vmem_limit_bytes=4 << 20),
         name="split",
-    )(active, panel, data)
-
-
-def series_kernel(blocks, offset, active, d0, d1, d2, d3, x_ref, whole):
+    )(active, panel)
+
+
+def series_kernel(blocks, offset, active, own, d1, far, x_ref, whole):
     z = lax.axis_index("tgrp")
     rows = x_ref.shape[1]
     for c in range(3):
         whole[c, 4 * blocks :] = jnp.zeros((whole.shape[1] - 4 * blocks, 128), jnp.float32)
-    for b, ref in enumerate((d0, d1, d2, d3)):
-        wide = ref[...].astype(jnp.float32)
+    wide = [own[...].astype(jnp.float32), d1[...].astype(jnp.float32), far[...].astype(jnp.float32)]
+    for b in range(4):
         at = pl.multiple_of(blocks * (z ^ b), 8)
         for c in range(3):
-            whole[c, pl.ds(at, blocks), :] = wide[c * blocks : c * blocks + blocks]
+            first = c * blocks + (3 * blocks if b == 3 else 0)
+            whole[c, pl.ds(at, blocks), :] = wide[min(b, 2)][first : first + blocks]
     row, lane = offset[0] // 128, offset[0] % 128
     spill = lanes((rows, 128)) >= 128 - lane
     for c in range(3):
@@ -160,21 +152,31 @@
     return pl.pallas_call(
         functools.partial(series_kernel, blocks),
         out_shape=jax.ShapeDtypeStruct((3, rows, 128), jnp.bfloat16),
-        in_specs=[pl.BlockSpec(memory_space=pltpu.SMEM)] * 2 + [pl.BlockSpec(memory_space=pltpu.VMEM)] * 4,
+        in_specs=[pl.BlockSpec(memory_space=pltpu.SMEM)] * 2 + [pl.BlockSpec(memory_space=pltpu.VMEM)] * 3,
         out_specs=pl.BlockSpec(memory_space=pltpu.VMEM),
         scratch_shapes=[pltpu.VMEM((3, rows + 8, 128), jnp.float32)],
+        compiler_params=pltpu.CompilerParams(vmem_limit_bytes=4 << 20),
         name="series",
     )(offset, active, *pieces)
 
 
 def correlate_kernel(span, nb, t0, t1, t2, t3, x0, x1, x2, x3, masks, first_ref, second_ref,
-                     tp_ref, xf_ref, a_ref, z_ref, d_ref, rs_ref, acc_ref, tot_ref, tr_ref):
-    ts, xs = (t0, t1, t2, t3), (x0, x1, x2, x3)
+                     tp_ref, xb_ref, xf_ref, a_ref, z_ref, d_ref, acc_ref, tot_ref, tr_ref, sems):
     lb = span // 128
     kb = lb + 1
     rows = xf_ref.shape[1]
     loop_at = lax.axis_index("loop")
     half, core = loop_at // 2, loop_at % 2
+    x_first = pl.multiple_of(2 * nb * core, 16)
+    copies = []
+    for s, (t, x) in enumerate(((t0, x0), (t1, x1), (t2, x2), (t3, x3))):
+        copies.append(pltpu.make_async_copy(t, tp_ref.at[pl.ds(3 * s, 3), :, pl.ds(128, span)], sems.at[2 * s]))
+        copies.append(pltpu.make_async_copy(x.at[:, pl.ds(x_first, rows), :], xb_ref.at[pl.ds(3 * s, 3)], sems.at[2 * s + 1]))
+    for copy in copies:
+        copy.start()
+    tp_ref[:, :, 0:128] = jnp.zeros((12, ROWS, 128), jnp.bfloat16)
+    tp_ref[:, :, 128 + span :] = jnp.zeros((12, ROWS, 128), jnp.bfloat16)
+    tot_ref[...] = jnp.zeros(tot_ref.shape, jnp.float32)
     k_first = 2 * ROWS * lax.axis_index("tgrp") + ROWS * half
     lane = lanes((8, 128))
     sub = lax.broadcasted_iota(jnp.int32, (8, 128), 0)
@@ -183,28 +185,27 @@
     own = k_first + lane % ROWS
     diagonal = lanes((ROWS, 128)) % ROWS == lax.broadcasted_iota(jnp.int32, (ROWS, 128), 0)
     lane_r = lanes((rows, 128))
-    for s in range(4):
+    for copy in copies:
+        copy.wait()
+
+    def row_scale(s):
         norm = jnp.zeros((ROWS, 128), jnp.float32)
-        squares = jnp.zeros((rows, 128), jnp.float32)
         for c in range(3):
-            i = 3 * s + c
-            t = ts[s][c]
-            tp_ref[i, :, 0:128] = jnp.zeros((ROWS, 128), jnp.bfloat16)
-            tp_ref[i, :, 128 : 128 + span] = t
-            tp_ref[i, :, 128 + span :] = jnp.zeros((ROWS, 128), jnp.bfloat16)
-            wide = t.astype(jnp.float32)
-            wide = wide * wide
             for b in range(lb):
-                norm = norm + wide[:, 128 * b : 128 * b + 128]
-            x = xs[s][c, pl.ds(pl.multiple_of(2 * nb * core, 16), rows), :].astype(jnp.float32)
-            xf_ref[i] = x
-            squares = squares + x * x
+                wide = tp_ref[3 * s + c, :, 128 * b + 128 : 128 * b + 256].astype(jnp.float32)
+                norm = norm + wide * wide
         inverse = 1.0 / jnp.sqrt(jnp.sum(norm, axis=1, keepdims=True) / (3.0 * span) + epsilon)
         inverse = jnp.where(diagonal, jnp.broadcast_to(inverse, (ROWS, 128)), 0.0)
         inverse = jnp.sum(inverse, axis=0, keepdims=True)
         here = masks[pl.ds(loop_at ^ s, 1), :].astype(jnp.float32) * weight
         here = jnp.take_along_axis(jnp.broadcast_to(here, (8, 128)), own, axis=1)
-        rs_ref[s] = here[0:1] * inverse / (3.0 * span)
+        return here[0:1] * inverse / (3.0 * span)
+
+    def data_scale(s):
+        squares = jnp.zeros((rows, 128), jnp.float32)
+        for c in range(3):
+            x = xb_ref[3 * s + c].astype(jnp.float32)
+            squares = squares + x * x
         b = 1
         while b < 128:
             after = pltpu.roll(squares, rows - 1, 0)
@@ -214,7 +215,7 @@
         while b < lb:
             squares = squares + pltpu.roll(squares, rows - b, 0)
             b *= 2
-        d_ref[s] = 1.0 / jnp.sqrt(squares / (3.0 * span) + epsilon)
+        d_ref[...] = 1.0 / jnp.sqrt(squares / (3.0 * span) + epsilon)
 
     from_lane = (lane + sub) % 128
     inside = lane + sub < 128
@@ -224,8 +225,10 @@
             n = ROWS * (8 * (r % 2) + r // 2)
             a_ref[slot, n : n + ROWS, :] = tp_ref[i, :, 128 - 8 * r : 128 - 8 * r + 128 * kb]
 
+        xf_ref[slot] = xb_ref[i].astype(jnp.float32)
+
         def turned(j):
-            row = xf_ref[i, pl.ds(j, 8, stride=0), :]
+            row = xf_ref[slot, pl.ds(j, 8, stride=0), :]
             return jnp.take_along_axis(row, from_lane, axis=1)
 
         before, tiles = turned(0), []
@@ -240,17 +243,15 @@
         left = jnp.concatenate([z_ref[slot, b : b + nb].reshape(16 * nb, 128) for b in range(kb)], axis=1)
         return lax.dot_general(left, a_ref[slot], (((1,), (1,)), ((), ())), preferred_element_type=jnp.float32)
 
-    def weighted(s):
+    def weighted(rs):
         for v in (0, 1):
             index = 16 * (lane // 16) + 8 * v + sub
-            rs = rs_ref[s]
             for j in range(nb):
                 for h in (0, 1):
                     at = 16 * j + 8 * h
-                    scale = jnp.take_along_axis(d_ref[s, pl.ds(j + nb * h, 8, stride=0), :], index, axis=1) * rs
+                    scale = jnp.take_along_axis(d_ref[pl.ds(j + nb * h, 8, stride=0), :], index, axis=1) * rs
                     tot_ref[v, at : at + 8, :] += acc_ref[at : at + 8, 128 * v : 128 * v + 128] * scale
 
-    tot_ref[...] = jnp.zeros(tot_ref.shape, jnp.float32)
     build(0, 0)
 
     def station(s, carry):
@@ -261,7 +262,11 @@
                 acc_ref[...] = m
             else:
                 acc_ref[...] += m
-        weighted(s)
+            if c == 0:
+                rs = row_scale(s)
+            if c == 1:
+                data_scale(s)
+        weighted(rs)
         return carry
 
     lax.fori_loop(0, 4, station, 0)
@@ -300,20 +305,21 @@
     return pl.pallas_call(
         functools.partial(correlate_kernel, span, nb),
         out_shape=(block, block),
-        in_specs=[vmem] * 9,
+        in_specs=[pl.BlockSpec(memory_space=pl.ANY)] * 8 + [vmem],
         out_specs=(vmem, vmem),
         scratch_shapes=[
             pltpu.VMEM((12, ROWS, span + 256), jnp.bfloat16),
-            pltpu.VMEM((12, rows, 128), jnp.float32),
+            pltpu.VMEM((12, rows, 128), jnp.bfloat16),
+            pltpu.VMEM((3, rows, 128), jnp.float32),
             pltpu.VMEM((3, ROWS * SHIFTS, span + 128), jnp.bfloat16),
             pltpu.VMEM((3, nb + lb, 16, 128), jnp.bfloat16),
-            pltpu.VMEM((4, rows, 128), jnp.float32),
-            pltpu.VMEM((4, 1, 128), jnp.float32),
+            pltpu.VMEM((rows, 128), jnp.float32),
             pltpu.VMEM((16 * nb, 256), jnp.float32),
             pltpu.VMEM((2, 16 * nb, 128), jnp.float32),
             pltpu.VMEM((2, 16 * nb, 128), jnp.float32),
+            pltpu.SemaphoreType.DMA((8,)),
         ],
-        compiler_params=pltpu.CompilerParams(vmem_limit_bytes=40 << 20),
+        compiler_params=pltpu.CompilerParams(vmem_limit_bytes=24 << 20),
         name="correlate",
     )(*panels, *series, masks)
 
@@ -332,13 +338,15 @@
     span = templates.shape[3]
     nb = data.shape[2] // 128
     panel = templates[:, 0].transpose(1, 0, 2)
-    keep, send, pieces = split(active, panel, data)
+    keep, send = split(active, panel)
+    pieces = data.reshape(3 * nb, 128)
+    d1 = swapped(pieces, 0, 1)
+    near = jnp.concatenate([pieces, d1], axis=0)
+    send, _ = lax.optimization_barrier((send, near))
+    far = swapped(near, 0, 2)
     panel_y = swapped(send, 2, 0)
     panel_c = swapped(keep, 1, 0)
-    d1 = swapped(pieces, 0, 1)
-    d2 = swapped(pieces, 0, 2)
-    d3 = swapped(d1, 0, 2)
-    series = make_series(offsets, active, (pieces, d1, d2, d3), nb, 4 * nb + span // 128 + 8)
+    series = make_series(offsets, active, (pieces, d1, far), nb, 4 * nb + span // 128 + 8)
     series_y = swapped(series, 2, 0)
     series_c = swapped(series, 1, 0)
     series_yc = swapped(series_y, 1, 0)

time: 47.6 us -> 43.5 us (0.914)
  Pallas kernels: 11.9 us -> 9.68 us
  starting transfers between devices: 18.7 us -> 16.6 us
  waiting for transfers between devices: 12.1 us -> 13 us
  local copies, waits for them, and re-layouts: 3 us -> 2.43 us
    ppermute x9 -> x8, starting transfers between devices: 13.3 us -> 11.6 us  [swapped(): return lax.ppermute(value, ('loop', 'tgrp'), pairs)]
    unnamed x12 -> x7, local copies, waits for them, and re-layouts: 3 us -> 1.66 us
    pallas_call x1, Pallas kernels: 1.81 us -> 0.62 us  [split(): pl.pallas_call(split_kernel, out_shape=(half, half), in_specs=[pl.BlockSp...]
    ppermute x9 -> x8, waiting for transfers between devices: 3.05 us -> 4.1 us  [swapped(): return lax.ppermute(value, ('loop', 'tgrp'), pairs)]
    pallas_call x1, Pallas kernels: 1.62 us -> 0.72 us  [make_series(): pl.pallas_call(functools.partial(series_kernel, blocks), out_shape=jax.Sh...]
    reshape x0 -> x1, local copies, waits for them, and re-layouts: none -> 0.76 us  [local_plane(): pieces = data.reshape(3 * nb, 128)]
  transfers between devices with their start and end apart: 11 -> 10, of which waited for: 4 -> 5; matrix products, arithmetic and copies ran while one was open for 0% -> 0% of each run, Pallas kernels for 3% -> 3%
where the time goes in v2:
time: 43.5 us; the launch traced here: 43.2 us
  starting transfers between devices  16.6 us (38%)
  waiting for transfers between devices  13 us (30%)
  Pallas kernels  9.68 us (22%)
  local copies, waits for them, and re-layouts  2.43 us (6%)
  other arithmetic  0.8 us (2%)
  between operations  0.74 us (2%)
    ppermute x8, starting transfers between devices, swapped(): return lax.ppermute(value, ('loop', 'tgrp'), pairs)  11.6 us
    ppermute x2, waiting for transfers between devices, to_owner(): return lax.ppermute(value, ('loop', 'tgrp'), pairs)  8.89 us
    pallas_call x1, Pallas kernels, correlate_stations(): pl.pallas_call(functools.partial(correlate_kernel, span, nb), out_shape=(...  8.34 us
    ppermute x2, starting transfers between devices, to_owner(): return lax.ppermute(value, ('loop', 'tgrp'), pairs)  5.03 us
    ppermute x8, waiting for transfers between devices, swapped(): return lax.ppermute(value, ('loop', 'tgrp'), pairs)  4.1 us
    unnamed x7, local copies, waits for them, and re-layouts  1.66 us
  transfers between devices with their start and end apart: 10, of which 5 were waited for; matrix products, arithmetic and copies ran while one was open for 0% of the time, Pallas kernels for 3%

profile of v2, /device:TPU:1, one launch (start us, length us, event | category | flops | bytes accessed | tf_op | source)
XLA Modules:
  0.0 43.2 jit_solution(9594228818209321155)
XLA Ops:
  0.0 0.8 %reshape.3.own = bf16[72,128]{1,0:T(8,128)(2,1)S(1)} reshape(bf16[1,3,3072]{2,1,0:T(4,128)(2,1)} %param.5) | data formatting | bytes 36864 | tf_op jit(solution)/shard_map/reshape | solution.py:342
  0.8 2.2 %collective-permute-start.1 = (bf16[72,128]{1,0:T(8,128)(2,1)S(1)}, bf16[72,128]{1,0:T(8,128)(2,1)S(1)}, u32[]{:S(2)}, u32[]{:S(2)}) collective-permute-start(bf16[72,128]{1,0:T(8,128)(2,1)S(1)} %reshape.3.own), channel_id=1, source_target_pairs={{0,1},{1,0},{2,3},{3,2},{4,5},{5,4},{6,7},{7,6},{8,9},{9,8},{10,11... | collective-permute-start | bytes 55304 | tf_op jit(solution)/shard_map/ppermute | solution.py:329
  3.0 0.7 %copy-done.2 = s32[1,3]{1,0:T(1,128)S(1)} copy-done((s32[1,3]{1,0:T(1,128)S(1)}, s32[1,3]{1,0:T(1,128)}, u32[]{:S(2)}) %copy-start.2) | copy-done | bytes 36
  3.6 1.0 %copy-done = bf16[32,1,3,2048]{3,0,2,1:T(8,128)(2,1)S(1)} copy-done((bf16[32,1,3,2048]{3,0,2,1:T(8,128)(2,1)S(1)}, bf16[32,1,3,2048]{3,0,2,1:T(8,128)(2,1)}, u32[]{:S(2)}) %copy-start) | copy-done | bytes 393240
  4.6 0.6 %split.1 = (bf16[3,16,2048]{2,1,0:T(8,128)(2,1)S(1)}, bf16[3,16,2048]{2,1,0:T(8,128)(2,1)S(1)}) custom-call(s32[1,3]{1,0:T(1,128)S(1)} %copy-done.2, bf16[3,32,2048]{2,1,0:T(8,128)(2,1)S(1)} %bitcast.4), custom_call_target="tpu_custom_call" | custom-call | tf_op jit(solution)/shard_map/split/pallas_call | solution.py:121
  5.2 0.0 collective-permute-done.1.d1
  5.3 1.3 %collective-permute-start.2 = (bf16[3,16,2048]{2,1,0:T(8,128)(2,1)S(1)}, bf16[3,16,2048]{2,1,0:T(8,128)(2,1)S(1)}, u32[]{:S(2)}, u32[]{:S(2)}) collective-permute-start(bf16[3,16,2048]{2,1,0:T(8,128)(2,1)S(1)} %get-tuple-element.12), channel_id=1, source_target_pairs={{0,8},{1,9},{2,10},{3,11},{4,12},{5,13},{6,14},{7,15},{8,0},{9,1},... | collective-permute-start | bytes 589832 | tf_op jit(solution)/shard_map/ppermute | solution.py:329
  6.6 2.3 %collective-permute-start.4 = (bf16[144,128]{1,0:T(8,128)(2,1)S(1)}, bf16[144,128]{1,0:T(8,128)(2,1)S(1)}, u32[]{:S(2)}, u32[]{:S(2)}) collective-permute-start(bf16[144,128]{1,0:T(8,128)(2,1)S(1)} %constant_dynamic-update-slice_fusion), channel_id=1, source_target_pairs={{0,2},{1,3},{2,0},{3,1},{4,6},{5,7},{6,4},{7,5},{8,10},{9,11},{10,... | collective-permute-start | bytes 110600 | tf_op jit(solution)/shard_map/ppermute | solution.py:329
  8.9 1.5 %collective-permute-start = (bf16[3,16,2048]{2,1,0:T(8,128)(2,1)S(1)}, bf16[3,16,2048]{2,1,0:T(8,128)(2,1)S(1)}, u32[]{:S(2)}, u32[]{:S(2)}) collective-permute-start(bf16[3,16,2048]{2,1,0:T(8,128)(2,1)S(1)} %get-tuple-element.10.t0), channel_id=1, source_target_pairs={{0,4},{1,5},{2,6},{3,7},{4,0},{5,1},{6,2},{7,3},{8,12},{9,13},{10,... | collective-permute-start | bytes 589832 | tf_op jit(solution)/shard_map/ppermute | solution.py:329
  10.4 0.4 collective-permute-done.2.t2
  10.8 1.9 %collective-permute-start.3 = (bf16[3,16,2048]{2,1,0:T(8,128)(2,1)S(1)}, bf16[3,16,2048]{2,1,0:T(8,128)(2,1)S(1)}, u32[]{:S(2)}, u32[]{:S(2)}) collective-permute-start(bf16[3,16,2048]{2,1,0:T(8,128)(2,1)S(1)} %collective-permute-done.2.t2), channel_id=1, source_target_pairs={{0,4},{1,5},{2,6},{3,7},{4,0},{5,1},{6,2},{7,3},{8,12},{9,13},{10,... | collective-permute-start | bytes 589832 | tf_op jit(solution)/shard_map/ppermute | solution.py:329
  13.3 0.0 copy-start.1
  13.3 0.7 %series.1.x0 = bf16[3,120,128]{2,1,0:T(8,128)(2,1)S(1)} custom-call(s32[1]{0:T(128)S(6)} %copy.7.offset, s32[1,3]{1,0:T(1,128)S(1)} %copy-done.2, bf16[72,128]{1,0:T(8,128)(2,1)S(1)} %reshape.3.own, bf16[72,128]{1,0:T(8,128)(2,1)S(1)} %collective-permute-done.1.d1, bf16[144,128]{1,0:T(8,128)(2,1)S(1)} %collective-permute-done.4.far), custom_call_target="tpu_custom_call" | custom-call | tf_op jit(solution)/shard_map/series/pallas_call | solution.py:152
  14.0 1.3 %collective-permute-start.6 = (bf16[3,120,128]{2,1,0:T(8,128)(2,1)S(1)}, bf16[3,120,128]{2,1,0:T(8,128)(2,1)S(1)}, u32[]{:S(2)}, u32[]{:S(2)}) collective-permute-start(bf16[3,120,128]{2,1,0:T(8,128)(2,1)S(1)} %series.1.x0), channel_id=1, source_target_pairs={{0,8},{1,9},{2,10},{3,11},{4,12},{5,13},{6,14},{7,15},{8,0},{9,1},... | collective-permute-start | bytes 276488 | tf_op jit(solution)/shard_map/ppermute | solution.py:329
  15.4 0.3 collective-permute-start.5
  15.6 2.8 %collective-permute-done.6.x2 = bf16[3,120,128]{2,1,0:T(8,128)(2,1)S(1)} collective-permute-done((bf16[3,120,128]{2,1,0:T(8,128)(2,1)S(1)}, bf16[3,120,128]{2,1,0:T(8,128)(2,1)S(1)}, u32[]{:S(2)}, u32[]{:S(2)}) %collective-permute-start.6) | collective-permute-done | bytes 92192 | tf_op jit(solution)/shard_map/ppermute | solution.py:329
  18.4 0.8 %collective-permute-start.7 = (bf16[3,120,128]{2,1,0:T(8,128)(2,1)S(1)}, bf16[3,120,128]{2,1,0:T(8,128)(2,1)S(1)}, u32[]{:S(2)}, u32[]{:S(2)}) collective-permute-start(bf16[3,120,128]{2,1,0:T(8,128)(2,1)S(1)} %collective-permute-done.6.x2), channel_id=1, source_target_pairs={{0,4},{1,5},{2,6},{3,7},{4,0},{5,1},{6,2},{7,3},{8,12},{9,13},{10,... | collective-permute-start | bytes 276488 | tf_op jit(solution)/shard_map/ppermute | solution.py:329
  19.2 0.9 %collective-permute-done.7.x3 = bf16[3,120,128]{2,1,0:T(8,128)(2,1)S(1)} collective-permute-done((bf16[3,120,128]{2,1,0:T(8,128)(2,1)S(1)}, bf16[3,120,128]{2,1,0:T(8,128)(2,1)S(1)}, u32[]{:S(2)}, u32[]{:S(2)}) %collective-permute-start.7) | collective-permute-done | bytes 92192 | tf_op jit(solution)/shard_map/ppermute | solution.py:329
  20.1 8.3 %correlate.1 = (f32[16,3072]{1,0:T(8,128)S(1)}, f32[16,3072]{1,0:T(8,128)S(1)}) custom-call(bf16[3,16,2048]{2,1,0:T(8,128)(2,1)S(1)} %get-tuple-element.10.t0, bf16[3,16,2048]{2,1,0:T(8,128)(2,1)S(1)} %collective-permute-done.t1, bf16[3,16,2048]{2,1,0:T(8,128)(2,1)S(1)} %collective-permute-done.2.t2, bf16[3,16,2048]{2,1,0:T(8,128)(2,1)S(1)} %collective-permute-done.3.t3, ...), custom_call_target="tpu_custom_call" | custom-call | tf_op jit(solution)/shard_map/correlate/pallas_call | solution.py:305
  28.5 2.7 %collective-permute-start.8 = (f32[16,3072]{1,0:T(8,128)S(1)}, f32[16,3072]{1,0:T(8,128)S(1)}, u32[]{:S(2)}, u32[]{:S(2)}) collective-permute-start(f32[16,3072]{1,0:T(8,128)S(1)} %get-tuple-element.13), channel_id=1, source_target_pairs={{0,1},{1,5},{2,9},{3,13},{4,3},{5,7},{6,11},{7,15},{8,0},{9,4},{10... | collective-permute-start | bytes 589832 | tf_op jit(solution)/shard_map/ppermute | solution.py:334
  31.2 2.3 %collective-permute-start.9 = (f32[16,3072]{1,0:T(8,128)S(1)}, f32[16,3072]{1,0:T(8,128)S(1)}, u32[]{:S(2)}, u32[]{:S(2)}) collective-permute-start(f32[16,3072]{1,0:T(8,128)S(1)} %get-tuple-element.14), channel_id=1, source_target_pairs={{0,0},{1,4},{2,8},{3,12},{4,2},{5,6},{6,10},{7,14},{8,1},{9,5},{10... | collective-permute-start | bytes 589832 | tf_op jit(solution)/shard_map/ppermute | solution.py:334
  33.5 5.3 %collective-permute-done.8 = f32[16,3072]{1,0:T(8,128)S(1)} collective-permute-done((f32[16,3072]{1,0:T(8,128)S(1)}, f32[16,3072]{1,0:T(8,128)S(1)}, u32[]{:S(2)}, u32[]{:S(2)}) %collective-permute-start.8) | collective-permute-done | bytes 196640 | tf_op jit(solution)/shard_map/ppermute | solution.py:334
  38.8 3.6 %collective-permute-done.9 = f32[16,3072]{1,0:T(8,128)S(1)} collective-permute-done((f32[16,3072]{1,0:T(8,128)S(1)}, f32[16,3072]{1,0:T(8,128)S(1)}, u32[]{:S(2)}, u32[]{:S(2)}) %collective-permute-start.9) | collective-permute-done | bytes 196640 | tf_op jit(solution)/shard_map/ppermute | solution.py:334
  42.5 0.8 %pad_maximum_fusion = f32[32,3072]{1,0:T(8,128)} fusion(f32[16,3072]{1,0:T(8,128)S(1)} %get-tuple-element.16, f32[16,3072]{1,0:T(8,128)S(1)} %get-tuple-element.15), kind=kLoop, calls=%fused_computation | loop fusion | flops 98304 | bytes 786432 | tf_op jit(solution)/shard_map/concatenate | solution.py:359
  (10 shorter events, 0.1 us)
Async XLA Ops:
  0.8 4.5 %collective-permute-start.1 = (bf16[72,128]{1,0:T(8,128)(2,1)S(1)}, bf16[72,128]{1,0:T(8,128)(2,1)S(1)}, u32[]{:S(2)}, u32[]{:S(2)}) collective-permute-start(bf16[72,128]{1,0:T(8,128)(2,1)S(1)} %reshape.3.own), channel_id=1, source_target_pairs={{0,1},{1,0},{2,3},{3,2},{4,5},{5,4},{6,7},{7,6},{8,9},{9,8},{10,11... | collective-permute-start | bytes 55304 | tf_op jit(solution)/shard_map/ppermute | solution.py:329
  3.0 0.7 %copy-start.2 = (s32[1,3]{1,0:T(1,128)S(1)}, s32[1,3]{1,0:T(1,128)}, u32[]{:S(2)}) copy-start(s32[1,3]{1,0:T(1,128)} %active.3) | copy-start | bytes 40
  3.6 1.0 %copy-start = (bf16[32,1,3,2048]{3,0,2,1:T(8,128)(2,1)S(1)}, bf16[32,1,3,2048]{3,0,2,1:T(8,128)(2,1)}, u32[]{:S(2)}) copy-start(bf16[32,1,3,2048]{3,0,2,1:T(8,128)(2,1)} %param.6) | copy-start | bytes 1179652
  5.3 5.5 %collective-permute-start.2 = (bf16[3,16,2048]{2,1,0:T(8,128)(2,1)S(1)}, bf16[3,16,2048]{2,1,0:T(8,128)(2,1)S(1)}, u32[]{:S(2)}, u32[]{:S(2)}) collective-permute-start(bf16[3,16,2048]{2,1,0:T(8,128)(2,1)S(1)} %get-tuple-element.12), channel_id=1, source_target_pairs={{0,8},{1,9},{2,10},{3,11},{4,12},{5,13},{6,14},{7,15},{8,0},{9,1},... | collective-permute-start | bytes 589832 | tf_op jit(solution)/shard_map/ppermute | solution.py:329
  6.6 6.7 %collective-permute-start.4 = (bf16[144,128]{1,0:T(8,128)(2,1)S(1)}, bf16[144,128]{1,0:T(8,128)(2,1)S(1)}, u32[]{:S(2)}, u32[]{:S(2)}) collective-permute-start(bf16[144,128]{1,0:T(8,128)(2,1)S(1)} %constant_dynamic-update-slice_fusion), channel_id=1, source_target_pairs={{0,2},{1,3},{2,0},{3,1},{4,6},{5,7},{6,4},{7,5},{8,10},{9,11},{10,... | collective-permute-start | bytes 110600 | tf_op jit(solution)/shard_map/ppermute | solution.py:329
  8.9 10.3 %collective-permute-start = (bf16[3,16,2048]{2,1,0:T(8,128)(2,1)S(1)}, bf16[3,16,2048]{2,1,0:T(8,128)(2,1)S(1)}, u32[]{:S(2)}, u32[]{:S(2)}) collective-permute-start(bf16[3,16,2048]{2,1,0:T(8,128)(2,1)S(1)} %get-tuple-element.10.t0), channel_id=1, source_target_pairs={{0,4},{1,5},{2,6},{3,7},{4,0},{5,1},{6,2},{7,3},{8,12},{9,13},{10,... | collective-permute-start | bytes 589832 | tf_op jit(solution)/shard_map/ppermute | solution.py:329
  10.8 9.3 %collective-permute-start.3 = (bf16[3,16,2048]{2,1,0:T(8,128)(2,1)S(1)}, bf16[3,16,2048]{2,1,0:T(8,128)(2,1)S(1)}, u32[]{:S(2)}, u32[]{:S(2)}) collective-permute-start(bf16[3,16,2048]{2,1,0:T(8,128)(2,1)S(1)} %collective-permute-done.2.t2), channel_id=1, source_target_pairs={{0,4},{1,5},{2,6},{3,7},{4,0},{5,1},{6,2},{7,3},{8,12},{9,13},{10,... | collective-permute-start | bytes 589832 | tf_op jit(solution)/shard_map/ppermute | solution.py:329
  13.3 6.8 %copy-start.1 = (s32[128,4]{0,1:T(4,128)S(1)}, s32[128,4]{0,1:T(4,128)}, u32[]{:S(2)}) copy-start(s32[128,4]{0,1:T(4,128)} %param.7) | copy-start | bytes 6148
  14.0 4.4 %collective-permute-start.6 = (bf16[3,120,128]{2,1,0:T(8,128)(2,1)S(1)}, bf16[3,120,128]{2,1,0:T(8,128)(2,1)S(1)}, u32[]{:S(2)}, u32[]{:S(2)}) collective-permute-start(bf16[3,120,128]{2,1,0:T(8,128)(2,1)S(1)} %series.1.x0), channel_id=1, source_target_pairs={{0,8},{1,9},{2,10},{3,11},{4,12},{5,13},{6,14},{7,15},{8,0},{9,1},... | collective-permute-start | bytes 276488 | tf_op jit(solution)/shard_map/ppermute | solution.py:329
  15.4 3.8 %collective-permute-start.5 = (bf16[3,120,128]{2,1,0:T(8,128)(2,1)S(1)}, bf16[3,120,128]{2,1,0:T(8,128)(2,1)S(1)}, u32[]{:S(2)}, u32[]{:S(2)}) collective-permute-start(bf16[3,120,128]{2,1,0:T(8,128)(2,1)S(1)} %series.1.x0), channel_id=1, source_target_pairs={{0,4},{1,5},{2,6},{3,7},{4,0},{5,1},{6,2},{7,3},{8,12},{9,13},{10,... | collective-permute-start | bytes 276488 | tf_op jit(solution)/shard_map/ppermute | solution.py:329
  18.4 1.7 %collective-permute-start.7 = (bf16[3,120,128]{2,1,0:T(8,128)(2,1)S(1)}, bf16[3,120,128]{2,1,0:T(8,128)(2,1)S(1)}, u32[]{:S(2)}, u32[]{:S(2)}) collective-permute-start(bf16[3,120,128]{2,1,0:T(8,128)(2,1)S(1)} %collective-permute-done.6.x2), channel_id=1, source_target_pairs={{0,4},{1,5},{2,6},{3,7},{4,0},{5,1},{6,2},{7,3},{8,12},{9,13},{10,... | collective-permute-start | bytes 276488 | tf_op jit(solution)/shard_map/ppermute | solution.py:329
  28.5 10.3 %collective-permute-start.8 = (f32[16,3072]{1,0:T(8,128)S(1)}, f32[16,3072]{1,0:T(8,128)S(1)}, u32[]{:S(2)}, u32[]{:S(2)}) collective-permute-start(f32[16,3072]{1,0:T(8,128)S(1)} %get-tuple-element.13), channel_id=1, source_target_pairs={{0,1},{1,5},{2,9},{3,13},{4,3},{5,7},{6,11},{7,15},{8,0},{9,4},{10... | collective-permute-start | bytes 589832 | tf_op jit(solution)/shard_map/ppermute | solution.py:334
  31.2 11.2 %collective-permute-start.9 = (f32[16,3072]{1,0:T(8,128)S(1)}, f32[16,3072]{1,0:T(8,128)S(1)}, u32[]{:S(2)}, u32[]{:S(2)}) collective-permute-start(f32[16,3072]{1,0:T(8,128)S(1)} %get-tuple-element.14), channel_id=1, source_target_pairs={{0,0},{1,4},{2,8},{3,12},{4,2},{5,6},{6,10},{7,14},{8,1},{9,5},{10... | collective-permute-start | bytes 589832 | tf_op jit(solution)/shard_map/ppermute | solution.py:334

commit v3 on v2

--- a/solution.py
+++ b/solution.py
@@ -101,6 +101,8 @@
 
 ROWS = 16
 SHIFTS = 16
+STEPS = 32700.0
+LEVELS = 64.0
 
 
 def lanes(shape):
@@ -292,15 +294,46 @@
                 for p in range(8):
                     at = nb * (8 * q + p) + 8 * jb
                     tr_ref[f, at : at + 8, :] = v[q][p]
+        levels = [jnp.zeros((8, 128), jnp.float32)] * 2
         for j in range(nb):
+            codes = []
             for q in (0, 1):
-                out[8 * q : 8 * q + 8, 128 * j : 128 * j + 128] = tr_ref[f, pl.ds(8 * nb * q + j, 8, stride=nb), :]
+                value = tr_ref[f, pl.ds(8 * nb * q + j, 8, stride=nb), :]
+                top = jnp.maximum(jnp.max(jnp.abs(value), axis=1, keepdims=True), 2e-33)
+                level = jnp.ceil(jnp.log2(jnp.broadcast_to(top, (8, 128))) * LEVELS)
+                levels[q] = jnp.where(lane == j, level, levels[q])
+                codes.append(jnp.round(value * (STEPS * jnp.exp2(level * (-1.0 / LEVELS)))))
+            out[:, 128 * j : 128 * j + 128] = jnp.concatenate(codes, axis=0).astype(jnp.int32).astype(jnp.int16)
+        out[:, 128 * nb :] = jnp.concatenate(levels, axis=0).astype(jnp.int32).astype(jnp.int16)
+
+
+def decode_kernel(a_ref, b_ref, out_ref):
+    odd = lax.axis_index("tgrp") % 2
+    nb = out_ref.shape[1] // 128
+    for ref, half in ((a_ref, odd), (b_ref, 1 - odd)):
+        at = pl.multiple_of(ROWS * half, ROWS)
+        step = jnp.exp2(ref[:, 128 * nb :].astype(jnp.float32) * (1.0 / LEVELS)) * (1.0 / STEPS)
+        for j in range(nb):
+            value = ref[:, 128 * j : 128 * j + 128].astype(jnp.float32)
+            out_ref[pl.ds(at, ROWS), 128 * j : 128 * j + 128] = value * step[:, j : j + 1]
+
+
+def decode(first, second):
+    vmem = pl.BlockSpec(memory_space=pltpu.VMEM)
+    return pl.pallas_call(
+        decode_kernel,
+        out_shape=jax.ShapeDtypeStruct((2 * ROWS, first.shape[1] - 128), jnp.float32),
+        in_specs=[vmem, vmem],
+        out_specs=vmem,
+        compiler_params=pltpu.CompilerParams(vmem_limit_bytes=4 << 20),
+        name="decode",
+    )(first, second)
 
 
 def correlate_stations(panels, series, masks, span, nb):
     lb = span // 128
     rows = 2 * nb + lb + 8
-    block = jax.ShapeDtypeStruct((ROWS, 128 * nb), jnp.float32)
+    block = jax.ShapeDtypeStruct((ROWS, 128 * nb + 128), jnp.int16)
     vmem = pl.BlockSpec(memory_space=pltpu.VMEM)
     return pl.pallas_call(
         functools.partial(correlate_kernel, span, nb),
@@ -354,9 +387,7 @@
     first, second = correlate_stations(
         (keep, panel_c, panel_y, panel_yc), (series, series_c, series_y, series_yc), masks.T, span, nb
     )
-    first, second = to_owner(first, 0), to_owner(second, 1)
-    odd = lax.axis_index("tgrp") % 2 == 1
-    return jnp.concatenate([jnp.where(odd, second, first), jnp.where(odd, first, second)], axis=0)
+    return decode(to_owner(first, 0), to_owner(second, 1))
 
 
 def solution(mesh):

time: 43.5 us -> 41.6 us (0.956)
  waiting for transfers between devices: 13 us -> 9.33 us
  starting transfers between devices: 16.6 us -> 18 us
  Pallas kernels: 9.68 us -> 10.9 us
  other arithmetic: 0.8 us -> 0 us
    ppermute x2, waiting for transfers between devices: 8.89 us -> 5.23 us  [to_owner(): return lax.ppermute(value, ('loop', 'tgrp'), pairs)]
    ppermute x2, starting transfers between devices: 5.03 us -> 6.47 us  [to_owner(): return lax.ppermute(value, ('loop', 'tgrp'), pairs)]
    pallas_call x0 -> x1, Pallas kernels: none -> 0.98 us  [decode(): pl.pallas_call(decode_kernel, out_shape=jax.ShapeDtypeStruct((2 * ROWS, f...]
    concatenate x1 -> x0, other arithmetic: 0.77 us -> none  [local_plane(): jnp.concatenate([jnp.where(odd, second, first), jnp.where(odd, first, sec...]
where the time goes in v3:
time: 41.6 us; the launch traced here: 41.4 us
  starting transfers between devices  18 us (43%)
  Pallas kernels  10.9 us (26%)
  waiting for transfers between devices  9.33 us (22%)
  local copies, waits for them, and re-layouts  2.43 us (6%)
  between operations  0.72 us (2%)
    ppermute x8, starting transfers between devices, swapped(): return lax.ppermute(value, ('loop', 'tgrp'), pairs)  11.6 us
    pallas_call x1, Pallas kernels, correlate_stations(): pl.pallas_call(functools.partial(correlate_kernel, span, nb), out_shape=(...  8.55 us
    ppermute x2, starting transfers between devices, to_owner(): return lax.ppermute(value, ('loop', 'tgrp'), pairs)  6.47 us
    ppermute x2, waiting for transfers between devices, to_owner(): return lax.ppermute(value, ('loop', 'tgrp'), pairs)  5.23 us
    ppermute x8, waiting for transfers between devices, swapped(): return lax.ppermute(value, ('loop', 'tgrp'), pairs)  4.1 us
    unnamed x7, local copies, waits for them, and re-layouts  1.66 us
    pallas_call x1, Pallas kernels, decode(): pl.pallas_call(decode_kernel, out_shape=jax.ShapeDtypeStruct((2 * ROWS, f...  0.98 us
  transfers between devices with their start and end apart: 10, of which 5 were waited for; matrix products, arithmetic and copies ran while one was open for 0% of the time, Pallas kernels for 3%

profile of v3, /device:TPU:1, one launch (start us, length us, event | category | flops | bytes accessed | tf_op | source)
XLA Modules:
  0.0 41.4 jit_solution(1941885756671172469)
XLA Ops:
  0.0 0.8 %reshape.3.own = bf16[72,128]{1,0:T(8,128)(2,1)S(1)} reshape(bf16[1,3,3072]{2,1,0:T(4,128)(2,1)} %param.5) | data formatting | bytes 36864 | tf_op jit(solution)/shard_map/reshape | solution.py:375
  0.8 2.2 %collective-permute-start.1 = (bf16[72,128]{1,0:T(8,128)(2,1)S(1)}, bf16[72,128]{1,0:T(8,128)(2,1)S(1)}, u32[]{:S(2)}, u32[]{:S(2)}) collective-permute-start(bf16[72,128]{1,0:T(8,128)(2,1)S(1)} %reshape.3.own), channel_id=1, source_target_pairs={{0,1},{1,0},{2,3},{3,2},{4,5},{5,4},{6,7},{7,6},{8,9},{9,8},{10,11... | collective-permute-start | bytes 55304 | tf_op jit(solution)/shard_map/ppermute | solution.py:362
  3.0 0.7 %copy-done.2 = s32[1,3]{1,0:T(1,128)S(1)} copy-done((s32[1,3]{1,0:T(1,128)S(1)}, s32[1,3]{1,0:T(1,128)}, u32[]{:S(2)}) %copy-start.2) | copy-done | bytes 36
  3.6 1.0 %copy-done = bf16[32,1,3,2048]{3,0,2,1:T(8,128)(2,1)S(1)} copy-done((bf16[32,1,3,2048]{3,0,2,1:T(8,128)(2,1)S(1)}, bf16[32,1,3,2048]{3,0,2,1:T(8,128)(2,1)}, u32[]{:S(2)}) %copy-start) | copy-done | bytes 393240
  4.6 0.6 %split.1 = (bf16[3,16,2048]{2,1,0:T(8,128)(2,1)S(1)}, bf16[3,16,2048]{2,1,0:T(8,128)(2,1)S(1)}) custom-call(s32[1,3]{1,0:T(1,128)S(1)} %copy-done.2, bf16[3,32,2048]{2,1,0:T(8,128)(2,1)S(1)} %bitcast.4), custom_call_target="tpu_custom_call" | custom-call | tf_op jit(solution)/shard_map/split/pallas_call | solution.py:123
  5.3 1.3 %collective-permute-start.2 = (bf16[3,16,2048]{2,1,0:T(8,128)(2,1)S(1)}, bf16[3,16,2048]{2,1,0:T(8,128)(2,1)S(1)}, u32[]{:S(2)}, u32[]{:S(2)}) collective-permute-start(bf16[3,16,2048]{2,1,0:T(8,128)(2,1)S(1)} %get-tuple-element.12), channel_id=1, source_target_pairs={{0,8},{1,9},{2,10},{3,11},{4,12},{5,13},{6,14},{7,15},{8,0},{9,1},... | collective-permute-start | bytes 589832 | tf_op jit(solution)/shard_map/ppermute | solution.py:362
  6.6 2.3 %collective-permute-start.4 = (bf16[144,128]{1,0:T(8,128)(2,1)S(1)}, bf16[144,128]{1,0:T(8,128)(2,1)S(1)}, u32[]{:S(2)}, u32[]{:S(2)}) collective-permute-start(bf16[144,128]{1,0:T(8,128)(2,1)S(1)} %constant_dynamic-update-slice_fusion), channel_id=1, source_target_pairs={{0,2},{1,3},{2,0},{3,1},{4,6},{5,7},{6,4},{7,5},{8,10},{9,11},{10,... | collective-permute-start | bytes 110600 | tf_op jit(solution)/shard_map/ppermute | solution.py:362
  8.9 1.5 %collective-permute-start = (bf16[3,16,2048]{2,1,0:T(8,128)(2,1)S(1)}, bf16[3,16,2048]{2,1,0:T(8,128)(2,1)S(1)}, u32[]{:S(2)}, u32[]{:S(2)}) collective-permute-start(bf16[3,16,2048]{2,1,0:T(8,128)(2,1)S(1)} %get-tuple-element.10.t0), channel_id=1, source_target_pairs={{0,4},{1,5},{2,6},{3,7},{4,0},{5,1},{6,2},{7,3},{8,12},{9,13},{10,... | collective-permute-start | bytes 589832 | tf_op jit(solution)/shard_map/ppermute | solution.py:362
  10.4 0.4 collective-permute-done.2.t2
  10.8 1.9 %collective-permute-start.3 = (bf16[3,16,2048]{2,1,0:T(8,128)(2,1)S(1)}, bf16[3,16,2048]{2,1,0:T(8,128)(2,1)S(1)}, u32[]{:S(2)}, u32[]{:S(2)}) collective-permute-start(bf16[3,16,2048]{2,1,0:T(8,128)(2,1)S(1)} %collective-permute-done.2.t2), channel_id=1, source_target_pairs={{0,4},{1,5},{2,6},{3,7},{4,0},{5,1},{6,2},{7,3},{8,12},{9,13},{10,... | collective-permute-start | bytes 589832 | tf_op jit(solution)/shard_map/ppermute | solution.py:362
  13.3 0.0 collective-permute-done.4.far
  13.3 0.0 copy-start.1
  13.3 0.7 %series.1.x0 = bf16[3,120,128]{2,1,0:T(8,128)(2,1)S(1)} custom-call(s32[1]{0:T(128)S(6)} %copy.7.offset, s32[1,3]{1,0:T(1,128)S(1)} %copy-done.2, bf16[72,128]{1,0:T(8,128)(2,1)S(1)} %reshape.3.own, bf16[72,128]{1,0:T(8,128)(2,1)S(1)} %collective-permute-done.1.d1, bf16[144,128]{1,0:T(8,128)(2,1)S(1)} %collective-permute-done.4.far), custom_call_target="tpu_custom_call" | custom-call | tf_op jit(solution)/shard_map/series/pallas_call | solution.py:154
  14.0 1.3 %collective-permute-start.6 = (bf16[3,120,128]{2,1,0:T(8,128)(2,1)S(1)}, bf16[3,120,128]{2,1,0:T(8,128)(2,1)S(1)}, u32[]{:S(2)}, u32[]{:S(2)}) collective-permute-start(bf16[3,120,128]{2,1,0:T(8,128)(2,1)S(1)} %series.1.x0), channel_id=1, source_target_pairs={{0,8},{1,9},{2,10},{3,11},{4,12},{5,13},{6,14},{7,15},{8,0},{9,1},... | collective-permute-start | bytes 276488 | tf_op jit(solution)/shard_map/ppermute | solution.py:362
  15.4 0.3 collective-permute-start.5
  15.6 2.8 %collective-permute-done.6.x2 = bf16[3,120,128]{2,1,0:T(8,128)(2,1)S(1)} collective-permute-done((bf16[3,120,128]{2,1,0:T(8,128)(2,1)S(1)}, bf16[3,120,128]{2,1,0:T(8,128)(2,1)S(1)}, u32[]{:S(2)}, u32[]{:S(2)}) %collective-permute-start.6) | collective-permute-done | bytes 92192 | tf_op jit(solution)/shard_map/ppermute | solution.py:362
  18.4 0.8 %collective-permute-start.7 = (bf16[3,120,128]{2,1,0:T(8,128)(2,1)S(1)}, bf16[3,120,128]{2,1,0:T(8,128)(2,1)S(1)}, u32[]{:S(2)}, u32[]{:S(2)}) collective-permute-start(bf16[3,120,128]{2,1,0:T(8,128)(2,1)S(1)} %collective-permute-done.6.x2), channel_id=1, source_target_pairs={{0,4},{1,5},{2,6},{3,7},{4,0},{5,1},{6,2},{7,3},{8,12},{9,13},{10,... | collective-permute-start | bytes 276488 | tf_op jit(solution)/shard_map/ppermute | solution.py:362
  19.2 0.9 %collective-permute-done.7.x3 = bf16[3,120,128]{2,1,0:T(8,128)(2,1)S(1)} collective-permute-done((bf16[3,120,128]{2,1,0:T(8,128)(2,1)S(1)}, bf16[3,120,128]{2,1,0:T(8,128)(2,1)S(1)}, u32[]{:S(2)}, u32[]{:S(2)}) %collective-permute-start.7) | collective-permute-done | bytes 92192 | tf_op jit(solution)/shard_map/ppermute | solution.py:362
  20.1 8.5 %correlate.1 = (s16[16,3200]{1,0:T(8,128)(2,1)S(1)}, s16[16,3200]{1,0:T(8,128)(2,1)S(1)}) custom-call(bf16[3,16,2048]{2,1,0:T(8,128)(2,1)S(1)} %get-tuple-element.10.t0, bf16[3,16,2048]{2,1,0:T(8,128)(2,1)S(1)} %collective-permute-done.t1, bf16[3,16,2048]{2,1,0:T(8,128)(2,1)S(1)} %collective-permute-done.2.t2, ...), custom_call_target="tpu_custom_call" | custom-call | tf_op jit(solution)/shard_map/correlate/pallas_call | solution.py:338
  28.7 4.5 %collective-permute-start.8 = (s16[16,3200]{1,0:T(8,128)(2,1)S(1)}, s16[16,3200]{1,0:T(8,128)(2,1)S(1)}, u32[]{:S(2)}, u32[]{:S(2)}) collective-permute-start(s16[16,3200]{1,0:T(8,128)(2,1)S(1)} %get-tuple-element.13), channel_id=1, source_target_pairs={{0,0},{1,4},{2,8},{3,12},{4,2},{5,6},{6,10},{7,14},{8,1},{9,5},{10... | collective-permute-start | bytes 307208 | tf_op jit(solution)/shard_map/ppermute | solution.py:367
  33.2 2.0 %collective-permute-start.9 = (s16[16,3200]{1,0:T(8,128)(2,1)S(1)}, s16[16,3200]{1,0:T(8,128)(2,1)S(1)}, u32[]{:S(2)}, u32[]{:S(2)}) collective-permute-start(s16[16,3200]{1,0:T(8,128)(2,1)S(1)} %get-tuple-element.14), channel_id=1, source_target_pairs={{0,1},{1,5},{2,9},{3,13},{4,3},{5,7},{6,11},{7,15},{8,0},{9,4},{10... | collective-permute-start | bytes 307208 | tf_op jit(solution)/shard_map/ppermute | solution.py:367
  35.2 0.6 %collective-permute-done.8.a_ref = s16[16,3200]{1,0:T(8,128)(2,1)S(1)} collective-permute-done((s16[16,3200]{1,0:T(8,128)(2,1)S(1)}, s16[16,3200]{1,0:T(8,128)(2,1)S(1)}, u32[]{:S(2)}, u32[]{:S(2)}) %collective-permute-start.8) | collective-permute-done | bytes 102432 | tf_op jit(solution)/shard_map/ppermute | solution.py:367
  35.7 4.7 %collective-permute-done.9.b_ref = s16[16,3200]{1,0:T(8,128)(2,1)S(1)} collective-permute-done((s16[16,3200]{1,0:T(8,128)(2,1)S(1)}, s16[16,3200]{1,0:T(8,128)(2,1)S(1)}, u32[]{:S(2)}, u32[]{:S(2)}) %collective-permute-start.9) | collective-permute-done | bytes 102432 | tf_op jit(solution)/shard_map/ppermute | solution.py:367
  40.4 1.0 %decode.1 = f32[32,3072]{1,0:T(8,128)} custom-call(s16[16,3200]{1,0:T(8,128)(2,1)S(1)} %collective-permute-done.8.a_ref, s16[16,3200]{1,0:T(8,128)(2,1)S(1)} %collective-permute-done.9.b_ref), custom_call_target="tpu_custom_call" | custom-call | tf_op jit(solution)/shard_map/decode/pallas_call | solution.py:323
  (9 shorter events, 0.0 us)
Async XLA Ops:
  0.8 4.5 %collective-permute-start.1 = (bf16[72,128]{1,0:T(8,128)(2,1)S(1)}, bf16[72,128]{1,0:T(8,128)(2,1)S(1)}, u32[]{:S(2)}, u32[]{:S(2)}) collective-permute-start(bf16[72,128]{1,0:T(8,128)(2,1)S(1)} %reshape.3.own), channel_id=1, source_target_pairs={{0,1},{1,0},{2,3},{3,2},{4,5},{5,4},{6,7},{7,6},{8,9},{9,8},{10,11... | collective-permute-start | bytes 55304 | tf_op jit(solution)/shard_map/ppermute | solution.py:362
  3.0 0.7 %copy-start.2 = (s32[1,3]{1,0:T(1,128)S(1)}, s32[1,3]{1,0:T(1,128)}, u32[]{:S(2)}) copy-start(s32[1,3]{1,0:T(1,128)} %active.3) | copy-start | bytes 40
  3.6 1.0 %copy-start = (bf16[32,1,3,2048]{3,0,2,1:T(8,128)(2,1)S(1)}, bf16[32,1,3,2048]{3,0,2,1:T(8,128)(2,1)}, u32[]{:S(2)}) copy-start(bf16[32,1,3,2048]{3,0,2,1:T(8,128)(2,1)} %param.6) | copy-start | bytes 1179652
  5.3 5.5 %collective-permute-start.2 = (bf16[3,16,2048]{2,1,0:T(8,128)(2,1)S(1)}, bf16[3,16,2048]{2,1,0:T(8,128)(2,1)S(1)}, u32[]{:S(2)}, u32[]{:S(2)}) collective-permute-start(bf16[3,16,2048]{2,1,0:T(8,128)(2,1)S(1)} %get-tuple-element.12), channel_id=1, source_target_pairs={{0,8},{1,9},{2,10},{3,11},{4,12},{5,13},{6,14},{7,15},{8,0},{9,1},... | collective-permute-start | bytes 589832 | tf_op jit(solution)/shard_map/ppermute | solution.py:362
  6.6 6.7 %collective-permute-start.4 = (bf16[144,128]{1,0:T(8,128)(2,1)S(1)}, bf16[144,128]{1,0:T(8,128)(2,1)S(1)}, u32[]{:S(2)}, u32[]{:S(2)}) collective-permute-start(bf16[144,128]{1,0:T(8,128)(2,1)S(1)} %constant_dynamic-update-slice_fusion), channel_id=1, source_target_pairs={{0,2},{1,3},{2,0},{3,1},{4,6},{5,7},{6,4},{7,5},{8,10},{9,11},{10,... | collective-permute-start | bytes 110600 | tf_op jit(solution)/shard_map/ppermute | solution.py:362
  8.9 10.3 %collective-permute-start = (bf16[3,16,2048]{2,1,0:T(8,128)(2,1)S(1)}, bf16[3,16,2048]{2,1,0:T(8,128)(2,1)S(1)}, u32[]{:S(2)}, u32[]{:S(2)}) collective-permute-start(bf16[3,16,2048]{2,1,0:T(8,128)(2,1)S(1)} %get-tuple-element.10.t0), channel_id=1, source_target_pairs={{0,4},{1,5},{2,6},{3,7},{4,0},{5,1},{6,2},{7,3},{8,12},{9,13},{10,... | collective-permute-start | bytes 589832 | tf_op jit(solution)/shard_map/ppermute | solution.py:362
  10.8 9.3 %collective-permute-start.3 = (bf16[3,16,2048]{2,1,0:T(8,128)(2,1)S(1)}, bf16[3,16,2048]{2,1,0:T(8,128)(2,1)S(1)}, u32[]{:S(2)}, u32[]{:S(2)}) collective-permute-start(bf16[3,16,2048]{2,1,0:T(8,128)(2,1)S(1)} %collective-permute-done.2.t2), channel_id=1, source_target_pairs={{0,4},{1,5},{2,6},{3,7},{4,0},{5,1},{6,2},{7,3},{8,12},{9,13},{10,... | collective-permute-start | bytes 589832 | tf_op jit(solution)/shard_map/ppermute | solution.py:362
  13.3 6.8 %copy-start.1 = (s32[128,4]{0,1:T(4,128)S(1)}, s32[128,4]{0,1:T(4,128)}, u32[]{:S(2)}) copy-start(s32[128,4]{0,1:T(4,128)} %param.7) | copy-start | bytes 6148
  14.0 4.4 %collective-permute-start.6 = (bf16[3,120,128]{2,1,0:T(8,128)(2,1)S(1)}, bf16[3,120,128]{2,1,0:T(8,128)(2,1)S(1)}, u32[]{:S(2)}, u32[]{:S(2)}) collective-permute-start(bf16[3,120,128]{2,1,0:T(8,128)(2,1)S(1)} %series.1.x0), channel_id=1, source_target_pairs={{0,8},{1,9},{2,10},{3,11},{4,12},{5,13},{6,14},{7,15},{8,0},{9,1},... | collective-permute-start | bytes 276488 | tf_op jit(solution)/shard_map/ppermute | solution.py:362
  15.4 3.8 %collective-permute-start.5 = (bf16[3,120,128]{2,1,0:T(8,128)(2,1)S(1)}, bf16[3,120,128]{2,1,0:T(8,128)(2,1)S(1)}, u32[]{:S(2)}, u32[]{:S(2)}) collective-permute-start(bf16[3,120,128]{2,1,0:T(8,128)(2,1)S(1)} %series.1.x0), channel_id=1, source_target_pairs={{0,4},{1,5},{2,6},{3,7},{4,0},{5,1},{6,2},{7,3},{8,12},{9,13},{10,... | collective-permute-start | bytes 276488 | tf_op jit(solution)/shard_map/ppermute | solution.py:362
  18.4 1.7 %collective-permute-start.7 = (bf16[3,120,128]{2,1,0:T(8,128)(2,1)S(1)}, bf16[3,120,128]{2,1,0:T(8,128)(2,1)S(1)}, u32[]{:S(2)}, u32[]{:S(2)}) collective-permute-start(bf16[3,120,128]{2,1,0:T(8,128)(2,1)S(1)} %collective-permute-done.6.x2), channel_id=1, source_target_pairs={{0,4},{1,5},{2,6},{3,7},{4,0},{5,1},{6,2},{7,3},{8,12},{9,13},{10,... | collective-permute-start | bytes 276488 | tf_op jit(solution)/shard_map/ppermute | solution.py:362
  28.7 7.0 %collective-permute-start.8 = (s16[16,3200]{1,0:T(8,128)(2,1)S(1)}, s16[16,3200]{1,0:T(8,128)(2,1)S(1)}, u32[]{:S(2)}, u32[]{:S(2)}) collective-permute-start(s16[16,3200]{1,0:T(8,128)(2,1)S(1)} %get-tuple-element.13), channel_id=1, source_target_pairs={{0,0},{1,4},{2,8},{3,12},{4,2},{5,6},{6,10},{7,14},{8,1},{9,5},{10... | collective-permute-start | bytes 307208 | tf_op jit(solution)/shard_map/ppermute | solution.py:367
  33.2 7.2 %collective-permute-start.9 = (s16[16,3200]{1,0:T(8,128)(2,1)S(1)}, s16[16,3200]{1,0:T(8,128)(2,1)S(1)}, u32[]{:S(2)}, u32[]{:S(2)}) collective-permute-start(s16[16,3200]{1,0:T(8,128)(2,1)S(1)} %get-tuple-element.14), channel_id=1, source_target_pairs={{0,1},{1,5},{2,9},{3,13},{4,3},{5,7},{6,11},{7,15},{8,0},{9,4},{10... | collective-permute-start | bytes 307208 | tf_op jit(solution)/shard_map/ppermute | solution.py:367

commit v4 on v3

--- a/solution.py
+++ b/solution.py
@@ -383,6 +383,7 @@
     series_y = swapped(series, 2, 0)
     series_c = swapped(series, 1, 0)
     series_yc = swapped(series_y, 1, 0)
+    panel_y, _ = lax.optimization_barrier((panel_y, series_y))
     panel_yc = swapped(panel_y, 1, 0)
     first, second = correlate_stations(
         (keep, panel_c, panel_y, panel_yc), (series, series_c, series_y, series_yc), masks.T, span, nb

time: 41.6 us -> 40 us (0.962)
  waiting for transfers between devices: 9.33 us -> 7.74 us
    ppermute x8, waiting for transfers between devices: 4.1 us -> 2.91 us  [swapped(): return lax.ppermute(value, ('loop', 'tgrp'), pairs)]
    ppermute x2, starting transfers between devices: 6.47 us -> 5.76 us  [to_owner(): return lax.ppermute(value, ('loop', 'tgrp'), pairs)]
    ppermute x8, starting transfers between devices: 11.6 us -> 12.1 us  [swapped(): return lax.ppermute(value, ('loop', 'tgrp'), pairs)]
  transfers between devices with their start and end apart: 10 -> 10, of which waited for: 5 -> 6; matrix products, arithmetic and copies ran while one was open for 0% -> 0% of each run, Pallas kernels for 3% -> 3%
where the time goes in v4:
time: 40 us; the launch traced here: 39.6 us
  starting transfers between devices  17.9 us (45%)
  Pallas kernels  10.9 us (27%)
  waiting for transfers between devices  7.74 us (19%)
  local copies, waits for them, and re-layouts  2.43 us (6%)
  between operations  0.72 us (2%)
    ppermute x8, starting transfers between devices, swapped(): return lax.ppermute(value, ('loop', 'tgrp'), pairs)  12.1 us
    pallas_call x1, Pallas kernels, correlate_stations(): pl.pallas_call(functools.partial(correlate_kernel, span, nb), out_shape=(...  8.54 us
    ppermute x2, starting transfers between devices, to_owner(): return lax.ppermute(value, ('loop', 'tgrp'), pairs)  5.76 us
    ppermute x2, waiting for transfers between devices, to_owner(): return lax.ppermute(value, ('loop', 'tgrp'), pairs)  4.83 us
    ppermute x8, waiting for transfers between devices, swapped(): return lax.ppermute(value, ('loop', 'tgrp'), pairs)  2.91 us
    unnamed x7, local copies, waits for them, and re-layouts  1.66 us
    pallas_call x1, Pallas kernels, decode(): pl.pallas_call(decode_kernel, out_shape=jax.ShapeDtypeStruct((2 * ROWS, f...  0.98 us
  transfers between devices with their start and end apart: 10, of which 6 were waited for; matrix products, arithmetic and copies ran while one was open for 0% of the time, Pallas kernels for 3%

profile of v4, /device:TPU:1, one launch (start us, length us, event | category | flops | bytes accessed | tf_op | source)
XLA Modules:
  0.0 39.6 jit_solution(1589272960489738032)
XLA Ops:
  0.0 0.8 %reshape.3.own = bf16[72,128]{1,0:T(8,128)(2,1)S(1)} reshape(bf16[1,3,3072]{2,1,0:T(4,128)(2,1)} %param.5) | data formatting | bytes 36864 | tf_op jit(solution)/shard_map/reshape | solution.py:375
  0.8 2.2 %collective-permute-start.1 = (bf16[72,128]{1,0:T(8,128)(2,1)S(1)}, bf16[72,128]{1,0:T(8,128)(2,1)S(1)}, u32[]{:S(2)}, u32[]{:S(2)}) collective-permute-start(bf16[72,128]{1,0:T(8,128)(2,1)S(1)} %reshape.3.own), channel_id=1, source_target_pairs={{0,1},{1,0},{2,3},{3,2},{4,5},{5,4},{6,7},{7,6},{8,9},{9,8},{10,11... | collective-permute-start | bytes 55304 | tf_op jit(solution)/shard_map/ppermute | solution.py:362
  3.0 0.7 %copy-done.2 = s32[1,3]{1,0:T(1,128)S(1)} copy-done((s32[1,3]{1,0:T(1,128)S(1)}, s32[1,3]{1,0:T(1,128)}, u32[]{:S(2)}) %copy-start.2) | copy-done | bytes 36
  3.6 1.0 %copy-done = bf16[32,1,3,2048]{3,0,2,1:T(8,128)(2,1)S(1)} copy-done((bf16[32,1,3,2048]{3,0,2,1:T(8,128)(2,1)S(1)}, bf16[32,1,3,2048]{3,0,2,1:T(8,128)(2,1)}, u32[]{:S(2)}) %copy-start) | copy-done | bytes 393240
  4.6 0.6 %split.1 = (bf16[3,16,2048]{2,1,0:T(8,128)(2,1)S(1)}, bf16[3,16,2048]{2,1,0:T(8,128)(2,1)S(1)}) custom-call(s32[1,3]{1,0:T(1,128)S(1)} %copy-done.2, bf16[3,32,2048]{2,1,0:T(8,128)(2,1)S(1)} %bitcast.4), custom_call_target="tpu_custom_call" | custom-call | tf_op jit(solution)/shard_map/split/pallas_call | solution.py:123
  5.3 1.3 %collective-permute-start.2 = (bf16[3,16,2048]{2,1,0:T(8,128)(2,1)S(1)}, bf16[3,16,2048]{2,1,0:T(8,128)(2,1)S(1)}, u32[]{:S(2)}, u32[]{:S(2)}) collective-permute-start(bf16[3,16,2048]{2,1,0:T(8,128)(2,1)S(1)} %get-tuple-element.13), channel_id=1, source_target_pairs={{0,8},{1,9},{2,10},{3,11},{4,12},{5,13},{6,14},{7,15},{8,0},{9,1},... | collective-permute-start | bytes 589832 | tf_op jit(solution)/shard_map/ppermute | solution.py:362
  6.6 2.3 %collective-permute-start.3 = (bf16[144,128]{1,0:T(8,128)(2,1)S(1)}, bf16[144,128]{1,0:T(8,128)(2,1)S(1)}, u32[]{:S(2)}, u32[]{:S(2)}) collective-permute-start(bf16[144,128]{1,0:T(8,128)(2,1)S(1)} %constant_dynamic-update-slice_fusion), channel_id=1, source_target_pairs={{0,2},{1,3},{2,0},{3,1},{4,6},{5,7},{6,4},{7,5},{8,10},{9,11},{10,... | collective-permute-start | bytes 110600 | tf_op jit(solution)/shard_map/ppermute | solution.py:362
  9.5 1.1 %collective-permute-done.3.far = bf16[144,128]{1,0:T(8,128)(2,1)S(1)} collective-permute-done((bf16[144,128]{1,0:T(8,128)(2,1)S(1)}, bf16[144,128]{1,0:T(8,128)(2,1)S(1)}, u32[]{:S(2)}, u32[]{:S(2)}) %collective-permute-start.3) | collective-permute-done | bytes 36896 | tf_op jit(solution)/shard_map/ppermute | solution.py:362
  10.6 0.7 %series.1.x0 = bf16[3,120,128]{2,1,0:T(8,128)(2,1)S(1)} custom-call(s32[1]{0:T(128)S(6)} %copy.7.offset, s32[1,3]{1,0:T(1,128)S(1)} %copy-done.2, bf16[72,128]{1,0:T(8,128)(2,1)S(1)} %reshape.3.own, bf16[72,128]{1,0:T(8,128)(2,1)S(1)} %collective-permute-done.1.d1, bf16[144,128]{1,0:T(8,128)(2,1)S(1)} %collective-permute-done.3.far), custom_call_target="tpu_custom_call" | custom-call | tf_op jit(solution)/shard_map/series/pallas_call | solution.py:154
  11.4 0.0 copy-start.1
  11.4 0.3 collective-permute-start.4
  11.7 2.3 %collective-permute-start = (bf16[3,16,2048]{2,1,0:T(8,128)(2,1)S(1)}, bf16[3,16,2048]{2,1,0:T(8,128)(2,1)S(1)}, u32[]{:S(2)}, u32[]{:S(2)}) collective-permute-start(bf16[3,16,2048]{2,1,0:T(8,128)(2,1)S(1)} %get-tuple-element.11.t0), channel_id=1, source_target_pairs={{0,4},{1,5},{2,6},{3,7},{4,0},{5,1},{6,2},{7,3},{8,12},{9,13},{10,... | collective-permute-start | bytes 589832 | tf_op jit(solution)/shard_map/ppermute | solution.py:362
  14.0 0.9 %collective-permute-done.4.x2 = bf16[3,120,128]{2,1,0:T(8,128)(2,1)S(1)} collective-permute-done((bf16[3,120,128]{2,1,0:T(8,128)(2,1)S(1)}, bf16[3,120,128]{2,1,0:T(8,128)(2,1)S(1)}, u32[]{:S(2)}, u32[]{:S(2)}) %collective-permute-start.4) | collective-permute-done | bytes 92192 | tf_op jit(solution)/shard_map/ppermute | solution.py:362
  14.8 3.2 %collective-permute-start.5 = (bf16[3,16,2048]{2,1,0:T(8,128)(2,1)S(1)}, bf16[3,16,2048]{2,1,0:T(8,128)(2,1)S(1)}, u32[]{:S(2)}, u32[]{:S(2)}) collective-permute-start(bf16[3,16,2048]{2,1,0:T(8,128)(2,1)S(1)} %collective-permute-done.2.t2), channel_id=1, source_target_pairs={{0,4},{1,5},{2,6},{3,7},{4,0},{5,1},{6,2},{7,3},{8,12},{9,13},{10,... | collective-permute-start | bytes 589832 | tf_op jit(solution)/shard_map/ppermute | solution.py:362
  18.0 0.0 collective-permute-start.6
  18.0 0.5 %collective-permute-start.7 = (bf16[3,120,128]{2,1,0:T(8,128)(2,1)S(1)}, bf16[3,120,128]{2,1,0:T(8,128)(2,1)S(1)}, u32[]{:S(2)}, u32[]{:S(2)}) collective-permute-start(bf16[3,120,128]{2,1,0:T(8,128)(2,1)S(1)} %collective-permute-done.4.x2), channel_id=1, source_target_pairs={{0,4},{1,5},{2,6},{3,7},{4,0},{5,1},{6,2},{7,3},{8,12},{9,13},{10,... | collective-permute-start | bytes 276488 | tf_op jit(solution)/shard_map/ppermute | solution.py:362
  18.5 0.8 %collective-permute-done.6.x1 = bf16[3,120,128]{2,1,0:T(8,128)(2,1)S(1)} collective-permute-done((bf16[3,120,128]{2,1,0:T(8,128)(2,1)S(1)}, bf16[3,120,128]{2,1,0:T(8,128)(2,1)S(1)}, u32[]{:S(2)}, u32[]{:S(2)}) %collective-permute-start.6) | collective-permute-done | bytes 92192 | tf_op jit(solution)/shard_map/ppermute | solution.py:362
  19.3 0.2 collective-permute-done.7.x3
  19.5 8.5 %correlate.1 = (s16[16,3200]{1,0:T(8,128)(2,1)S(1)}, s16[16,3200]{1,0:T(8,128)(2,1)S(1)}) custom-call(bf16[3,16,2048]{2,1,0:T(8,128)(2,1)S(1)} %get-tuple-element.11.t0, bf16[3,16,2048]{2,1,0:T(8,128)(2,1)S(1)} %collective-permute-done.t1, bf16[3,16,2048]{2,1,0:T(8,128)(2,1)S(1)} %collective-permute-done.2.t2, ...), custom_call_target="tpu_custom_call" | custom-call | tf_op jit(solution)/shard_map/correlate/pallas_call | solution.py:338
  28.0 4.6 %collective-permute-start.8 = (s16[16,3200]{1,0:T(8,128)(2,1)S(1)}, s16[16,3200]{1,0:T(8,128)(2,1)S(1)}, u32[]{:S(2)}, u32[]{:S(2)}) collective-permute-start(s16[16,3200]{1,0:T(8,128)(2,1)S(1)} %get-tuple-element.15), channel_id=1, source_target_pairs={{0,0},{1,4},{2,8},{3,12},{4,2},{5,6},{6,10},{7,14},{8,1},{9,5},{10... | collective-permute-start | bytes 307208 | tf_op jit(solution)/shard_map/ppermute | solution.py:367
  32.6 1.2 %collective-permute-start.9 = (s16[16,3200]{1,0:T(8,128)(2,1)S(1)}, s16[16,3200]{1,0:T(8,128)(2,1)S(1)}, u32[]{:S(2)}, u32[]{:S(2)}) collective-permute-start(s16[16,3200]{1,0:T(8,128)(2,1)S(1)} %get-tuple-element.16), channel_id=1, source_target_pairs={{0,1},{1,5},{2,9},{3,13},{4,3},{5,7},{6,11},{7,15},{8,0},{9,4},{10... | collective-permute-start | bytes 307208 | tf_op jit(solution)/shard_map/ppermute | solution.py:367
  33.8 1.2 %collective-permute-done.8.a_ref = s16[16,3200]{1,0:T(8,128)(2,1)S(1)} collective-permute-done((s16[16,3200]{1,0:T(8,128)(2,1)S(1)}, s16[16,3200]{1,0:T(8,128)(2,1)S(1)}, u32[]{:S(2)}, u32[]{:S(2)}) %collective-permute-start.8) | collective-permute-done | bytes 102432 | tf_op jit(solution)/shard_map/ppermute | solution.py:367
  35.0 3.6 %collective-permute-done.9.b_ref = s16[16,3200]{1,0:T(8,128)(2,1)S(1)} collective-permute-done((s16[16,3200]{1,0:T(8,128)(2,1)S(1)}, s16[16,3200]{1,0:T(8,128)(2,1)S(1)}, u32[]{:S(2)}, u32[]{:S(2)}) %collective-permute-start.9) | collective-permute-done | bytes 102432 | tf_op jit(solution)/shard_map/ppermute | solution.py:367
  38.6 1.0 %decode.1 = f32[32,3072]{1,0:T(8,128)} custom-call(s16[16,3200]{1,0:T(8,128)(2,1)S(1)} %collective-permute-done.8.a_ref, s16[16,3200]{1,0:T(8,128)(2,1)S(1)} %collective-permute-done.9.b_ref), custom_call_target="tpu_custom_call" | custom-call | tf_op jit(solution)/shard_map/decode/pallas_call | solution.py:323
  (9 shorter events, 0.0 us)
Async XLA Ops:
  0.8 4.5 %collective-permute-start.1 = (bf16[72,128]{1,0:T(8,128)(2,1)S(1)}, bf16[72,128]{1,0:T(8,128)(2,1)S(1)}, u32[]{:S(2)}, u32[]{:S(2)}) collective-permute-start(bf16[72,128]{1,0:T(8,128)(2,1)S(1)} %reshape.3.own), channel_id=1, source_target_pairs={{0,1},{1,0},{2,3},{3,2},{4,5},{5,4},{6,7},{7,6},{8,9},{9,8},{10,11... | collective-permute-start | bytes 55304 | tf_op jit(solution)/shard_map/ppermute | solution.py:362
  3.0 0.7 %copy-start.2 = (s32[1,3]{1,0:T(1,128)S(1)}, s32[1,3]{1,0:T(1,128)}, u32[]{:S(2)}) copy-start(s32[1,3]{1,0:T(1,128)} %active.3) | copy-start | bytes 40
  3.6 1.0 %copy-start = (bf16[32,1,3,2048]{3,0,2,1:T(8,128)(2,1)S(1)}, bf16[32,1,3,2048]{3,0,2,1:T(8,128)(2,1)}, u32[]{:S(2)}) copy-start(bf16[32,1,3,2048]{3,0,2,1:T(8,128)(2,1)} %param.6) | copy-start | bytes 1179652
  5.3 9.6 %collective-permute-start.2 = (bf16[3,16,2048]{2,1,0:T(8,128)(2,1)S(1)}, bf16[3,16,2048]{2,1,0:T(8,128)(2,1)S(1)}, u32[]{:S(2)}, u32[]{:S(2)}) collective-permute-start(bf16[3,16,2048]{2,1,0:T(8,128)(2,1)S(1)} %get-tuple-element.13), channel_id=1, source_target_pairs={{0,8},{1,9},{2,10},{3,11},{4,12},{5,13},{6,14},{7,15},{8,0},{9,1},... | collective-permute-start | bytes 589832 | tf_op jit(solution)/shard_map/ppermute | solution.py:362
  6.6 4.1 %collective-permute-start.3 = (bf16[144,128]{1,0:T(8,128)(2,1)S(1)}, bf16[144,128]{1,0:T(8,128)(2,1)S(1)}, u32[]{:S(2)}, u32[]{:S(2)}) collective-permute-start(bf16[144,128]{1,0:T(8,128)(2,1)S(1)} %constant_dynamic-update-slice_fusion), channel_id=1, source_target_pairs={{0,2},{1,3},{2,0},{3,1},{4,6},{5,7},{6,4},{7,5},{8,10},{9,11},{10,... | collective-permute-start | bytes 110600 | tf_op jit(solution)/shard_map/ppermute | solution.py:362
  11.4 8.1 %copy-start.1 = (s32[128,4]{0,1:T(4,128)S(1)}, s32[128,4]{0,1:T(4,128)}, u32[]{:S(2)}) copy-start(s32[128,4]{0,1:T(4,128)} %param.7) | copy-start | bytes 6148
  11.4 3.5 %collective-permute-start.4 = (bf16[3,120,128]{2,1,0:T(8,128)(2,1)S(1)}, bf16[3,120,128]{2,1,0:T(8,128)(2,1)S(1)}, u32[]{:S(2)}, u32[]{:S(2)}) collective-permute-start(bf16[3,120,128]{2,1,0:T(8,128)(2,1)S(1)} %series.1.x0), channel_id=1, source_target_pairs={{0,8},{1,9},{2,10},{3,11},{4,12},{5,13},{6,14},{7,15},{8,0},{9,1},... | collective-permute-start | bytes 276488 | tf_op jit(solution)/shard_map/ppermute | solution.py:362
  11.7 7.7 %collective-permute-start = (bf16[3,16,2048]{2,1,0:T(8,128)(2,1)S(1)}, bf16[3,16,2048]{2,1,0:T(8,128)(2,1)S(1)}, u32[]{:S(2)}, u32[]{:S(2)}) collective-permute-start(bf16[3,16,2048]{2,1,0:T(8,128)(2,1)S(1)} %get-tuple-element.11.t0), channel_id=1, source_target_pairs={{0,4},{1,5},{2,6},{3,7},{4,0},{5,1},{6,2},{7,3},{8,12},{9,13},{10,... | collective-permute-start | bytes 589832 | tf_op jit(solution)/shard_map/ppermute | solution.py:362
  14.8 4.6 %collective-permute-start.5 = (bf16[3,16,2048]{2,1,0:T(8,128)(2,1)S(1)}, bf16[3,16,2048]{2,1,0:T(8,128)(2,1)S(1)}, u32[]{:S(2)}, u32[]{:S(2)}) collective-permute-start(bf16[3,16,2048]{2,1,0:T(8,128)(2,1)S(1)} %collective-permute-done.2.t2), channel_id=1, source_target_pairs={{0,4},{1,5},{2,6},{3,7},{4,0},{5,1},{6,2},{7,3},{8,12},{9,13},{10,... | collective-permute-start | bytes 589832 | tf_op jit(solution)/shard_map/ppermute | solution.py:362
  18.0 1.3 %collective-permute-start.6 = (bf16[3,120,128]{2,1,0:T(8,128)(2,1)S(1)}, bf16[3,120,128]{2,1,0:T(8,128)(2,1)S(1)}, u32[]{:S(2)}, u32[]{:S(2)}) collective-permute-start(bf16[3,120,128]{2,1,0:T(8,128)(2,1)S(1)} %series.1.x0), channel_id=1, source_target_pairs={{0,4},{1,5},{2,6},{3,7},{4,0},{5,1},{6,2},{7,3},{8,12},{9,13},{10,... | collective-permute-start | bytes 276488 | tf_op jit(solution)/shard_map/ppermute | solution.py:362
  18.0 1.4 %collective-permute-start.7 = (bf16[3,120,128]{2,1,0:T(8,128)(2,1)S(1)}, bf16[3,120,128]{2,1,0:T(8,128)(2,1)S(1)}, u32[]{:S(2)}, u32[]{:S(2)}) collective-permute-start(bf16[3,120,128]{2,1,0:T(8,128)(2,1)S(1)} %collective-permute-done.4.x2), channel_id=1, source_target_pairs={{0,4},{1,5},{2,6},{3,7},{4,0},{5,1},{6,2},{7,3},{8,12},{9,13},{10,... | collective-permute-start | bytes 276488 | tf_op jit(solution)/shard_map/ppermute | solution.py:362
  28.0 7.0 %collective-permute-start.8 = (s16[16,3200]{1,0:T(8,128)(2,1)S(1)}, s16[16,3200]{1,0:T(8,128)(2,1)S(1)}, u32[]{:S(2)}, u32[]{:S(2)}) collective-permute-start(s16[16,3200]{1,0:T(8,128)(2,1)S(1)} %get-tuple-element.15), channel_id=1, source_target_pairs={{0,0},{1,4},{2,8},{3,12},{4,2},{5,6},{6,10},{7,14},{8,1},{9,5},{10... | collective-permute-start | bytes 307208 | tf_op jit(solution)/shard_map/ppermute | solution.py:367
  32.6 6.0 %collective-permute-start.9 = (s16[16,3200]{1,0:T(8,128)(2,1)S(1)}, s16[16,3200]{1,0:T(8,128)(2,1)S(1)}, u32[]{:S(2)}, u32[]{:S(2)}) collective-permute-start(s16[16,3200]{1,0:T(8,128)(2,1)S(1)} %get-tuple-element.16), channel_id=1, source_target_pairs={{0,1},{1,5},{2,9},{3,13},{4,3},{5,7},{6,11},{7,15},{8,0},{9,4},{10... | collective-permute-start | bytes 307208 | tf_op jit(solution)/shard_map/ppermute | solution.py:367

commit v5 on v3

--- a/solution.py
+++ b/solution.py
@@ -109,71 +109,93 @@
     return lax.broadcasted_iota(jnp.int32, shape, len(shape) - 1)
 
 
-def split_kernel(active, t_ref, keep_ref, send_ref):
+def split_kernel(offset, active, t_ref, keep_ref, send_ref):
     half = lax.axis_index("loop") // 2
+    span = t_ref.shape[2]
+    sub = lax.broadcasted_iota(jnp.int32, (ROWS, 128), 0)
+    high, low = (offset[0] // 32).astype(jnp.float32), (offset[0] % 32).astype(jnp.float32)
     for c in range(3):
         on = active[0, c].astype(jnp.float32)
+        told = jnp.where(sub == 0, high, jnp.where(sub == 1, low, jnp.where(sub == 2, on, 0.0)))
         for out, first in ((keep_ref, half), (send_ref, 1 - half)):
             rows = t_ref[c, pl.ds(pl.multiple_of(ROWS * first, ROWS), ROWS), :]
-            out[c] = (rows.astype(jnp.float32) * on).astype(jnp.bfloat16)
-
-
-def split(active, panel):
-    half = jax.ShapeDtypeStruct((3, ROWS, panel.shape[2]), jnp.bfloat16)
+            out[c, :, :span] = (rows.astype(jnp.float32) * on).astype(jnp.bfloat16)
+            out[c, :, span:] = told.astype(jnp.bfloat16)
+
+
+def split(offset, active, panel):
+    half = jax.ShapeDtypeStruct((3, ROWS, panel.shape[2] + 128), jnp.bfloat16)
     return pl.pallas_call(
         split_kernel,
         out_shape=(half, half),
-        in_specs=[pl.BlockSpec(memory_space=pltpu.SMEM), pl.BlockSpec(memory_space=pltpu.VMEM)],
+        in_specs=[pl.BlockSpec(memory_space=pltpu.SMEM)] * 2 + [pl.BlockSpec(memory_space=pltpu.VMEM)],
         out_specs=(pl.BlockSpec(memory_space=pltpu.VMEM),) * 2,
         compiler_params=pltpu.CompilerParams(vmem_limit_bytes=4 << 20),
         name="split",
-    )(active, panel)
-
-
-def series_kernel(blocks, offset, active, own, d1, far, x_ref, whole):
+    )(offset, active, panel)
+
+
+def series_kernel(blocks, offset, active, told, near, far, mine_ref, mate_ref, whole):
     z = lax.axis_index("tgrp")
-    rows = x_ref.shape[1]
-    for c in range(3):
-        whole[c, 4 * blocks :] = jnp.zeros((whole.shape[1] - 4 * blocks, 128), jnp.float32)
-    wide = [own[...].astype(jnp.float32), d1[...].astype(jnp.float32), far[...].astype(jnp.float32)]
+    core = lax.axis_index("loop") % 2
+    rows = mine_ref.shape[1]
+    span = told.shape[2] - 128
+    lane = lanes((rows, 128))
+    whole[:, 4 * blocks :] = jnp.zeros((6, whole.shape[1] - 4 * blocks, 128), jnp.float32)
+    wide = [near[...].astype(jnp.float32), far[...].astype(jnp.float32)]
     for b in range(4):
         at = pl.multiple_of(blocks * (z ^ b), 8)
+        for i in range(6):
+            first = 6 * blocks * (b % 2) + i * blocks
+            whole[i, pl.ds(at, blocks), :] = wide[b // 2][first : first + blocks]
+    for station in range(2):
+        if station == 0:
+            shift = offset[0]
+        else:
+            words = told[0, :, span:].astype(jnp.float32)
+            shift = (32.0 * jnp.max(words[0:1]) + jnp.max(words[1:2])).astype(jnp.int32)
+        row, turn = shift // 128, shift % 128
+        spill = lane >= 128 - turn
         for c in range(3):
-            first = c * blocks + (3 * blocks if b == 3 else 0)
-            whole[c, pl.ds(at, blocks), :] = wide[min(b, 2)][first : first + blocks]
-    row, lane = offset[0] // 128, offset[0] % 128
-    spill = lanes((rows, 128)) >= 128 - lane
-    for c in range(3):
-        on = active[0, c].astype(jnp.float32)
-        here = pltpu.roll(whole[c, pl.ds(row, rows), :], 128 - lane, 1)
-        after = pltpu.roll(whole[c, pl.ds(row + 1, rows), :], 128 - lane, 1)
-        x_ref[c] = (jnp.where(spill, after, here) * on).astype(jnp.bfloat16)
-
-
-def make_series(offset, active, pieces, blocks, rows):
+            i = 3 * station + c
+            if station == 0:
+                on = active[0, c].astype(jnp.float32)
+            else:
+                on = told[c, :, span:].astype(jnp.float32)[2:3]
+            for out, half in ((mine_ref, core), (mate_ref, 1 - core)):
+                at = row + 2 * blocks * half
+                here = pltpu.roll(whole[i, pl.ds(at, rows), :], 128 - turn, 1)
+                after = pltpu.roll(whole[i, pl.ds(at + 1, rows), :], 128 - turn, 1)
+                out[i] = (jnp.where(spill, after, here) * on).astype(jnp.bfloat16)
+
+
+def make_series(offset, active, told, near, far, blocks, rows):
+    window = jax.ShapeDtypeStruct((6, rows, 128), jnp.bfloat16)
+    vmem = pl.BlockSpec(memory_space=pltpu.VMEM)
     return pl.pallas_call(
         functools.partial(series_kernel, blocks),
-        out_shape=jax.ShapeDtypeStruct((3, rows, 128), jnp.bfloat16),
-        in_specs=[pl.BlockSpec(memory_space=pltpu.SMEM)] * 2 + [pl.BlockSpec(memory_space=pltpu.VMEM)] * 3,
-        out_specs=pl.BlockSpec(memory_space=pltpu.VMEM),
-        scratch_shapes=[pltpu.VMEM((3, rows + 8, 128), jnp.float32)],
+        out_shape=(window, window),
+        in_specs=[pl.BlockSpec(memory_space=pltpu.SMEM)] * 2 + [vmem] * 3,
+        out_specs=(vmem, vmem),
+        scratch_shapes=[pltpu.VMEM((6, 2 * blocks + rows + 8, 128), jnp.float32)],
         compiler_params=pltpu.CompilerParams(vmem_limit_bytes=4 << 20),
         name="series",
-    )(offset, active, *pieces)
-
-
-def correlate_kernel(span, nb, t0, t1, t2, t3, x0, x1, x2, x3, masks, first_ref, second_ref,
+    )(offset, active, told, near, far)
+
+
+def correlate_kernel(span, nb, t0, t1, t2, t3, mine, mate, masks, first_ref, second_ref,
                      tp_ref, xb_ref, xf_ref, a_ref, z_ref, d_ref, acc_ref, tot_ref, tr_ref, sems):
     lb = span // 128
     kb = lb + 1
     rows = xf_ref.shape[1]
     loop_at = lax.axis_index("loop")
-    half, core = loop_at // 2, loop_at % 2
-    x_first = pl.multiple_of(2 * nb * core, 16)
+    half = loop_at // 2
     copies = []
-    for s, (t, x) in enumerate(((t0, x0), (t1, x1), (t2, x2), (t3, x3))):
+    for s, t in enumerate((t0, t1, t2, t3)):
+        x = (mine, mate)[s % 2].at[pl.ds(3 * (s // 2), 3)]
+        t = t.at[:, :, pl.ds(0, span)]
         copies.append(pltpu.make_async_copy(t, tp_ref.at[pl.ds(3 * s, 3), :, pl.ds(128, span)], sems.at[2 * s]))
-        copies.append(pltpu.make_async_copy(x.at[:, pl.ds(x_first, rows), :], xb_ref.at[pl.ds(3 * s, 3)], sems.at[2 * s + 1]))
+        copies.append(pltpu.make_async_copy(x, xb_ref.at[pl.ds(3 * s, 3)], sems.at[2 * s + 1]))
     for copy in copies:
         copy.start()
     tp_ref[:, :, 0:128] = jnp.zeros((12, ROWS, 128), jnp.bfloat16)
@@ -332,13 +354,13 @@
 
 def correlate_stations(panels, series, masks, span, nb):
     lb = span // 128
-    rows = 2 * nb + lb + 8
+    rows = series[0].shape[1]
     block = jax.ShapeDtypeStruct((ROWS, 128 * nb + 128), jnp.int16)
     vmem = pl.BlockSpec(memory_space=pltpu.VMEM)
     return pl.pallas_call(
         functools.partial(correlate_kernel, span, nb),
         out_shape=(block, block),
-        in_specs=[pl.BlockSpec(memory_space=pl.ANY)] * 8 + [vmem],
+        in_specs=[pl.BlockSpec(memory_space=pl.ANY)] * 6 + [vmem],
         out_specs=(vmem, vmem),
         scratch_shapes=[
             pltpu.VMEM((12, ROWS, span + 256), jnp.bfloat16),
@@ -371,21 +393,19 @@
     span = templates.shape[3]
     nb = data.shape[2] // 128
     panel = templates[:, 0].transpose(1, 0, 2)
-    keep, send = split(active, panel)
-    pieces = data.reshape(3 * nb, 128)
-    d1 = swapped(pieces, 0, 1)
-    near = jnp.concatenate([pieces, d1], axis=0)
-    send, _ = lax.optimization_barrier((send, near))
-    far = swapped(near, 0, 2)
+    keep, send = split(offsets, active, panel)
     panel_y = swapped(send, 2, 0)
     panel_c = swapped(keep, 1, 0)
-    series = make_series(offsets, active, (pieces, d1, far), nb, 4 * nb + span // 128 + 8)
-    series_y = swapped(series, 2, 0)
-    series_c = swapped(series, 1, 0)
-    series_yc = swapped(series_y, 1, 0)
-    panel_yc = swapped(panel_y, 1, 0)
+    pieces = data.reshape(3 * nb, 128)
+    pair = jnp.concatenate([pieces, swapped(pieces, 2, 0)], axis=0)
+    near = jnp.concatenate([pair, swapped(pair, 0, 1)], axis=0)
+    far = swapped(near, 0, 2)
+    mine, mate = make_series(offsets, active, panel_y, near, far, nb, 2 * nb + span // 128 + 8)
+    mate = swapped(mate, 1, 0)
+    panel_late, _ = lax.optimization_barrier((panel_y, far))
+    panel_yc = swapped(panel_late, 1, 0)
     first, second = correlate_stations(
-        (keep, panel_c, panel_y, panel_yc), (series, series_c, series_y, series_yc), masks.T, span, nb
+        (keep, panel_c, panel_y, panel_yc), (mine, mate), masks.T, span, nb
     )
     return decode(to_owner(first, 0), to_owner(second, 1))
 

time: 41.6 us -> 40.1 us (0.964); the launches traced: 41.4 us -> 39.3 us
  waiting for transfers between devices: 9.33 us -> 6.64 us
    ppermute x8 -> x7, waiting for transfers between devices: 4.1 us -> 2.65 us  [swapped(): return lax.ppermute(value, ('loop', 'tgrp'), pairs)]
    ppermute x2, waiting for transfers between devices: 5.23 us -> 3.99 us  [to_owner(): return lax.ppermute(value, ('loop', 'tgrp'), pairs)]
    ppermute x8 -> x7, starting transfers between devices: 11.6 us -> 11.4 us  [swapped(): return lax.ppermute(value, ('loop', 'tgrp'), pairs)]
    unnamed x7 -> x8, local copies, waits for them, and re-layouts: 1.66 us -> 1.66 us
  transfers between devices with their start and end apart: 10 -> 9, of which waited for: 5 -> 4; matrix products, arithmetic and copies ran while one was open for 0% -> 0% of each run, Pallas kernels for 3% -> 4%
where the time goes in v5:
time: 40.1 us; the launch traced here: 39.3 us
  starting transfers between devices  18.2 us (45%)
  Pallas kernels  11.3 us (28%)
  waiting for transfers between devices  6.64 us (17%)
  local copies, waits for them, and re-layouts  2.44 us (6%)
  between operations  0.75 us (2%)
    ppermute x7, starting transfers between devices, swapped(): return lax.ppermute(value, ('loop', 'tgrp'), pairs)  11.4 us
    pallas_call x1, Pallas kernels, correlate_stations(): pl.pallas_call(functools.partial(correlate_kernel, span, nb), out_shape=(...  8.73 us
    ppermute x2, starting transfers between devices, to_owner(): return lax.ppermute(value, ('loop', 'tgrp'), pairs)  6.8 us
    ppermute x2, waiting for transfers between devices, to_owner(): return lax.ppermute(value, ('loop', 'tgrp'), pairs)  3.99 us
    ppermute x7, waiting for transfers between devices, swapped(): return lax.ppermute(value, ('loop', 'tgrp'), pairs)  2.65 us
    unnamed x8, local copies, waits for them, and re-layouts  1.66 us
    pallas_call x1, Pallas kernels, make_series(): pl.pallas_call(functools.partial(series_kernel, blocks), out_shape=(windo...  1 us
    pallas_call x1, Pallas kernels, decode(): pl.pallas_call(decode_kernel, out_shape=jax.ShapeDtypeStruct((2 * ROWS, f...  0.98 us
  transfers between devices with their start and end apart: 9, of which 4 were waited for; matrix products, arithmetic and copies ran while one was open for 0% of the time, Pallas kernels for 4%

profile of v5, /device:TPU:1, one launch (start us, length us, event | category | flops | bytes accessed | tf_op | source)
XLA Modules:
  0.0 39.3 jit_solution(16461747503360214544)
XLA Ops:
  0.0 0.8 %reshape.3 = bf16[72,128]{1,0:T(8,128)(2,1)S(1)} reshape(bf16[1,3,3072]{2,1,0:T(4,128)(2,1)} %param.5) | data formatting | bytes 36864 | tf_op jit(solution)/shard_map/reshape | solution.py:399
  0.8 2.1 %collective-permute-start.2 = (bf16[72,128]{1,0:T(8,128)(2,1)S(1)}, bf16[72,128]{1,0:T(8,128)(2,1)S(1)}, u32[]{:S(2)}, u32[]{:S(2)}) collective-permute-start(bf16[72,128]{1,0:T(8,128)(2,1)S(1)} %reshape.3), channel_id=1, source_target_pairs={{0,8},{1,9},{2,10},{3,11},{4,12},{5,13},{6,14},{7,15},{8,0},{9,1},... | collective-permute-start | bytes 55304 | tf_op jit(solution)/shard_map/ppermute | solution.py:384
  3.5 0.0 copy-start.2
  3.6 0.6 %copy-done.2 = s32[1,3]{1,0:T(1,128)S(1)} copy-done((s32[1,3]{1,0:T(1,128)S(1)}, s32[1,3]{1,0:T(1,128)}, u32[]{:S(2)}) %copy-start.2) | copy-done | bytes 36
  4.2 1.0 %copy-done = bf16[32,1,3,2048]{3,0,2,1:T(8,128)(2,1)S(1)} copy-done((bf16[32,1,3,2048]{3,0,2,1:T(8,128)(2,1)S(1)}, bf16[32,1,3,2048]{3,0,2,1:T(8,128)(2,1)}, u32[]{:S(2)}) %copy-start) | copy-done | bytes 393240
  5.2 0.6 %split.1 = (bf16[3,16,2176]{2,1,0:T(8,128)(2,1)S(1)}, bf16[3,16,2176]{2,1,0:T(8,128)(2,1)S(1)}) custom-call(s32[1]{0:T(128)S(6)} %copy.8.offset, s32[1,3]{1,0:T(1,128)S(1)} %copy-done.2, bf16[3,32,2048]{2,1,0:T(8,128)(2,1)S(1)} %bitcast.4), custom_call_target="tpu_custom_call" | custom-call | tf_op jit(solution)/shard_map/split/pallas_call | solution.py:128
  5.8 0.1 collective-permute-start.1
  6.0 1.6 %collective-permute-start.3 = (bf16[144,128]{1,0:T(8,128)(2,1)S(1)}, bf16[144,128]{1,0:T(8,128)(2,1)S(1)}, u32[]{:S(2)}, u32[]{:S(2)}) collective-permute-start(bf16[144,128]{1,0:T(8,128)(2,1)S(1)} %pad_maximum_fusion), channel_id=1, source_target_pairs={{0,1},{1,0},{2,3},{3,2},{4,5},{5,4},{6,7},{7,6},{8,9},{9,8},{10,11... | collective-permute-start | bytes 110600 | tf_op jit(solution)/shard_map/ppermute | solution.py:384
  7.5 1.3 %collective-permute-done.3 = bf16[144,128]{1,0:T(8,128)(2,1)S(1)} collective-permute-done((bf16[144,128]{1,0:T(8,128)(2,1)S(1)}, bf16[144,128]{1,0:T(8,128)(2,1)S(1)}, u32[]{:S(2)}, u32[]{:S(2)}) %collective-permute-start.3) | collective-permute-done | bytes 36896 | tf_op jit(solution)/shard_map/ppermute | solution.py:384
  8.9 2.5 %collective-permute-start.4 = (bf16[288,128]{1,0:T(8,128)(2,1)S(1)}, bf16[288,128]{1,0:T(8,128)(2,1)S(1)}, u32[]{:S(2)}, u32[]{:S(2)}) collective-permute-start(bf16[288,128]{1,0:T(8,128)(2,1)S(1)} %constant_dynamic-update-slice_fusion.near), channel_id=1, source_target_pairs={{0,2},{1,3},{2,0},{3,1},{4,6},{5,7},{6,4},{7,5},{8,10},{9,11},{10,... | collective-permute-start | bytes 221192 | tf_op jit(solution)/shard_map/ppermute | solution.py:384
  11.4 2.7 %collective-permute-start = (bf16[3,16,2176]{2,1,0:T(8,128)(2,1)S(1)}, bf16[3,16,2176]{2,1,0:T(8,128)(2,1)S(1)}, u32[]{:S(2)}, u32[]{:S(2)}) collective-permute-start(bf16[3,16,2176]{2,1,0:T(8,128)(2,1)S(1)} %get-tuple-element.12.t0), channel_id=1, source_target_pairs={{0,4},{1,5},{2,6},{3,7},{4,0},{5,1},{6,2},{7,3},{8,12},{9,13},{10,... | collective-permute-start | bytes 626696 | tf_op jit(solution)/shard_map/ppermute | solution.py:384
  14.1 0.0 collective-permute-done.4.far
  14.1 0.0 collective-permute-done.1.told.t2
  14.1 2.3 %collective-permute-start.5 = (bf16[3,16,2176]{2,1,0:T(8,128)(2,1)S(1)}, bf16[3,16,2176]{2,1,0:T(8,128)(2,1)S(1)}, u32[]{:S(2)}, u32[]{:S(2)}) collective-permute-start(bf16[3,16,2176]{2,1,0:T(8,128)(2,1)S(1)} %collective-permute-done.1.told.t2), channel_id=1, source_target_pairs={{0,4},{1,5},{2,6},{3,7},{4,0},{5,1},{6,2},{7,3},{8,12},{9,13},{10,... | collective-permute-start | bytes 626696 | tf_op jit(solution)/shard_map/ppermute | solution.py:384
  16.4 1.0 %series.1 = (bf16[6,72,128]{2,1,0:T(8,128)(2,1)S(1)}, bf16[6,72,128]{2,1,0:T(8,128)(2,1)S(1)}) custom-call(s32[1]{0:T(128)S(6)} %copy.8.offset, s32[1,3]{1,0:T(1,128)S(1)} %copy-done.2, bf16[3,16,2176]{2,1,0:T(8,128)(2,1)S(1)} %collective-permute-done.1.told.t2, bf16[288,128]{1,0:T(8,128)(2,1)S(1)} %constant_dynamic-update-slice_fusion.near, ...), custom_call_target="tpu_custom_call" | custom-call | tf_op jit(solution)/shard_map/series/pallas_call | solution.py:175
  17.4 0.0 copy-start.1
  17.4 0.1 collective-permute-start.6
  17.5 1.3 %collective-permute-done.6.mate = bf16[6,72,128]{2,1,0:T(8,128)(2,1)S(1)} collective-permute-done((bf16[6,72,128]{2,1,0:T(8,128)(2,1)S(1)}, bf16[6,72,128]{2,1,0:T(8,128)(2,1)S(1)}, u32[]{:S(2)}, u32[]{:S(2)}) %collective-permute-start.6) | collective-permute-done | bytes 110624 | tf_op jit(solution)/shard_map/ppermute | solution.py:384
  18.8 8.7 %correlate.1 = (s16[16,3200]{1,0:T(8,128)(2,1)S(1)}, s16[16,3200]{1,0:T(8,128)(2,1)S(1)}) custom-call(bf16[3,16,2176]{2,1,0:T(8,128)(2,1)S(1)} %get-tuple-element.12.t0, bf16[3,16,2176]{2,1,0:T(8,128)(2,1)S(1)} %collective-permute-done.t1, bf16[3,16,2176]{2,1,0:T(8,128)(2,1)S(1)} %collective-permute-done.1.told.t2, ...), custom_call_target="tpu_custom_call" | custom-call | tf_op jit(solution)/shard_map/correlate/pallas_call | solution.py:360
  27.5 4.7 %collective-permute-start.7 = (s16[16,3200]{1,0:T(8,128)(2,1)S(1)}, s16[16,3200]{1,0:T(8,128)(2,1)S(1)}, u32[]{:S(2)}, u32[]{:S(2)}) collective-permute-start(s16[16,3200]{1,0:T(8,128)(2,1)S(1)} %get-tuple-element.17), channel_id=1, source_target_pairs={{0,0},{1,4},{2,8},{3,12},{4,2},{5,6},{6,10},{7,14},{8,1},{9,5},{10... | collective-permute-start | bytes 307208 | tf_op jit(solution)/shard_map/ppermute | solution.py:389
  32.2 2.1 %collective-permute-start.8 = (s16[16,3200]{1,0:T(8,128)(2,1)S(1)}, s16[16,3200]{1,0:T(8,128)(2,1)S(1)}, u32[]{:S(2)}, u32[]{:S(2)}) collective-permute-start(s16[16,3200]{1,0:T(8,128)(2,1)S(1)} %get-tuple-element.18), channel_id=1, source_target_pairs={{0,1},{1,5},{2,9},{3,13},{4,3},{5,7},{6,11},{7,15},{8,0},{9,4},{10... | collective-permute-start | bytes 307208 | tf_op jit(solution)/shard_map/ppermute | solution.py:389
  34.4 0.2 collective-permute-done.7.a_ref
  34.5 3.8 %collective-permute-done.8.b_ref = s16[16,3200]{1,0:T(8,128)(2,1)S(1)} collective-permute-done((s16[16,3200]{1,0:T(8,128)(2,1)S(1)}, s16[16,3200]{1,0:T(8,128)(2,1)S(1)}, u32[]{:S(2)}, u32[]{:S(2)}) %collective-permute-start.8) | collective-permute-done | bytes 102432 | tf_op jit(solution)/shard_map/ppermute | solution.py:389
  38.3 1.0 %decode.1 = f32[32,3072]{1,0:T(8,128)} custom-call(s16[16,3200]{1,0:T(8,128)(2,1)S(1)} %collective-permute-done.7.a_ref, s16[16,3200]{1,0:T(8,128)(2,1)S(1)} %collective-permute-done.8.b_ref), custom_call_target="tpu_custom_call" | custom-call | tf_op jit(solution)/shard_map/decode/pallas_call | solution.py:345
  (9 shorter events, 0.0 us)
Async XLA Ops:
  0.8 5.2 %collective-permute-start.2 = (bf16[72,128]{1,0:T(8,128)(2,1)S(1)}, bf16[72,128]{1,0:T(8,128)(2,1)S(1)}, u32[]{:S(2)}, u32[]{:S(2)}) collective-permute-start(bf16[72,128]{1,0:T(8,128)(2,1)S(1)} %reshape.3), channel_id=1, source_target_pairs={{0,8},{1,9},{2,10},{3,11},{4,12},{5,13},{6,14},{7,15},{8,0},{9,1},... | collective-permute-start | bytes 55304 | tf_op jit(solution)/shard_map/ppermute | solution.py:384
  3.5 0.7 %copy-start.2 = (s32[1,3]{1,0:T(1,128)S(1)}, s32[1,3]{1,0:T(1,128)}, u32[]{:S(2)}) copy-start(s32[1,3]{1,0:T(1,128)} %active.3) | copy-start | bytes 40
  4.2 1.0 %copy-start = (bf16[32,1,3,2048]{3,0,2,1:T(8,128)(2,1)S(1)}, bf16[32,1,3,2048]{3,0,2,1:T(8,128)(2,1)}, u32[]{:S(2)}) copy-start(bf16[32,1,3,2048]{3,0,2,1:T(8,128)(2,1)} %param.6) | copy-start | bytes 1179652
  5.8 8.2 %collective-permute-start.1 = (bf16[3,16,2176]{2,1,0:T(8,128)(2,1)S(1)}, bf16[3,16,2176]{2,1,0:T(8,128)(2,1)S(1)}, u32[]{:S(2)}, u32[]{:S(2)}) collective-permute-start(bf16[3,16,2176]{2,1,0:T(8,128)(2,1)S(1)} %get-tuple-element.13), channel_id=1, source_target_pairs={{0,8},{1,9},{2,10},{3,11},{4,12},{5,13},{6,14},{7,15},{8,0},{9,1},... | collective-permute-start | bytes 626696 | tf_op jit(solution)/shard_map/ppermute | solution.py:384
  6.0 2.9 %collective-permute-start.3 = (bf16[144,128]{1,0:T(8,128)(2,1)S(1)}, bf16[144,128]{1,0:T(8,128)(2,1)S(1)}, u32[]{:S(2)}, u32[]{:S(2)}) collective-permute-start(bf16[144,128]{1,0:T(8,128)(2,1)S(1)} %pad_maximum_fusion), channel_id=1, source_target_pairs={{0,1},{1,0},{2,3},{3,2},{4,5},{5,4},{6,7},{7,6},{8,9},{9,8},{10,11... | collective-permute-start | bytes 110600 | tf_op jit(solution)/shard_map/ppermute | solution.py:384
  8.9 5.2 %collective-permute-start.4 = (bf16[288,128]{1,0:T(8,128)(2,1)S(1)}, bf16[288,128]{1,0:T(8,128)(2,1)S(1)}, u32[]{:S(2)}, u32[]{:S(2)}) collective-permute-start(bf16[288,128]{1,0:T(8,128)(2,1)S(1)} %constant_dynamic-update-slice_fusion.near), channel_id=1, source_target_pairs={{0,2},{1,3},{2,0},{3,1},{4,6},{5,7},{6,4},{7,5},{8,10},{9,11},{10,... | collective-permute-start | bytes 221192 | tf_op jit(solution)/shard_map/ppermute | solution.py:384
  11.4 6.1 %collective-permute-start = (bf16[3,16,2176]{2,1,0:T(8,128)(2,1)S(1)}, bf16[3,16,2176]{2,1,0:T(8,128)(2,1)S(1)}, u32[]{:S(2)}, u32[]{:S(2)}) collective-permute-start(bf16[3,16,2176]{2,1,0:T(8,128)(2,1)S(1)} %get-tuple-element.12.t0), channel_id=1, source_target_pairs={{0,4},{1,5},{2,6},{3,7},{4,0},{5,1},{6,2},{7,3},{8,12},{9,13},{10,... | collective-permute-start | bytes 626696 | tf_op jit(solution)/shard_map/ppermute | solution.py:384
  14.1 4.7 %collective-permute-start.5 = (bf16[3,16,2176]{2,1,0:T(8,128)(2,1)S(1)}, bf16[3,16,2176]{2,1,0:T(8,128)(2,1)S(1)}, u32[]{:S(2)}, u32[]{:S(2)}) collective-permute-start(bf16[3,16,2176]{2,1,0:T(8,128)(2,1)S(1)} %collective-permute-done.1.told.t2), channel_id=1, source_target_pairs={{0,4},{1,5},{2,6},{3,7},{4,0},{5,1},{6,2},{7,3},{8,12},{9,13},{10,... | collective-permute-start | bytes 626696 | tf_op jit(solution)/shard_map/ppermute | solution.py:384
  17.4 1.4 %copy-start.1 = (s32[128,4]{0,1:T(4,128)S(1)}, s32[128,4]{0,1:T(4,128)}, u32[]{:S(2)}) copy-start(s32[128,4]{0,1:T(4,128)} %param.7) | copy-start | bytes 6148
  17.4 1.4 %collective-permute-start.6 = (bf16[6,72,128]{2,1,0:T(8,128)(2,1)S(1)}, bf16[6,72,128]{2,1,0:T(8,128)(2,1)S(1)}, u32[]{:S(2)}, u32[]{:S(2)}) collective-permute-start(bf16[6,72,128]{2,1,0:T(8,128)(2,1)S(1)} %get-tuple-element.16), channel_id=1, source_target_pairs={{0,4},{1,5},{2,6},{3,7},{4,0},{5,1},{6,2},{7,3},{8,12},{9,13},{10,... | collective-permute-start | bytes 331784 | tf_op jit(solution)/shard_map/ppermute | solution.py:384
  27.5 7.0 %collective-permute-start.7 = (s16[16,3200]{1,0:T(8,128)(2,1)S(1)}, s16[16,3200]{1,0:T(8,128)(2,1)S(1)}, u32[]{:S(2)}, u32[]{:S(2)}) collective-permute-start(s16[16,3200]{1,0:T(8,128)(2,1)S(1)} %get-tuple-element.17), channel_id=1, source_target_pairs={{0,0},{1,4},{2,8},{3,12},{4,2},{5,6},{6,10},{7,14},{8,1},{9,5},{10... | collective-permute-start | bytes 307208 | tf_op jit(solution)/shard_map/ppermute | solution.py:389
  32.2 6.1 %collective-permute-start.8 = (s16[16,3200]{1,0:T(8,128)(2,1)S(1)}, s16[16,3200]{1,0:T(8,128)(2,1)S(1)}, u32[]{:S(2)}, u32[]{:S(2)}) collective-permute-start(s16[16,3200]{1,0:T(8,128)(2,1)S(1)} %get-tuple-element.18), channel_id=1, source_target_pairs={{0,1},{1,5},{2,9},{3,13},{4,3},{5,7},{6,11},{7,15},{8,0},{9,4},{10... | collective-permute-start | bytes 307208 | tf_op jit(solution)/shard_map/ppermute | solution.py:389

commit v6 on v5

--- a/solution.py
+++ b/solution.py
@@ -109,7 +109,16 @@
     return lax.broadcasted_iota(jnp.int32, shape, len(shape) - 1)
 
 
-def split_kernel(offset, active, t_ref, keep_ref, send_ref):
+def split_kernel(offset_in, active_in, t_in, keep_ref, send_ref, offset, active, t_ref, sems):
+    copies = [
+        pltpu.make_async_copy(t_in, t_ref, sems.at[0]),
+        pltpu.make_async_copy(offset_in, offset, sems.at[1]),
+        pltpu.make_async_copy(active_in, active, sems.at[2]),
+    ]
+    for copy in copies:
+        copy.start()
+    for copy in copies:
+        copy.wait()
     half = lax.axis_index("loop") // 2
     span = t_ref.shape[2]
     sub = lax.broadcasted_iota(jnp.int32, (ROWS, 128), 0)
@@ -128,14 +137,20 @@
     return pl.pallas_call(
         split_kernel,
         out_shape=(half, half),
-        in_specs=[pl.BlockSpec(memory_space=pltpu.SMEM)] * 2 + [pl.BlockSpec(memory_space=pltpu.VMEM)],
+        in_specs=[pl.BlockSpec(memory_space=pltpu.HBM)] * 3,
         out_specs=(pl.BlockSpec(memory_space=pltpu.VMEM),) * 2,
+        scratch_shapes=[
+            pltpu.SMEM(offset.shape, jnp.int32),
+            pltpu.SMEM(active.shape, jnp.int32),
+            pltpu.VMEM(panel.shape, jnp.bfloat16),
+            pltpu.SemaphoreType.DMA((3,)),
+        ],
         compiler_params=pltpu.CompilerParams(vmem_limit_bytes=4 << 20),
         name="split",
     )(offset, active, panel)
 
 
-def series_kernel(blocks, offset, active, told, near, far, mine_ref, mate_ref, whole):
+def series_kernel(blocks, own, told, near, far, mine_ref, mate_ref, whole):
     z = lax.axis_index("tgrp")
     core = lax.axis_index("loop") % 2
     rows = mine_ref.shape[1]
@@ -149,19 +164,14 @@
             first = 6 * blocks * (b % 2) + i * blocks
             whole[i, pl.ds(at, blocks), :] = wide[b // 2][first : first + blocks]
     for station in range(2):
-        if station == 0:
-            shift = offset[0]
-        else:
-            words = told[0, :, span:].astype(jnp.float32)
-            shift = (32.0 * jnp.max(words[0:1]) + jnp.max(words[1:2])).astype(jnp.int32)
+        words = (own, told)[station]
+        first = words[0, :, span:].astype(jnp.float32)
+        shift = (32.0 * jnp.max(first[0:1]) + jnp.max(first[1:2])).astype(jnp.int32)
         row, turn = shift // 128, shift % 128
         spill = lane >= 128 - turn
         for c in range(3):
             i = 3 * station + c
-            if station == 0:
-                on = active[0, c].astype(jnp.float32)
-            else:
-                on = told[c, :, span:].astype(jnp.float32)[2:3]
+            on = words[c, :, span:].astype(jnp.float32)[2:3]
             for out, half in ((mine_ref, core), (mate_ref, 1 - core)):
                 at = row + 2 * blocks * half
                 here = pltpu.roll(whole[i, pl.ds(at, rows), :], 128 - turn, 1)
@@ -169,18 +179,18 @@
                 out[i] = (jnp.where(spill, after, here) * on).astype(jnp.bfloat16)
 
 
-def make_series(offset, active, told, near, far, blocks, rows):
+def make_series(own, told, near, far, blocks, rows):
     window = jax.ShapeDtypeStruct((6, rows, 128), jnp.bfloat16)
     vmem = pl.BlockSpec(memory_space=pltpu.VMEM)
     return pl.pallas_call(
         functools.partial(series_kernel, blocks),
         out_shape=(window, window),
-        in_specs=[pl.BlockSpec(memory_space=pltpu.SMEM)] * 2 + [vmem] * 3,
+        in_specs=[vmem] * 4,
         out_specs=(vmem, vmem),
         scratch_shapes=[pltpu.VMEM((6, 2 * blocks + rows + 8, 128), jnp.float32)],
         compiler_params=pltpu.CompilerParams(vmem_limit_bytes=4 << 20),
         name="series",
-    )(offset, active, told, near, far)
+    )(own, told, near, far)
 
 
 def correlate_kernel(span, nb, t0, t1, t2, t3, mine, mate, masks, first_ref, second_ref,
@@ -393,14 +403,16 @@
     span = templates.shape[3]
     nb = data.shape[2] // 128
     panel = templates[:, 0].transpose(1, 0, 2)
-    keep, send = split(offsets, active, panel)
-    panel_y = swapped(send, 2, 0)
-    panel_c = swapped(keep, 1, 0)
     pieces = data.reshape(3 * nb, 128)
     pair = jnp.concatenate([pieces, swapped(pieces, 2, 0)], axis=0)
+    panel, _ = lax.optimization_barrier((panel, pair))
+    keep, send = split(offsets, active, panel)
+    panel_c = swapped(keep, 1, 0)
     near = jnp.concatenate([pair, swapped(pair, 0, 1)], axis=0)
     far = swapped(near, 0, 2)
-    mine, mate = make_series(offsets, active, panel_y, near, far, nb, 2 * nb + span // 128 + 8)
+    send, _ = lax.optimization_barrier((send, near))
+    panel_y = swapped(send, 2, 0)
+    mine, mate = make_series(keep, panel_y, near, far, nb, 2 * nb + span // 128 + 8)
     mate = swapped(mate, 1, 0)
     panel_late, _ = lax.optimization_barrier((panel_y, far))
     panel_yc = swapped(panel_late, 1, 0)

time: 40.1 us -> 39.6 us (0.988); the launches traced: 39.3 us -> 39.4 us
  starting transfers between devices: 18.2 us -> 19 us
  waiting for transfers between devices: 6.64 us -> 6.13 us
    ppermute x7, starting transfers between devices: 11.4 us -> 13.5 us  [swapped(): return lax.ppermute(value, ('loop', 'tgrp'), pairs)]
    ppermute x2, starting transfers between devices: 6.8 us -> 5.45 us  [to_owner(): return lax.ppermute(value, ('loop', 'tgrp'), pairs)]
    pallas_call x1, Pallas kernels: 1 us -> 0.57 us  [make_series(): pl.pallas_call(functools.partial(series_kernel, blocks), out_shape=(windo...]
where the time goes in v6:
time: 39.6 us; the launch traced here: 39.4 us
  starting transfers between devices  19 us (48%)
  Pallas kernels  11.1 us (28%)
  waiting for transfers between devices  6.13 us (15%)
  local copies, waits for them, and re-layouts  2.44 us (6%)
  between operations  0.74 us (2%)
    ppermute x7, starting transfers between devices, swapped(): return lax.ppermute(value, ('loop', 'tgrp'), pairs)  13.5 us
    pallas_call x1, Pallas kernels, correlate_stations(): pl.pallas_call(functools.partial(correlate_kernel, span, nb), out_shape=(...  8.73 us
    ppermute x2, starting transfers between devices, to_owner(): return lax.ppermute(value, ('loop', 'tgrp'), pairs)  5.45 us
    ppermute x2, waiting for transfers between devices, to_owner(): return lax.ppermute(value, ('loop', 'tgrp'), pairs)  3.68 us
    ppermute x7, waiting for transfers between devices, swapped(): return lax.ppermute(value, ('loop', 'tgrp'), pairs)  2.45 us
    unnamed x8, local copies, waits for them, and re-layouts  1.67 us
    pallas_call x1, Pallas kernels, decode(): pl.pallas_call(decode_kernel, out_shape=jax.ShapeDtypeStruct((2 * ROWS, f...  0.98 us
    pallas_call x1, Pallas kernels, split(): pl.pallas_call(split_kernel, out_shape=(half, half), in_specs=[pl.BlockSp...  0.84 us
  transfers between devices with their start and end apart: 9, of which 4 were waited for; matrix products, arithmetic and copies ran while one was open for 0% of the time, Pallas kernels for 4%

profile of v6, /device:TPU:1, one launch (start us, length us, event | category | flops | bytes accessed | tf_op | source)
XLA Modules:
  0.0 39.4 jit_solution(17142035778000612190)
XLA Ops:
  0.0 0.8 %reshape.3 = bf16[72,128]{1,0:T(8,128)(2,1)S(1)} reshape(bf16[1,3,3072]{2,1,0:T(4,128)(2,1)} %param.5) | data formatting | bytes 36864 | tf_op jit(solution)/shard_map/reshape | solution.py:406
  0.8 2.1 %collective-permute-start = (bf16[72,128]{1,0:T(8,128)(2,1)S(1)}, bf16[72,128]{1,0:T(8,128)(2,1)S(1)}, u32[]{:S(2)}, u32[]{:S(2)}) collective-permute-start(bf16[72,128]{1,0:T(8,128)(2,1)S(1)} %reshape.3), channel_id=1, source_target_pairs={{0,8},{1,9},{2,10},{3,11},{4,12},{5,13},{6,14},{7,15},{8,0},{9,1},... | collective-permute-start | bytes 55304 | tf_op jit(solution)/shard_map/ppermute | solution.py:394
  2.9 1.1 %collective-permute-done = bf16[72,128]{1,0:T(8,128)(2,1)S(1)} collective-permute-done((bf16[72,128]{1,0:T(8,128)(2,1)S(1)}, bf16[72,128]{1,0:T(8,128)(2,1)S(1)}, u32[]{:S(2)}, u32[]{:S(2)}) %collective-permute-start) | collective-permute-done | bytes 18464 | tf_op jit(solution)/shard_map/ppermute | solution.py:394
  4.1 1.6 %collective-permute-start.2 = (bf16[144,128]{1,0:T(8,128)(2,1)S(1)}, bf16[144,128]{1,0:T(8,128)(2,1)S(1)}, u32[]{:S(2)}, u32[]{:S(2)}) collective-permute-start(bf16[144,128]{1,0:T(8,128)(2,1)S(1)} %get-tuple-element.24), channel_id=1, source_target_pairs={{0,1},{1,0},{2,3},{3,2},{4,5},{5,4},{6,7},{7,6},{8,9},{9,8},{10,11... | collective-permute-start | bytes 110600 | tf_op jit(solution)/shard_map/ppermute | solution.py:394
  6.3 0.0 copy-start.2
  6.3 0.6 %copy-done.2 = s32[1,3]{1,0:T(1,128)S(1)} copy-done((s32[1,3]{1,0:T(1,128)S(1)}, s32[1,3]{1,0:T(1,128)}, u32[]{:S(2)}) %copy-start.2) | copy-done | bytes 36
  7.0 1.0 %copy-done = bf16[32,1,3,2048]{3,0,2,1:T(8,128)(2,1)S(1)} copy-done((bf16[32,1,3,2048]{3,0,2,1:T(8,128)(2,1)S(1)}, bf16[32,1,3,2048]{3,0,2,1:T(8,128)(2,1)}, u32[]{:S(2)}) %copy-start) | copy-done | bytes 393240
  7.9 0.8 %split.1 = (bf16[3,16,2176]{2,1,0:T(8,128)(2,1)S(1)}, bf16[3,16,2176]{2,1,0:T(8,128)(2,1)S(1)}) custom-call(s32[1]{0:T(128)S(6)} %copy.9.offset_in, s32[1,3]{1,0:T(1,128)S(1)} %copy-done.2, bf16[3,32,2048]{2,1,0:T(8,128)(2,1)S(1)} %bitcast.4), custom_call_target="tpu_custom_call" | custom-call | tf_op jit(solution)/shard_map/split/pallas_call | solution.py:137
  8.8 0.0 collective-permute-done.2
  8.8 1.3 %collective-permute-start.3 = (bf16[3,16,2176]{2,1,0:T(8,128)(2,1)S(1)}, bf16[3,16,2176]{2,1,0:T(8,128)(2,1)S(1)}, u32[]{:S(2)}, u32[]{:S(2)}) collective-permute-start(bf16[3,16,2176]{2,1,0:T(8,128)(2,1)S(1)} %get-tuple-element.17), channel_id=1, source_target_pairs={{0,8},{1,9},{2,10},{3,11},{4,12},{5,13},{6,14},{7,15},{8,0},{9,1},... | collective-permute-start | bytes 626696 | tf_op jit(solution)/shard_map/ppermute | solution.py:394
  10.1 2.3 %collective-permute-start.4 = (bf16[288,128]{1,0:T(8,128)(2,1)S(1)}, bf16[288,128]{1,0:T(8,128)(2,1)S(1)}, u32[]{:S(2)}, u32[]{:S(2)}) collective-permute-start(bf16[288,128]{1,0:T(8,128)(2,1)S(1)} %constant_dynamic-update-slice_fusion.2.near), channel_id=1, source_target_pairs={{0,2},{1,3},{2,0},{3,1},{4,6},{5,7},{6,4},{7,5},{8,10},{9,11},{10,... | collective-permute-start | bytes 221192 | tf_op jit(solution)/shard_map/ppermute | solution.py:394
  12.4 2.7 %collective-permute-start.1 = (bf16[3,16,2176]{2,1,0:T(8,128)(2,1)S(1)}, bf16[3,16,2176]{2,1,0:T(8,128)(2,1)S(1)}, u32[]{:S(2)}, u32[]{:S(2)}) collective-permute-start(bf16[3,16,2176]{2,1,0:T(8,128)(2,1)S(1)} %get-tuple-element.15.own.t0), channel_id=1, source_target_pairs={{0,4},{1,5},{2,6},{3,7},{4,0},{5,1},{6,2},{7,3},{8,12},{9,13},{10,... | collective-permute-start | bytes 626696 | tf_op jit(solution)/shard_map/ppermute | solution.py:394
  15.1 3.5 %collective-permute-start.5 = (bf16[3,16,2176]{2,1,0:T(8,128)(2,1)S(1)}, bf16[3,16,2176]{2,1,0:T(8,128)(2,1)S(1)}, u32[]{:S(2)}, u32[]{:S(2)}) collective-permute-start(bf16[3,16,2176]{2,1,0:T(8,128)(2,1)S(1)} %collective-permute-done.3.told.t2), channel_id=1, source_target_pairs={{0,4},{1,5},{2,6},{3,7},{4,0},{5,1},{6,2},{7,3},{8,12},{9,13},{10,... | collective-permute-start | bytes 626696 | tf_op jit(solution)/shard_map/ppermute | solution.py:394
  18.6 0.6 %series.1 = (bf16[6,72,128]{2,1,0:T(8,128)(2,1)S(1)}, bf16[6,72,128]{2,1,0:T(8,128)(2,1)S(1)}) custom-call(bf16[3,16,2176]{2,1,0:T(8,128)(2,1)S(1)} %get-tuple-element.15.own.t0, bf16[3,16,2176]{2,1,0:T(8,128)(2,1)S(1)} %collective-permute-done.3.told.t2, bf16[288,128]{1,0:T(8,128)(2,1)S(1)} %constant_dynamic-update-slice_fusion.2.near, ...), custom_call_target="tpu_custom_call" | custom-call | tf_op jit(solution)/shard_map/series/pallas_call | solution.py:185
  19.1 0.0 copy-start.1
  19.2 0.1 collective-permute-start.6
  19.2 0.0 collective-permute-done.1.t1
  19.2 1.3 %collective-permute-done.6.mate = bf16[6,72,128]{2,1,0:T(8,128)(2,1)S(1)} collective-permute-done((bf16[6,72,128]{2,1,0:T(8,128)(2,1)S(1)}, bf16[6,72,128]{2,1,0:T(8,128)(2,1)S(1)}, u32[]{:S(2)}, u32[]{:S(2)}) %collective-permute-start.6) | collective-permute-done | bytes 110624 | tf_op jit(solution)/shard_map/ppermute | solution.py:394
  20.5 8.7 %correlate.1 = (s16[16,3200]{1,0:T(8,128)(2,1)S(1)}, s16[16,3200]{1,0:T(8,128)(2,1)S(1)}) custom-call(bf16[3,16,2176]{2,1,0:T(8,128)(2,1)S(1)} %get-tuple-element.15.own.t0, bf16[3,16,2176]{2,1,0:T(8,128)(2,1)S(1)} %collective-permute-done.1.t1, bf16[3,16,2176]{2,1,0:T(8,128)(2,1)S(1)} %collective-permute-done.3.told.t2, ...), custom_call_target="tpu_custom_call" | custom-call | tf_op jit(solution)/shard_map/correlate/pallas_call | solution.py:370
  29.3 3.6 %collective-permute-start.7 = (s16[16,3200]{1,0:T(8,128)(2,1)S(1)}, s16[16,3200]{1,0:T(8,128)(2,1)S(1)}, u32[]{:S(2)}, u32[]{:S(2)}) collective-permute-start(s16[16,3200]{1,0:T(8,128)(2,1)S(1)} %get-tuple-element.21), channel_id=1, source_target_pairs={{0,0},{1,4},{2,8},{3,12},{4,2},{5,6},{6,10},{7,14},{8,1},{9,5},{10... | collective-permute-start | bytes 307208 | tf_op jit(solution)/shard_map/ppermute | solution.py:399
  32.9 1.9 %collective-permute-start.8 = (s16[16,3200]{1,0:T(8,128)(2,1)S(1)}, s16[16,3200]{1,0:T(8,128)(2,1)S(1)}, u32[]{:S(2)}, u32[]{:S(2)}) collective-permute-start(s16[16,3200]{1,0:T(8,128)(2,1)S(1)} %get-tuple-element.22), channel_id=1, source_target_pairs={{0,1},{1,5},{2,9},{3,13},{4,3},{5,7},{6,11},{7,15},{8,0},{9,4},{10... | collective-permute-start | bytes 307208 | tf_op jit(solution)/shard_map/ppermute | solution.py:399
  34.7 2.7 %collective-permute-done.7.a_ref = s16[16,3200]{1,0:T(8,128)(2,1)S(1)} collective-permute-done((s16[16,3200]{1,0:T(8,128)(2,1)S(1)}, s16[16,3200]{1,0:T(8,128)(2,1)S(1)}, u32[]{:S(2)}, u32[]{:S(2)}) %collective-permute-start.7) | collective-permute-done | bytes 102432 | tf_op jit(solution)/shard_map/ppermute | solution.py:399
  37.5 1.0 %collective-permute-done.8.b_ref = s16[16,3200]{1,0:T(8,128)(2,1)S(1)} collective-permute-done((s16[16,3200]{1,0:T(8,128)(2,1)S(1)}, s16[16,3200]{1,0:T(8,128)(2,1)S(1)}, u32[]{:S(2)}, u32[]{:S(2)}) %collective-permute-start.8) | collective-permute-done | bytes 102432 | tf_op jit(solution)/shard_map/ppermute | solution.py:399
  38.4 1.0 %decode.1 = f32[32,3072]{1,0:T(8,128)} custom-call(s16[16,3200]{1,0:T(8,128)(2,1)S(1)} %collective-permute-done.7.a_ref, s16[16,3200]{1,0:T(8,128)(2,1)S(1)} %collective-permute-done.8.b_ref), custom_call_target="tpu_custom_call" | custom-call | tf_op jit(solution)/shard_map/decode/pallas_call | solution.py:355
  (8 shorter events, 0.0 us)
Async XLA Ops:
  0.8 3.3 %collective-permute-start = (bf16[72,128]{1,0:T(8,128)(2,1)S(1)}, bf16[72,128]{1,0:T(8,128)(2,1)S(1)}, u32[]{:S(2)}, u32[]{:S(2)}) collective-permute-start(bf16[72,128]{1,0:T(8,128)(2,1)S(1)} %reshape.3), channel_id=1, source_target_pairs={{0,8},{1,9},{2,10},{3,11},{4,12},{5,13},{6,14},{7,15},{8,0},{9,1},... | collective-permute-start | bytes 55304 | tf_op jit(solution)/shard_map/ppermute | solution.py:394
  4.1 4.7 %collective-permute-start.2 = (bf16[144,128]{1,0:T(8,128)(2,1)S(1)}, bf16[144,128]{1,0:T(8,128)(2,1)S(1)}, u32[]{:S(2)}, u32[]{:S(2)}) collective-permute-start(bf16[144,128]{1,0:T(8,128)(2,1)S(1)} %get-tuple-element.24), channel_id=1, source_target_pairs={{0,1},{1,0},{2,3},{3,2},{4,5},{5,4},{6,7},{7,6},{8,9},{9,8},{10,11... | collective-permute-start | bytes 110600 | tf_op jit(solution)/shard_map/ppermute | solution.py:394
  6.3 0.7 %copy-start.2 = (s32[1,3]{1,0:T(1,128)S(1)}, s32[1,3]{1,0:T(1,128)}, u32[]{:S(2)}) copy-start(s32[1,3]{1,0:T(1,128)} %active_in.1) | copy-start | bytes 40
  7.0 1.0 %copy-start = (bf16[32,1,3,2048]{3,0,2,1:T(8,128)(2,1)S(1)}, bf16[32,1,3,2048]{3,0,2,1:T(8,128)(2,1)}, u32[]{:S(2)}) copy-start(bf16[32,1,3,2048]{3,0,2,1:T(8,128)(2,1)} %param.6) | copy-start | bytes 1179652
  8.8 6.3 %collective-permute-start.3 = (bf16[3,16,2176]{2,1,0:T(8,128)(2,1)S(1)}, bf16[3,16,2176]{2,1,0:T(8,128)(2,1)S(1)}, u32[]{:S(2)}, u32[]{:S(2)}) collective-permute-start(bf16[3,16,2176]{2,1,0:T(8,128)(2,1)S(1)} %get-tuple-element.17), channel_id=1, source_target_pairs={{0,8},{1,9},{2,10},{3,11},{4,12},{5,13},{6,14},{7,15},{8,0},{9,1},... | collective-permute-start | bytes 626696 | tf_op jit(solution)/shard_map/ppermute | solution.py:394
  10.1 5.0 %collective-permute-start.4 = (bf16[288,128]{1,0:T(8,128)(2,1)S(1)}, bf16[288,128]{1,0:T(8,128)(2,1)S(1)}, u32[]{:S(2)}, u32[]{:S(2)}) collective-permute-start(bf16[288,128]{1,0:T(8,128)(2,1)S(1)} %constant_dynamic-update-slice_fusion.2.near), channel_id=1, source_target_pairs={{0,2},{1,3},{2,0},{3,1},{4,6},{5,7},{6,4},{7,5},{8,10},{9,11},{10,... | collective-permute-start | bytes 221192 | tf_op jit(solution)/shard_map/ppermute | solution.py:394
  12.4 6.8 %collective-permute-start.1 = (bf16[3,16,2176]{2,1,0:T(8,128)(2,1)S(1)}, bf16[3,16,2176]{2,1,0:T(8,128)(2,1)S(1)}, u32[]{:S(2)}, u32[]{:S(2)}) collective-permute-start(bf16[3,16,2176]{2,1,0:T(8,128)(2,1)S(1)} %get-tuple-element.15.own.t0), channel_id=1, source_target_pairs={{0,4},{1,5},{2,6},{3,7},{4,0},{5,1},{6,2},{7,3},{8,12},{9,13},{10,... | collective-permute-start | bytes 626696 | tf_op jit(solution)/shard_map/ppermute | solution.py:394
  15.1 5.4 %collective-permute-start.5 = (bf16[3,16,2176]{2,1,0:T(8,128)(2,1)S(1)}, bf16[3,16,2176]{2,1,0:T(8,128)(2,1)S(1)}, u32[]{:S(2)}, u32[]{:S(2)}) collective-permute-start(bf16[3,16,2176]{2,1,0:T(8,128)(2,1)S(1)} %collective-permute-done.3.told.t2), channel_id=1, source_target_pairs={{0,4},{1,5},{2,6},{3,7},{4,0},{5,1},{6,2},{7,3},{8,12},{9,13},{10,... | collective-permute-start | bytes 626696 | tf_op jit(solution)/shard_map/ppermute | solution.py:394
  19.1 1.4 %copy-start.1 = (s32[128,4]{0,1:T(4,128)S(1)}, s32[128,4]{0,1:T(4,128)}, u32[]{:S(2)}) copy-start(s32[128,4]{0,1:T(4,128)} %param.7) | copy-start | bytes 6148
  19.2 1.4 %collective-permute-start.6 = (bf16[6,72,128]{2,1,0:T(8,128)(2,1)S(1)}, bf16[6,72,128]{2,1,0:T(8,128)(2,1)S(1)}, u32[]{:S(2)}, u32[]{:S(2)}) collective-permute-start(bf16[6,72,128]{2,1,0:T(8,128)(2,1)S(1)} %get-tuple-element.20), channel_id=1, source_target_pairs={{0,4},{1,5},{2,6},{3,7},{4,0},{5,1},{6,2},{7,3},{8,12},{9,13},{10,... | collective-permute-start | bytes 331784 | tf_op jit(solution)/shard_map/ppermute | solution.py:394
  29.3 8.2 %collective-permute-start.7 = (s16[16,3200]{1,0:T(8,128)(2,1)S(1)}, s16[16,3200]{1,0:T(8,128)(2,1)S(1)}, u32[]{:S(2)}, u32[]{:S(2)}) collective-permute-start(s16[16,3200]{1,0:T(8,128)(2,1)S(1)} %get-tuple-element.21), channel_id=1, source_target_pairs={{0,0},{1,4},{2,8},{3,12},{4,2},{5,6},{6,10},{7,14},{8,1},{9,5},{10... | collective-permute-start | bytes 307208 | tf_op jit(solution)/shard_map/ppermute | solution.py:399
  32.9 5.6 %collective-permute-start.8 = (s16[16,3200]{1,0:T(8,128)(2,1)S(1)}, s16[16,3200]{1,0:T(8,128)(2,1)S(1)}, u32[]{:S(2)}, u32[]{:S(2)}) collective-permute-start(s16[16,3200]{1,0:T(8,128)(2,1)S(1)} %get-tuple-element.22), channel_id=1, source_target_pairs={{0,1},{1,5},{2,9},{3,13},{4,3},{5,7},{6,11},{7,15},{8,0},{9,4},{10... | collective-permute-start | bytes 307208 | tf_op jit(solution)/shard_map/ppermute | solution.py:399

commit v7 on v6

--- a/solution.py
+++ b/solution.py
@@ -403,11 +403,10 @@
     span = templates.shape[3]
     nb = data.shape[2] // 128
     panel = templates[:, 0].transpose(1, 0, 2)
+    keep, send = split(offsets, active, panel)
+    panel_c = swapped(keep, 1, 0)
     pieces = data.reshape(3 * nb, 128)
     pair = jnp.concatenate([pieces, swapped(pieces, 2, 0)], axis=0)
-    panel, _ = lax.optimization_barrier((panel, pair))
-    keep, send = split(offsets, active, panel)
-    panel_c = swapped(keep, 1, 0)
     near = jnp.concatenate([pair, swapped(pair, 0, 1)], axis=0)
     far = swapped(near, 0, 2)
     send, _ = lax.optimization_barrier((send, near))

time: 39.6 us -> 39.8 us (level); the launches traced: 39.4 us -> 39.1 us
  starting transfers between devices: 19 us -> 18 us
  waiting for transfers between devices: 6.13 us -> 6.82 us
    ppermute x7, starting transfers between devices: 13.5 us -> 11.5 us  [swapped(): return lax.ppermute(value, ('loop', 'tgrp'), pairs)]
    ppermute x2, starting transfers between devices: 5.45 us -> 6.43 us  [to_owner(): return lax.ppermute(value, ('loop', 'tgrp'), pairs)]
where the time goes in v7:
time: 39.8 us; the launch traced here: 39.1 us
  starting transfers between devices  18 us (45%)
  Pallas kernels  11.1 us (28%)
  waiting for transfers between devices  6.82 us (17%)
  local copies, waits for them, and re-layouts  2.43 us (6%)
  between operations  0.74 us (2%)
    ppermute x7, starting transfers between devices, swapped(): return lax.ppermute(value, ('loop', 'tgrp'), pairs)  11.5 us
    pallas_call x1, Pallas kernels, correlate_stations(): pl.pallas_call(functools.partial(correlate_kernel, span, nb), out_shape=(...  8.73 us
    ppermute x2, starting transfers between devices, to_owner(): return lax.ppermute(value, ('loop', 'tgrp'), pairs)  6.43 us
    ppermute x2, waiting for transfers between devices, to_owner(): return lax.ppermute(value, ('loop', 'tgrp'), pairs)  4 us
    ppermute x7, waiting for transfers between devices, swapped(): return lax.ppermute(value, ('loop', 'tgrp'), pairs)  2.81 us
    unnamed x8, local copies, waits for them, and re-layouts  1.66 us
    pallas_call x1, Pallas kernels, decode(): pl.pallas_call(decode_kernel, out_shape=jax.ShapeDtypeStruct((2 * ROWS, f...  0.98 us
    pallas_call x1, Pallas kernels, split(): pl.pallas_call(split_kernel, out_shape=(half, half), in_specs=[pl.BlockSp...  0.84 us
  transfers between devices with their start and end apart: 9, of which 4 were waited for; matrix products, arithmetic and copies ran while one was open for 0% of the time, Pallas kernels for 4%

profile of v7, /device:TPU:1, one launch (start us, length us, event | category | flops | bytes accessed | tf_op | source)
XLA Modules:
  0.0 39.1 jit_solution(527155785549298232)
XLA Ops:
  0.0 0.8 %reshape.3 = bf16[72,128]{1,0:T(8,128)(2,1)S(1)} reshape(bf16[1,3,3072]{2,1,0:T(4,128)(2,1)} %param.5) | data formatting | bytes 36864 | tf_op jit(solution)/shard_map/reshape | solution.py:408
  0.8 2.1 %collective-permute-start.1 = (bf16[72,128]{1,0:T(8,128)(2,1)S(1)}, bf16[72,128]{1,0:T(8,128)(2,1)S(1)}, u32[]{:S(2)}, u32[]{:S(2)}) collective-permute-start(bf16[72,128]{1,0:T(8,128)(2,1)S(1)} %reshape.3), channel_id=1, source_target_pairs={{0,8},{1,9},{2,10},{3,11},{4,12},{5,13},{6,14},{7,15},{8,0},{9,1},... | collective-permute-start | bytes 55304 | tf_op jit(solution)/shard_map/ppermute | solution.py:394
  3.6 0.0 copy-start.2
  3.6 0.6 %copy-done.2 = s32[1,3]{1,0:T(1,128)S(1)} copy-done((s32[1,3]{1,0:T(1,128)S(1)}, s32[1,3]{1,0:T(1,128)}, u32[]{:S(2)}) %copy-start.2) | copy-done | bytes 36
  4.2 1.0 %copy-done = bf16[32,1,3,2048]{3,0,2,1:T(8,128)(2,1)S(1)} copy-done((bf16[32,1,3,2048]{3,0,2,1:T(8,128)(2,1)S(1)}, bf16[32,1,3,2048]{3,0,2,1:T(8,128)(2,1)}, u32[]{:S(2)}) %copy-start) | copy-done | bytes 393240
  5.2 0.8 %split.1 = (bf16[3,16,2176]{2,1,0:T(8,128)(2,1)S(1)}, bf16[3,16,2176]{2,1,0:T(8,128)(2,1)S(1)}) custom-call(s32[1]{0:T(128)S(6)} %copy.8.offset_in, s32[1,3]{1,0:T(1,128)S(1)} %copy-done.2, bf16[3,32,2048]{2,1,0:T(8,128)(2,1)S(1)} %bitcast.4), custom_call_target="tpu_custom_call" | custom-call | tf_op jit(solution)/shard_map/split/pallas_call | solution.py:137
  6.1 0.0 collective-permute-done.1
  6.1 1.4 %collective-permute-start.2 = (bf16[144,128]{1,0:T(8,128)(2,1)S(1)}, bf16[144,128]{1,0:T(8,128)(2,1)S(1)}, u32[]{:S(2)}, u32[]{:S(2)}) collective-permute-start(bf16[144,128]{1,0:T(8,128)(2,1)S(1)} %pad_maximum_fusion), channel_id=1, source_target_pairs={{0,1},{1,0},{2,3},{3,2},{4,5},{5,4},{6,7},{7,6},{8,9},{9,8},{10,11... | collective-permute-start | bytes 110600 | tf_op jit(solution)/shard_map/ppermute | solution.py:394
  7.5 1.5 %collective-permute-done.2 = bf16[144,128]{1,0:T(8,128)(2,1)S(1)} collective-permute-done((bf16[144,128]{1,0:T(8,128)(2,1)S(1)}, bf16[144,128]{1,0:T(8,128)(2,1)S(1)}, u32[]{:S(2)}, u32[]{:S(2)}) %collective-permute-start.2) | collective-permute-done | bytes 36896 | tf_op jit(solution)/shard_map/ppermute | solution.py:394
  9.0 0.1 collective-permute-start.3
  9.1 2.5 %collective-permute-start.4 = (bf16[288,128]{1,0:T(8,128)(2,1)S(1)}, bf16[288,128]{1,0:T(8,128)(2,1)S(1)}, u32[]{:S(2)}, u32[]{:S(2)}) collective-permute-start(bf16[288,128]{1,0:T(8,128)(2,1)S(1)} %constant_dynamic-update-slice_fusion.near), channel_id=1, source_target_pairs={{0,2},{1,3},{2,0},{3,1},{4,6},{5,7},{6,4},{7,5},{8,10},{9,11},{10,... | collective-permute-start | bytes 221192 | tf_op jit(solution)/shard_map/ppermute | solution.py:394
  11.6 2.7 %collective-permute-start = (bf16[3,16,2176]{2,1,0:T(8,128)(2,1)S(1)}, bf16[3,16,2176]{2,1,0:T(8,128)(2,1)S(1)}, u32[]{:S(2)}, u32[]{:S(2)}) collective-permute-start(bf16[3,16,2176]{2,1,0:T(8,128)(2,1)S(1)} %get-tuple-element.13.own.t0), channel_id=1, source_target_pairs={{0,4},{1,5},{2,6},{3,7},{4,0},{5,1},{6,2},{7,3},{8,12},{9,13},{10,... | collective-permute-start | bytes 626696 | tf_op jit(solution)/shard_map/ppermute | solution.py:394
  14.2 0.0 collective-permute-done.4.far
  14.2 2.7 %collective-permute-start.5 = (bf16[3,16,2176]{2,1,0:T(8,128)(2,1)S(1)}, bf16[3,16,2176]{2,1,0:T(8,128)(2,1)S(1)}, u32[]{:S(2)}, u32[]{:S(2)}) collective-permute-start(bf16[3,16,2176]{2,1,0:T(8,128)(2,1)S(1)} %collective-permute-done.3.told.t2), channel_id=1, source_target_pairs={{0,4},{1,5},{2,6},{3,7},{4,0},{5,1},{6,2},{7,3},{8,12},{9,13},{10,... | collective-permute-start | bytes 626696 | tf_op jit(solution)/shard_map/ppermute | solution.py:394
  16.9 0.6 %series.1 = (bf16[6,72,128]{2,1,0:T(8,128)(2,1)S(1)}, bf16[6,72,128]{2,1,0:T(8,128)(2,1)S(1)}) custom-call(bf16[3,16,2176]{2,1,0:T(8,128)(2,1)S(1)} %get-tuple-element.13.own.t0, bf16[3,16,2176]{2,1,0:T(8,128)(2,1)S(1)} %collective-permute-done.3.told.t2, bf16[288,128]{1,0:T(8,128)(2,1)S(1)} %constant_dynamic-update-slice_fusion.near, ...), custom_call_target="tpu_custom_call" | custom-call | tf_op jit(solution)/shard_map/series/pallas_call | solution.py:185
  17.5 0.0 copy-start.1
  17.5 0.1 collective-permute-start.6
  17.6 1.3 %collective-permute-done.6.mate = bf16[6,72,128]{2,1,0:T(8,128)(2,1)S(1)} collective-permute-done((bf16[6,72,128]{2,1,0:T(8,128)(2,1)S(1)}, bf16[6,72,128]{2,1,0:T(8,128)(2,1)S(1)}, u32[]{:S(2)}, u32[]{:S(2)}) %collective-permute-start.6) | collective-permute-done | bytes 110624 | tf_op jit(solution)/shard_map/ppermute | solution.py:394
  18.9 8.7 %correlate.1 = (s16[16,3200]{1,0:T(8,128)(2,1)S(1)}, s16[16,3200]{1,0:T(8,128)(2,1)S(1)}) custom-call(bf16[3,16,2176]{2,1,0:T(8,128)(2,1)S(1)} %get-tuple-element.13.own.t0, bf16[3,16,2176]{2,1,0:T(8,128)(2,1)S(1)} %collective-permute-done.t1, bf16[3,16,2176]{2,1,0:T(8,128)(2,1)S(1)} %collective-permute-done.3.told.t2, ...), custom_call_target="tpu_custom_call" | custom-call | tf_op jit(solution)/shard_map/correlate/pallas_call | solution.py:370
  27.6 4.3 %collective-permute-start.7 = (s16[16,3200]{1,0:T(8,128)(2,1)S(1)}, s16[16,3200]{1,0:T(8,128)(2,1)S(1)}, u32[]{:S(2)}, u32[]{:S(2)}) collective-permute-start(s16[16,3200]{1,0:T(8,128)(2,1)S(1)} %get-tuple-element.19), channel_id=1, source_target_pairs={{0,0},{1,4},{2,8},{3,12},{4,2},{5,6},{6,10},{7,14},{8,1},{9,5},{10... | collective-permute-start | bytes 307208 | tf_op jit(solution)/shard_map/ppermute | solution.py:399
  32.0 2.1 %collective-permute-start.8 = (s16[16,3200]{1,0:T(8,128)(2,1)S(1)}, s16[16,3200]{1,0:T(8,128)(2,1)S(1)}, u32[]{:S(2)}, u32[]{:S(2)}) collective-permute-start(s16[16,3200]{1,0:T(8,128)(2,1)S(1)} %get-tuple-element.20), channel_id=1, source_target_pairs={{0,1},{1,5},{2,9},{3,13},{4,3},{5,7},{6,11},{7,15},{8,0},{9,4},{10... | collective-permute-start | bytes 307208 | tf_op jit(solution)/shard_map/ppermute | solution.py:399
  34.1 0.5 %collective-permute-done.7.a_ref = s16[16,3200]{1,0:T(8,128)(2,1)S(1)} collective-permute-done((s16[16,3200]{1,0:T(8,128)(2,1)S(1)}, s16[16,3200]{1,0:T(8,128)(2,1)S(1)}, u32[]{:S(2)}, u32[]{:S(2)}) %collective-permute-start.7) | collective-permute-done | bytes 102432 | tf_op jit(solution)/shard_map/ppermute | solution.py:399
  34.6 3.5 %collective-permute-done.8.b_ref = s16[16,3200]{1,0:T(8,128)(2,1)S(1)} collective-permute-done((s16[16,3200]{1,0:T(8,128)(2,1)S(1)}, s16[16,3200]{1,0:T(8,128)(2,1)S(1)}, u32[]{:S(2)}, u32[]{:S(2)}) %collective-permute-start.8) | collective-permute-done | bytes 102432 | tf_op jit(solution)/shard_map/ppermute | solution.py:399
  38.1 1.0 %decode.1 = f32[32,3072]{1,0:T(8,128)} custom-call(s16[16,3200]{1,0:T(8,128)(2,1)S(1)} %collective-permute-done.7.a_ref, s16[16,3200]{1,0:T(8,128)(2,1)S(1)} %collective-permute-done.8.b_ref), custom_call_target="tpu_custom_call" | custom-call | tf_op jit(solution)/shard_map/decode/pallas_call | solution.py:355
  (9 shorter events, 0.0 us)
Async XLA Ops:
  0.8 5.3 %collective-permute-start.1 = (bf16[72,128]{1,0:T(8,128)(2,1)S(1)}, bf16[72,128]{1,0:T(8,128)(2,1)S(1)}, u32[]{:S(2)}, u32[]{:S(2)}) collective-permute-start(bf16[72,128]{1,0:T(8,128)(2,1)S(1)} %reshape.3), channel_id=1, source_target_pairs={{0,8},{1,9},{2,10},{3,11},{4,12},{5,13},{6,14},{7,15},{8,0},{9,1},... | collective-permute-start | bytes 55304 | tf_op jit(solution)/shard_map/ppermute | solution.py:394
  3.6 0.7 %copy-start.2 = (s32[1,3]{1,0:T(1,128)S(1)}, s32[1,3]{1,0:T(1,128)}, u32[]{:S(2)}) copy-start(s32[1,3]{1,0:T(1,128)} %active_in.1) | copy-start | bytes 40
  4.2 1.0 %copy-start = (bf16[32,1,3,2048]{3,0,2,1:T(8,128)(2,1)S(1)}, bf16[32,1,3,2048]{3,0,2,1:T(8,128)(2,1)}, u32[]{:S(2)}) copy-start(bf16[32,1,3,2048]{3,0,2,1:T(8,128)(2,1)} %param.6) | copy-start | bytes 1179652
  6.1 2.9 %collective-permute-start.2 = (bf16[144,128]{1,0:T(8,128)(2,1)S(1)}, bf16[144,128]{1,0:T(8,128)(2,1)S(1)}, u32[]{:S(2)}, u32[]{:S(2)}) collective-permute-start(bf16[144,128]{1,0:T(8,128)(2,1)S(1)} %pad_maximum_fusion), channel_id=1, source_target_pairs={{0,1},{1,0},{2,3},{3,2},{4,5},{5,4},{6,7},{7,6},{8,9},{9,8},{10,11... | collective-permute-start | bytes 110600 | tf_op jit(solution)/shard_map/ppermute | solution.py:394
  9.0 5.3 %collective-permute-start.3 = (bf16[3,16,2176]{2,1,0:T(8,128)(2,1)S(1)}, bf16[3,16,2176]{2,1,0:T(8,128)(2,1)S(1)}, u32[]{:S(2)}, u32[]{:S(2)}) collective-permute-start(bf16[3,16,2176]{2,1,0:T(8,128)(2,1)S(1)} %get-tuple-element.15), channel_id=1, source_target_pairs={{0,8},{1,9},{2,10},{3,11},{4,12},{5,13},{6,14},{7,15},{8,0},{9,1},... | collective-permute-start | bytes 626696 | tf_op jit(solution)/shard_map/ppermute | solution.py:394
  9.1 5.2 %collective-permute-start.4 = (bf16[288,128]{1,0:T(8,128)(2,1)S(1)}, bf16[288,128]{1,0:T(8,128)(2,1)S(1)}, u32[]{:S(2)}, u32[]{:S(2)}) collective-permute-start(bf16[288,128]{1,0:T(8,128)(2,1)S(1)} %constant_dynamic-update-slice_fusion.near), channel_id=1, source_target_pairs={{0,2},{1,3},{2,0},{3,1},{4,6},{5,7},{6,4},{7,5},{8,10},{9,11},{10,... | collective-permute-start | bytes 221192 | tf_op jit(solution)/shard_map/ppermute | solution.py:394
  11.6 6.0 %collective-permute-start = (bf16[3,16,2176]{2,1,0:T(8,128)(2,1)S(1)}, bf16[3,16,2176]{2,1,0:T(8,128)(2,1)S(1)}, u32[]{:S(2)}, u32[]{:S(2)}) collective-permute-start(bf16[3,16,2176]{2,1,0:T(8,128)(2,1)S(1)} %get-tuple-element.13.own.t0), channel_id=1, source_target_pairs={{0,4},{1,5},{2,6},{3,7},{4,0},{5,1},{6,2},{7,3},{8,12},{9,13},{10,... | collective-permute-start | bytes 626696 | tf_op jit(solution)/shard_map/ppermute | solution.py:394
  14.2 4.7 %collective-permute-start.5 = (bf16[3,16,2176]{2,1,0:T(8,128)(2,1)S(1)}, bf16[3,16,2176]{2,1,0:T(8,128)(2,1)S(1)}, u32[]{:S(2)}, u32[]{:S(2)}) collective-permute-start(bf16[3,16,2176]{2,1,0:T(8,128)(2,1)S(1)} %collective-permute-done.3.told.t2), channel_id=1, source_target_pairs={{0,4},{1,5},{2,6},{3,7},{4,0},{5,1},{6,2},{7,3},{8,12},{9,13},{10,... | collective-permute-start | bytes 626696 | tf_op jit(solution)/shard_map/ppermute | solution.py:394
  17.5 1.4 %copy-start.1 = (s32[128,4]{0,1:T(4,128)S(1)}, s32[128,4]{0,1:T(4,128)}, u32[]{:S(2)}) copy-start(s32[128,4]{0,1:T(4,128)} %param.7) | copy-start | bytes 6148
  17.5 1.4 %collective-permute-start.6 = (bf16[6,72,128]{2,1,0:T(8,128)(2,1)S(1)}, bf16[6,72,128]{2,1,0:T(8,128)(2,1)S(1)}, u32[]{:S(2)}, u32[]{:S(2)}) collective-permute-start(bf16[6,72,128]{2,1,0:T(8,128)(2,1)S(1)} %get-tuple-element.18), channel_id=1, source_target_pairs={{0,4},{1,5},{2,6},{3,7},{4,0},{5,1},{6,2},{7,3},{8,12},{9,13},{10,... | collective-permute-start | bytes 331784 | tf_op jit(solution)/shard_map/ppermute | solution.py:394
  27.6 7.0 %collective-permute-start.7 = (s16[16,3200]{1,0:T(8,128)(2,1)S(1)}, s16[16,3200]{1,0:T(8,128)(2,1)S(1)}, u32[]{:S(2)}, u32[]{:S(2)}) collective-permute-start(s16[16,3200]{1,0:T(8,128)(2,1)S(1)} %get-tuple-element.19), channel_id=1, source_target_pairs={{0,0},{1,4},{2,8},{3,12},{4,2},{5,6},{6,10},{7,14},{8,1},{9,5},{10... | collective-permute-start | bytes 307208 | tf_op jit(solution)/shard_map/ppermute | solution.py:399
  32.0 6.1 %collective-permute-start.8 = (s16[16,3200]{1,0:T(8,128)(2,1)S(1)}, s16[16,3200]{1,0:T(8,128)(2,1)S(1)}, u32[]{:S(2)}, u32[]{:S(2)}) collective-permute-start(s16[16,3200]{1,0:T(8,128)(2,1)S(1)} %get-tuple-element.20), channel_id=1, source_target_pairs={{0,1},{1,5},{2,9},{3,13},{4,3},{5,7},{6,11},{7,15},{8,0},{9,4},{10... | collective-permute-start | bytes 307208 | tf_op jit(solution)/shard_map/ppermute | solution.py:399

commit v8 on v7

--- a/solution.py
+++ b/solution.py
@@ -406,11 +406,11 @@
     keep, send = split(offsets, active, panel)
     panel_c = swapped(keep, 1, 0)
     pieces = data.reshape(3 * nb, 128)
-    pair = jnp.concatenate([pieces, swapped(pieces, 2, 0)], axis=0)
+    pieces_y, send = lax.optimization_barrier((swapped(pieces, 2, 0), send))
+    pair = jnp.concatenate([pieces, pieces_y], axis=0)
+    panel_y = swapped(send, 2, 0)
     near = jnp.concatenate([pair, swapped(pair, 0, 1)], axis=0)
     far = swapped(near, 0, 2)
-    send, _ = lax.optimization_barrier((send, near))
-    panel_y = swapped(send, 2, 0)
     mine, mate = make_series(keep, panel_y, near, far, nb, 2 * nb + span // 128 + 8)
     mate = swapped(mate, 1, 0)
     panel_late, _ = lax.optimization_barrier((panel_y, far))

time: 39.8 us -> 39.3 us (0.987)
  starting transfers between devices: 18 us -> 17.2 us
    ppermute x2, waiting for transfers between devices: 4 us -> 4.45 us  [to_owner(): return lax.ppermute(value, ('loop', 'tgrp'), pairs)]
    ppermute x2, starting transfers between devices: 6.43 us -> 6.01 us  [to_owner(): return lax.ppermute(value, ('loop', 'tgrp'), pairs)]
where the time goes in v8:
time: 39.3 us; the launch traced here: 38.6 us
  starting transfers between devices  17.2 us (44%)
  Pallas kernels  11.1 us (28%)
  waiting for transfers between devices  7.03 us (18%)
  local copies, waits for them, and re-layouts  2.43 us (6%)
  between operations  0.74 us (2%)
    ppermute x7, starting transfers between devices, swapped(): return lax.ppermute(value, ('loop', 'tgrp'), pairs)  11.2 us
    pallas_call x1, Pallas kernels, correlate_stations(): pl.pallas_call(functools.partial(correlate_kernel, span, nb), out_shape=(...  8.73 us
    ppermute x2, starting transfers between devices, to_owner(): return lax.ppermute(value, ('loop', 'tgrp'), pairs)  6.01 us
    ppermute x2, waiting for transfers between devices, to_owner(): return lax.ppermute(value, ('loop', 'tgrp'), pairs)  4.45 us
    ppermute x7, waiting for transfers between devices, swapped(): return lax.ppermute(value, ('loop', 'tgrp'), pairs)  2.58 us
    unnamed x8, local copies, waits for them, and re-layouts  1.66 us
    pallas_call x1, Pallas kernels, decode(): pl.pallas_call(decode_kernel, out_shape=jax.ShapeDtypeStruct((2 * ROWS, f...  0.98 us
    pallas_call x1, Pallas kernels, split(): pl.pallas_call(split_kernel, out_shape=(half, half), in_specs=[pl.BlockSp...  0.84 us
  transfers between devices with their start and end apart: 9, of which 4 were waited for; matrix products, arithmetic and copies ran while one was open for 0% of the time, Pallas kernels for 4%

profile of v8, /device:TPU:1, one launch (start us, length us, event | category | flops | bytes accessed | tf_op | source)
XLA Modules:
  0.0 38.6 jit_solution(13331727176290046644)
XLA Ops:
  0.0 0.8 %reshape.3 = bf16[72,128]{1,0:T(8,128)(2,1)S(1)} reshape(bf16[1,3,3072]{2,1,0:T(4,128)(2,1)} %param.5) | data formatting | bytes 36864 | tf_op jit(solution)/shard_map/reshape | solution.py:408
  0.8 2.1 %collective-permute-start.1 = (bf16[72,128]{1,0:T(8,128)(2,1)S(1)}, bf16[72,128]{1,0:T(8,128)(2,1)S(1)}, u32[]{:S(2)}, u32[]{:S(2)}) collective-permute-start(bf16[72,128]{1,0:T(8,128)(2,1)S(1)} %reshape.3), channel_id=1, source_target_pairs={{0,8},{1,9},{2,10},{3,11},{4,12},{5,13},{6,14},{7,15},{8,0},{9,1},... | collective-permute-start | bytes 55304 | tf_op jit(solution)/shard_map/ppermute | solution.py:394
  3.6 0.0 copy-start.2
  3.6 0.6 %copy-done.2 = s32[1,3]{1,0:T(1,128)S(1)} copy-done((s32[1,3]{1,0:T(1,128)S(1)}, s32[1,3]{1,0:T(1,128)}, u32[]{:S(2)}) %copy-start.2) | copy-done | bytes 36
  4.2 1.0 %copy-done = bf16[32,1,3,2048]{3,0,2,1:T(8,128)(2,1)S(1)} copy-done((bf16[32,1,3,2048]{3,0,2,1:T(8,128)(2,1)S(1)}, bf16[32,1,3,2048]{3,0,2,1:T(8,128)(2,1)}, u32[]{:S(2)}) %copy-start) | copy-done | bytes 393240
  5.2 0.8 %split.1 = (bf16[3,16,2176]{2,1,0:T(8,128)(2,1)S(1)}, bf16[3,16,2176]{2,1,0:T(8,128)(2,1)S(1)}) custom-call(s32[1]{0:T(128)S(6)} %copy.8.offset_in, s32[1,3]{1,0:T(1,128)S(1)} %copy-done.2, bf16[3,32,2048]{2,1,0:T(8,128)(2,1)S(1)} %bitcast.4), custom_call_target="tpu_custom_call" | custom-call | tf_op jit(solution)/shard_map/split/pallas_call | solution.py:137
  6.1 0.0 collective-permute-done.1
  6.1 1.4 %collective-permute-start.3 = (bf16[144,128]{1,0:T(8,128)(2,1)S(1)}, bf16[144,128]{1,0:T(8,128)(2,1)S(1)}, u32[]{:S(2)}, u32[]{:S(2)}) collective-permute-start(bf16[144,128]{1,0:T(8,128)(2,1)S(1)} %pad_maximum_fusion), channel_id=1, source_target_pairs={{0,1},{1,0},{2,3},{3,2},{4,5},{5,4},{6,7},{7,6},{8,9},{9,8},{10,11... | collective-permute-start | bytes 110600 | tf_op jit(solution)/shard_map/ppermute | solution.py:394
  7.4 0.2 collective-permute-start.2
  7.7 1.3 %collective-permute-done.3 = bf16[144,128]{1,0:T(8,128)(2,1)S(1)} collective-permute-done((bf16[144,128]{1,0:T(8,128)(2,1)S(1)}, bf16[144,128]{1,0:T(8,128)(2,1)S(1)}, u32[]{:S(2)}, u32[]{:S(2)}) %collective-permute-start.3) | collective-permute-done | bytes 36896 | tf_op jit(solution)/shard_map/ppermute | solution.py:394
  9.0 2.4 %collective-permute-start.4 = (bf16[288,128]{1,0:T(8,128)(2,1)S(1)}, bf16[288,128]{1,0:T(8,128)(2,1)S(1)}, u32[]{:S(2)}, u32[]{:S(2)}) collective-permute-start(bf16[288,128]{1,0:T(8,128)(2,1)S(1)} %constant_dynamic-update-slice_fusion.near), channel_id=1, source_target_pairs={{0,2},{1,3},{2,0},{3,1},{4,6},{5,7},{6,4},{7,5},{8,10},{9,11},{10,... | collective-permute-start | bytes 221192 | tf_op jit(solution)/shard_map/ppermute | solution.py:394
  11.3 2.4 %collective-permute-start = (bf16[3,16,2176]{2,1,0:T(8,128)(2,1)S(1)}, bf16[3,16,2176]{2,1,0:T(8,128)(2,1)S(1)}, u32[]{:S(2)}, u32[]{:S(2)}) collective-permute-start(bf16[3,16,2176]{2,1,0:T(8,128)(2,1)S(1)} %get-tuple-element.14.own.t0), channel_id=1, source_target_pairs={{0,4},{1,5},{2,6},{3,7},{4,0},{5,1},{6,2},{7,3},{8,12},{9,13},{10,... | collective-permute-start | bytes 626696 | tf_op jit(solution)/shard_map/ppermute | solution.py:394
  13.7 2.7 %collective-permute-start.5 = (bf16[3,16,2176]{2,1,0:T(8,128)(2,1)S(1)}, bf16[3,16,2176]{2,1,0:T(8,128)(2,1)S(1)}, u32[]{:S(2)}, u32[]{:S(2)}) collective-permute-start(bf16[3,16,2176]{2,1,0:T(8,128)(2,1)S(1)} %collective-permute-done.2.told.t2), channel_id=1, source_target_pairs={{0,4},{1,5},{2,6},{3,7},{4,0},{5,1},{6,2},{7,3},{8,12},{9,13},{10,... | collective-permute-start | bytes 626696 | tf_op jit(solution)/shard_map/ppermute | solution.py:394
  16.4 0.6 %series.1 = (bf16[6,72,128]{2,1,0:T(8,128)(2,1)S(1)}, bf16[6,72,128]{2,1,0:T(8,128)(2,1)S(1)}) custom-call(bf16[3,16,2176]{2,1,0:T(8,128)(2,1)S(1)} %get-tuple-element.14.own.t0, bf16[3,16,2176]{2,1,0:T(8,128)(2,1)S(1)} %collective-permute-done.2.told.t2, bf16[288,128]{1,0:T(8,128)(2,1)S(1)} %constant_dynamic-update-slice_fusion.near, ...), custom_call_target="tpu_custom_call" | custom-call | tf_op jit(solution)/shard_map/series/pallas_call | solution.py:185
  17.0 0.0 copy-start.1
  17.0 0.1 collective-permute-start.6
  17.1 0.0 collective-permute-done.t1
  17.1 1.3 %collective-permute-done.6.mate = bf16[6,72,128]{2,1,0:T(8,128)(2,1)S(1)} collective-permute-done((bf16[6,72,128]{2,1,0:T(8,128)(2,1)S(1)}, bf16[6,72,128]{2,1,0:T(8,128)(2,1)S(1)}, u32[]{:S(2)}, u32[]{:S(2)}) %collective-permute-start.6) | collective-permute-done | bytes 110624 | tf_op jit(solution)/shard_map/ppermute | solution.py:394
  18.4 8.7 %correlate.1 = (s16[16,3200]{1,0:T(8,128)(2,1)S(1)}, s16[16,3200]{1,0:T(8,128)(2,1)S(1)}) custom-call(bf16[3,16,2176]{2,1,0:T(8,128)(2,1)S(1)} %get-tuple-element.14.own.t0, bf16[3,16,2176]{2,1,0:T(8,128)(2,1)S(1)} %collective-permute-done.t1, bf16[3,16,2176]{2,1,0:T(8,128)(2,1)S(1)} %collective-permute-done.2.told.t2, ...), custom_call_target="tpu_custom_call" | custom-call | tf_op jit(solution)/shard_map/correlate/pallas_call | solution.py:370
  27.1 4.3 %collective-permute-start.7 = (s16[16,3200]{1,0:T(8,128)(2,1)S(1)}, s16[16,3200]{1,0:T(8,128)(2,1)S(1)}, u32[]{:S(2)}, u32[]{:S(2)}) collective-permute-start(s16[16,3200]{1,0:T(8,128)(2,1)S(1)} %get-tuple-element.21), channel_id=1, source_target_pairs={{0,0},{1,4},{2,8},{3,12},{4,2},{5,6},{6,10},{7,14},{8,1},{9,5},{10... | collective-permute-start | bytes 307208 | tf_op jit(solution)/shard_map/ppermute | solution.py:399
  31.4 1.7 %collective-permute-start.8 = (s16[16,3200]{1,0:T(8,128)(2,1)S(1)}, s16[16,3200]{1,0:T(8,128)(2,1)S(1)}, u32[]{:S(2)}, u32[]{:S(2)}) collective-permute-start(s16[16,3200]{1,0:T(8,128)(2,1)S(1)} %get-tuple-element.22), channel_id=1, source_target_pairs={{0,1},{1,5},{2,9},{3,13},{4,3},{5,7},{6,11},{7,15},{8,0},{9,4},{10... | collective-permute-start | bytes 307208 | tf_op jit(solution)/shard_map/ppermute | solution.py:399
  33.1 1.4 %collective-permute-done.7.a_ref = s16[16,3200]{1,0:T(8,128)(2,1)S(1)} collective-permute-done((s16[16,3200]{1,0:T(8,128)(2,1)S(1)}, s16[16,3200]{1,0:T(8,128)(2,1)S(1)}, u32[]{:S(2)}, u32[]{:S(2)}) %collective-permute-start.7) | collective-permute-done | bytes 102432 | tf_op jit(solution)/shard_map/ppermute | solution.py:399
  34.5 3.1 %collective-permute-done.8.b_ref = s16[16,3200]{1,0:T(8,128)(2,1)S(1)} collective-permute-done((s16[16,3200]{1,0:T(8,128)(2,1)S(1)}, s16[16,3200]{1,0:T(8,128)(2,1)S(1)}, u32[]{:S(2)}, u32[]{:S(2)}) %collective-permute-start.8) | collective-permute-done | bytes 102432 | tf_op jit(solution)/shard_map/ppermute | solution.py:399
  37.6 1.0 %decode.1 = f32[32,3072]{1,0:T(8,128)} custom-call(s16[16,3200]{1,0:T(8,128)(2,1)S(1)} %collective-permute-done.7.a_ref, s16[16,3200]{1,0:T(8,128)(2,1)S(1)} %collective-permute-done.8.b_ref), custom_call_target="tpu_custom_call" | custom-call | tf_op jit(solution)/shard_map/decode/pallas_call | solution.py:355
  (9 shorter events, 0.0 us)
Async XLA Ops:
  0.8 5.3 %collective-permute-start.1 = (bf16[72,128]{1,0:T(8,128)(2,1)S(1)}, bf16[72,128]{1,0:T(8,128)(2,1)S(1)}, u32[]{:S(2)}, u32[]{:S(2)}) collective-permute-start(bf16[72,128]{1,0:T(8,128)(2,1)S(1)} %reshape.3), channel_id=1, source_target_pairs={{0,8},{1,9},{2,10},{3,11},{4,12},{5,13},{6,14},{7,15},{8,0},{9,1},... | collective-permute-start | bytes 55304 | tf_op jit(solution)/shard_map/ppermute | solution.py:394
  3.6 0.7 %copy-start.2 = (s32[1,3]{1,0:T(1,128)S(1)}, s32[1,3]{1,0:T(1,128)}, u32[]{:S(2)}) copy-start(s32[1,3]{1,0:T(1,128)} %active_in.1) | copy-start | bytes 40
  4.2 1.0 %copy-start = (bf16[32,1,3,2048]{3,0,2,1:T(8,128)(2,1)S(1)}, bf16[32,1,3,2048]{3,0,2,1:T(8,128)(2,1)}, u32[]{:S(2)}) copy-start(bf16[32,1,3,2048]{3,0,2,1:T(8,128)(2,1)} %param.6) | copy-start | bytes 1179652
  6.1 2.9 %collective-permute-start.3 = (bf16[144,128]{1,0:T(8,128)(2,1)S(1)}, bf16[144,128]{1,0:T(8,128)(2,1)S(1)}, u32[]{:S(2)}, u32[]{:S(2)}) collective-permute-start(bf16[144,128]{1,0:T(8,128)(2,1)S(1)} %pad_maximum_fusion), channel_id=1, source_target_pairs={{0,1},{1,0},{2,3},{3,2},{4,5},{5,4},{6,7},{7,6},{8,9},{9,8},{10,11... | collective-permute-start | bytes 110600 | tf_op jit(solution)/shard_map/ppermute | solution.py:394
  7.4 6.3 %collective-permute-start.2 = (bf16[3,16,2176]{2,1,0:T(8,128)(2,1)S(1)}, bf16[3,16,2176]{2,1,0:T(8,128)(2,1)S(1)}, u32[]{:S(2)}, u32[]{:S(2)}) collective-permute-start(bf16[3,16,2176]{2,1,0:T(8,128)(2,1)S(1)} %get-tuple-element.16), channel_id=1, source_target_pairs={{0,8},{1,9},{2,10},{3,11},{4,12},{5,13},{6,14},{7,15},{8,0},{9,1},... | collective-permute-start | bytes 626696 | tf_op jit(solution)/shard_map/ppermute | solution.py:394
  9.0 4.8 %collective-permute-start.4 = (bf16[288,128]{1,0:T(8,128)(2,1)S(1)}, bf16[288,128]{1,0:T(8,128)(2,1)S(1)}, u32[]{:S(2)}, u32[]{:S(2)}) collective-permute-start(bf16[288,128]{1,0:T(8,128)(2,1)S(1)} %constant_dynamic-update-slice_fusion.near), channel_id=1, source_target_pairs={{0,2},{1,3},{2,0},{3,1},{4,6},{5,7},{6,4},{7,5},{8,10},{9,11},{10,... | collective-permute-start | bytes 221192 | tf_op jit(solution)/shard_map/ppermute | solution.py:394
  11.3 5.7 %collective-permute-start = (bf16[3,16,2176]{2,1,0:T(8,128)(2,1)S(1)}, bf16[3,16,2176]{2,1,0:T(8,128)(2,1)S(1)}, u32[]{:S(2)}, u32[]{:S(2)}) collective-permute-start(bf16[3,16,2176]{2,1,0:T(8,128)(2,1)S(1)} %get-tuple-element.14.own.t0), channel_id=1, source_target_pairs={{0,4},{1,5},{2,6},{3,7},{4,0},{5,1},{6,2},{7,3},{8,12},{9,13},{10,... | collective-permute-start | bytes 626696 | tf_op jit(solution)/shard_map/ppermute | solution.py:394
  13.7 4.6 %collective-permute-start.5 = (bf16[3,16,2176]{2,1,0:T(8,128)(2,1)S(1)}, bf16[3,16,2176]{2,1,0:T(8,128)(2,1)S(1)}, u32[]{:S(2)}, u32[]{:S(2)}) collective-permute-start(bf16[3,16,2176]{2,1,0:T(8,128)(2,1)S(1)} %collective-permute-done.2.told.t2), channel_id=1, source_target_pairs={{0,4},{1,5},{2,6},{3,7},{4,0},{5,1},{6,2},{7,3},{8,12},{9,13},{10,... | collective-permute-start | bytes 626696 | tf_op jit(solution)/shard_map/ppermute | solution.py:394
  17.0 1.4 %copy-start.1 = (s32[128,4]{0,1:T(4,128)S(1)}, s32[128,4]{0,1:T(4,128)}, u32[]{:S(2)}) copy-start(s32[128,4]{0,1:T(4,128)} %param.7) | copy-start | bytes 6148
  17.0 1.4 %collective-permute-start.6 = (bf16[6,72,128]{2,1,0:T(8,128)(2,1)S(1)}, bf16[6,72,128]{2,1,0:T(8,128)(2,1)S(1)}, u32[]{:S(2)}, u32[]{:S(2)}) collective-permute-start(bf16[6,72,128]{2,1,0:T(8,128)(2,1)S(1)} %get-tuple-element.20), channel_id=1, source_target_pairs={{0,4},{1,5},{2,6},{3,7},{4,0},{5,1},{6,2},{7,3},{8,12},{9,13},{10,... | collective-permute-start | bytes 331784 | tf_op jit(solution)/shard_map/ppermute | solution.py:394
  27.1 7.4 %collective-permute-start.7 = (s16[16,3200]{1,0:T(8,128)(2,1)S(1)}, s16[16,3200]{1,0:T(8,128)(2,1)S(1)}, u32[]{:S(2)}, u32[]{:S(2)}) collective-permute-start(s16[16,3200]{1,0:T(8,128)(2,1)S(1)} %get-tuple-element.21), channel_id=1, source_target_pairs={{0,0},{1,4},{2,8},{3,12},{4,2},{5,6},{6,10},{7,14},{8,1},{9,5},{10... | collective-permute-start | bytes 307208 | tf_op jit(solution)/shard_map/ppermute | solution.py:399
  31.4 6.1 %collective-permute-start.8 = (s16[16,3200]{1,0:T(8,128)(2,1)S(1)}, s16[16,3200]{1,0:T(8,128)(2,1)S(1)}, u32[]{:S(2)}, u32[]{:S(2)}) collective-permute-start(s16[16,3200]{1,0:T(8,128)(2,1)S(1)} %get-tuple-element.22), channel_id=1, source_target_pairs={{0,1},{1,5},{2,9},{3,13},{4,3},{5,7},{6,11},{7,15},{8,0},{9,4},{10... | collective-permute-start | bytes 307208 | tf_op jit(solution)/shard_map/ppermute | solution.py:399

commit v9 on v8

--- a/solution.py
+++ b/solution.py
@@ -161,8 +161,8 @@
     for b in range(4):
         at = pl.multiple_of(blocks * (z ^ b), 8)
         for i in range(6):
-            first = 6 * blocks * (b % 2) + i * blocks
-            whole[i, pl.ds(at, blocks), :] = wide[b // 2][first : first + blocks]
+            first = 6 * blocks * (b // 2) + i * blocks
+            whole[i, pl.ds(at, blocks), :] = wide[b % 2][first : first + blocks]
     for station in range(2):
         words = (own, told)[station]
         first = words[0, :, span:].astype(jnp.float32)
@@ -409,8 +409,8 @@
     pieces_y, send = lax.optimization_barrier((swapped(pieces, 2, 0), send))
     pair = jnp.concatenate([pieces, pieces_y], axis=0)
     panel_y = swapped(send, 2, 0)
-    near = jnp.concatenate([pair, swapped(pair, 0, 1)], axis=0)
-    far = swapped(near, 0, 2)
+    near = jnp.concatenate([pair, swapped(pair, 0, 2)], axis=0)
+    far = swapped(near, 0, 1)
     mine, mate = make_series(keep, panel_y, near, far, nb, 2 * nb + span // 128 + 8)
     mate = swapped(mate, 1, 0)
     panel_late, _ = lax.optimization_barrier((panel_y, far))

time: 39.3 us -> 38.9 us (0.990)
  waiting for transfers between devices: 7.03 us -> 7.54 us
  starting transfers between devices: 17.2 us -> 16.7 us
    ppermute x2, starting transfers between devices: 6.01 us -> 5.61 us  [to_owner(): return lax.ppermute(value, ('loop', 'tgrp'), pairs)]
  transfers between devices with their start and end apart: 9 -> 9, of which waited for: 4 -> 5; matrix products, arithmetic and copies ran while one was open for 0% -> 0% of each run, Pallas kernels for 4% -> 4%
where the time goes in v9:
time: 38.9 us; the launch traced here: 38.5 us
  starting transfers between devices  16.7 us (43%)
  Pallas kernels  11.1 us (29%)
  waiting for transfers between devices  7.54 us (19%)
  local copies, waits for them, and re-layouts  2.43 us (6%)
  between operations  0.74 us (2%)
    ppermute x7, starting transfers between devices, swapped(): return lax.ppermute(value, ('loop', 'tgrp'), pairs)  11.1 us
    pallas_call x1, Pallas kernels, correlate_stations(): pl.pallas_call(functools.partial(correlate_kernel, span, nb), out_shape=(...  8.73 us
    ppermute x2, starting transfers between devices, to_owner(): return lax.ppermute(value, ('loop', 'tgrp'), pairs)  5.61 us
    ppermute x2, waiting for transfers between devices, to_owner(): return lax.ppermute(value, ('loop', 'tgrp'), pairs)  4.8 us
    ppermute x7, waiting for transfers between devices, swapped(): return lax.ppermute(value, ('loop', 'tgrp'), pairs)  2.73 us
    unnamed x8, local copies, waits for them, and re-layouts  1.66 us
    pallas_call x1, Pallas kernels, decode(): pl.pallas_call(decode_kernel, out_shape=jax.ShapeDtypeStruct((2 * ROWS, f...  0.98 us
    pallas_call x1, Pallas kernels, split(): pl.pallas_call(split_kernel, out_shape=(half, half), in_specs=[pl.BlockSp...  0.84 us
  transfers between devices with their start and end apart: 9, of which 5 were waited for; matrix products, arithmetic and copies ran while one was open for 0% of the time, Pallas kernels for 4%

profile of v9, /device:TPU:1, one launch (start us, length us, event | category | flops | bytes accessed | tf_op | source)
XLA Modules:
  0.0 38.5 jit_solution(5595206593180070989)
XLA Ops:
  0.0 0.8 %reshape.3 = bf16[72,128]{1,0:T(8,128)(2,1)S(1)} reshape(bf16[1,3,3072]{2,1,0:T(4,128)(2,1)} %param.5) | data formatting | bytes 36864 | tf_op jit(solution)/shard_map/reshape | solution.py:408
  0.8 2.1 %collective-permute-start.1 = (bf16[72,128]{1,0:T(8,128)(2,1)S(1)}, bf16[72,128]{1,0:T(8,128)(2,1)S(1)}, u32[]{:S(2)}, u32[]{:S(2)}) collective-permute-start(bf16[72,128]{1,0:T(8,128)(2,1)S(1)} %reshape.3), channel_id=1, source_target_pairs={{0,8},{1,9},{2,10},{3,11},{4,12},{5,13},{6,14},{7,15},{8,0},{9,1},... | collective-permute-start | bytes 55304 | tf_op jit(solution)/shard_map/ppermute | solution.py:394
  3.6 0.0 copy-start.2
  3.6 0.6 %copy-done.2 = s32[1,3]{1,0:T(1,128)S(1)} copy-done((s32[1,3]{1,0:T(1,128)S(1)}, s32[1,3]{1,0:T(1,128)}, u32[]{:S(2)}) %copy-start.2) | copy-done | bytes 36
  4.2 1.0 %copy-done = bf16[32,1,3,2048]{3,0,2,1:T(8,128)(2,1)S(1)} copy-done((bf16[32,1,3,2048]{3,0,2,1:T(8,128)(2,1)S(1)}, bf16[32,1,3,2048]{3,0,2,1:T(8,128)(2,1)}, u32[]{:S(2)}) %copy-start) | copy-done | bytes 393240
  5.2 0.8 %split.1 = (bf16[3,16,2176]{2,1,0:T(8,128)(2,1)S(1)}, bf16[3,16,2176]{2,1,0:T(8,128)(2,1)S(1)}) custom-call(s32[1]{0:T(128)S(6)} %copy.8.offset_in, s32[1,3]{1,0:T(1,128)S(1)} %copy-done.2, bf16[3,32,2048]{2,1,0:T(8,128)(2,1)S(1)} %bitcast.4), custom_call_target="tpu_custom_call" | custom-call | tf_op jit(solution)/shard_map/split/pallas_call | solution.py:137
  6.1 0.0 collective-permute-done.1
  6.1 2.4 %collective-permute-start.3 = (bf16[144,128]{1,0:T(8,128)(2,1)S(1)}, bf16[144,128]{1,0:T(8,128)(2,1)S(1)}, u32[]{:S(2)}, u32[]{:S(2)}) collective-permute-start(bf16[144,128]{1,0:T(8,128)(2,1)S(1)} %pad_maximum_fusion), channel_id=1, source_target_pairs={{0,2},{1,3},{2,0},{3,1},{4,6},{5,7},{6,4},{7,5},{8,10},{9,11},{10,... | collective-permute-start | bytes 110600 | tf_op jit(solution)/shard_map/ppermute | solution.py:394
  8.5 0.2 collective-permute-start.2
  8.7 1.2 %collective-permute-done.3 = bf16[144,128]{1,0:T(8,128)(2,1)S(1)} collective-permute-done((bf16[144,128]{1,0:T(8,128)(2,1)S(1)}, bf16[144,128]{1,0:T(8,128)(2,1)S(1)}, u32[]{:S(2)}, u32[]{:S(2)}) %collective-permute-start.3) | collective-permute-done | bytes 36896 | tf_op jit(solution)/shard_map/ppermute | solution.py:394
  9.9 1.4 %collective-permute-start.4 = (bf16[288,128]{1,0:T(8,128)(2,1)S(1)}, bf16[288,128]{1,0:T(8,128)(2,1)S(1)}, u32[]{:S(2)}, u32[]{:S(2)}) collective-permute-start(bf16[288,128]{1,0:T(8,128)(2,1)S(1)} %constant_dynamic-update-slice_fusion.near), channel_id=1, source_target_pairs={{0,1},{1,0},{2,3},{3,2},{4,5},{5,4},{6,7},{7,6},{8,9},{9,8},{10,11... | collective-permute-start | bytes 221192 | tf_op jit(solution)/shard_map/ppermute | solution.py:394
  11.2 2.4 %collective-permute-start = (bf16[3,16,2176]{2,1,0:T(8,128)(2,1)S(1)}, bf16[3,16,2176]{2,1,0:T(8,128)(2,1)S(1)}, u32[]{:S(2)}, u32[]{:S(2)}) collective-permute-start(bf16[3,16,2176]{2,1,0:T(8,128)(2,1)S(1)} %get-tuple-element.14.own.t0), channel_id=1, source_target_pairs={{0,4},{1,5},{2,6},{3,7},{4,0},{5,1},{6,2},{7,3},{8,12},{9,13},{10,... | collective-permute-start | bytes 626696 | tf_op jit(solution)/shard_map/ppermute | solution.py:394
  13.6 0.3 collective-permute-done.2.told.t2
  13.9 2.5 %collective-permute-start.5 = (bf16[3,16,2176]{2,1,0:T(8,128)(2,1)S(1)}, bf16[3,16,2176]{2,1,0:T(8,128)(2,1)S(1)}, u32[]{:S(2)}, u32[]{:S(2)}) collective-permute-start(bf16[3,16,2176]{2,1,0:T(8,128)(2,1)S(1)} %collective-permute-done.2.told.t2), channel_id=1, source_target_pairs={{0,4},{1,5},{2,6},{3,7},{4,0},{5,1},{6,2},{7,3},{8,12},{9,13},{10,... | collective-permute-start | bytes 626696 | tf_op jit(solution)/shard_map/ppermute | solution.py:394
  16.4 0.6 %series.1 = (bf16[6,72,128]{2,1,0:T(8,128)(2,1)S(1)}, bf16[6,72,128]{2,1,0:T(8,128)(2,1)S(1)}) custom-call(bf16[3,16,2176]{2,1,0:T(8,128)(2,1)S(1)} %get-tuple-element.14.own.t0, bf16[3,16,2176]{2,1,0:T(8,128)(2,1)S(1)} %collective-permute-done.2.told.t2, bf16[288,128]{1,0:T(8,128)(2,1)S(1)} %constant_dynamic-update-slice_fusion.near, ...), custom_call_target="tpu_custom_call" | custom-call | tf_op jit(solution)/shard_map/series/pallas_call | solution.py:185
  17.0 0.0 copy-start.1
  17.0 0.1 collective-permute-start.6
  17.1 1.3 %collective-permute-done.6.mate = bf16[6,72,128]{2,1,0:T(8,128)(2,1)S(1)} collective-permute-done((bf16[6,72,128]{2,1,0:T(8,128)(2,1)S(1)}, bf16[6,72,128]{2,1,0:T(8,128)(2,1)S(1)}, u32[]{:S(2)}, u32[]{:S(2)}) %collective-permute-start.6) | collective-permute-done | bytes 110624 | tf_op jit(solution)/shard_map/ppermute | solution.py:394
  18.4 8.7 %correlate.1 = (s16[16,3200]{1,0:T(8,128)(2,1)S(1)}, s16[16,3200]{1,0:T(8,128)(2,1)S(1)}) custom-call(bf16[3,16,2176]{2,1,0:T(8,128)(2,1)S(1)} %get-tuple-element.14.own.t0, bf16[3,16,2176]{2,1,0:T(8,128)(2,1)S(1)} %collective-permute-done.t1, bf16[3,16,2176]{2,1,0:T(8,128)(2,1)S(1)} %collective-permute-done.2.told.t2, ...), custom_call_target="tpu_custom_call" | custom-call | tf_op jit(solution)/shard_map/correlate/pallas_call | solution.py:370
  27.1 4.3 %collective-permute-start.7 = (s16[16,3200]{1,0:T(8,128)(2,1)S(1)}, s16[16,3200]{1,0:T(8,128)(2,1)S(1)}, u32[]{:S(2)}, u32[]{:S(2)}) collective-permute-start(s16[16,3200]{1,0:T(8,128)(2,1)S(1)} %get-tuple-element.21), channel_id=1, source_target_pairs={{0,0},{1,4},{2,8},{3,12},{4,2},{5,6},{6,10},{7,14},{8,1},{9,5},{10... | collective-permute-start | bytes 307208 | tf_op jit(solution)/shard_map/ppermute | solution.py:399
  31.4 1.3 %collective-permute-start.8 = (s16[16,3200]{1,0:T(8,128)(2,1)S(1)}, s16[16,3200]{1,0:T(8,128)(2,1)S(1)}, u32[]{:S(2)}, u32[]{:S(2)}) collective-permute-start(s16[16,3200]{1,0:T(8,128)(2,1)S(1)} %get-tuple-element.22), channel_id=1, source_target_pairs={{0,1},{1,5},{2,9},{3,13},{4,3},{5,7},{6,11},{7,15},{8,0},{9,4},{10... | collective-permute-start | bytes 307208 | tf_op jit(solution)/shard_map/ppermute | solution.py:399
  32.7 1.8 %collective-permute-done.7.a_ref = s16[16,3200]{1,0:T(8,128)(2,1)S(1)} collective-permute-done((s16[16,3200]{1,0:T(8,128)(2,1)S(1)}, s16[16,3200]{1,0:T(8,128)(2,1)S(1)}, u32[]{:S(2)}, u32[]{:S(2)}) %collective-permute-start.7) | collective-permute-done | bytes 102432 | tf_op jit(solution)/shard_map/ppermute | solution.py:399
  34.5 3.0 %collective-permute-done.8.b_ref = s16[16,3200]{1,0:T(8,128)(2,1)S(1)} collective-permute-done((s16[16,3200]{1,0:T(8,128)(2,1)S(1)}, s16[16,3200]{1,0:T(8,128)(2,1)S(1)}, u32[]{:S(2)}, u32[]{:S(2)}) %collective-permute-start.8) | collective-permute-done | bytes 102432 | tf_op jit(solution)/shard_map/ppermute | solution.py:399
  37.5 1.0 %decode.1 = f32[32,3072]{1,0:T(8,128)} custom-call(s16[16,3200]{1,0:T(8,128)(2,1)S(1)} %collective-permute-done.7.a_ref, s16[16,3200]{1,0:T(8,128)(2,1)S(1)} %collective-permute-done.8.b_ref), custom_call_target="tpu_custom_call" | custom-call | tf_op jit(solution)/shard_map/decode/pallas_call | solution.py:355
  (9 shorter events, 0.0 us)
Async XLA Ops:
  0.8 5.3 %collective-permute-start.1 = (bf16[72,128]{1,0:T(8,128)(2,1)S(1)}, bf16[72,128]{1,0:T(8,128)(2,1)S(1)}, u32[]{:S(2)}, u32[]{:S(2)}) collective-permute-start(bf16[72,128]{1,0:T(8,128)(2,1)S(1)} %reshape.3), channel_id=1, source_target_pairs={{0,8},{1,9},{2,10},{3,11},{4,12},{5,13},{6,14},{7,15},{8,0},{9,1},... | collective-permute-start | bytes 55304 | tf_op jit(solution)/shard_map/ppermute | solution.py:394
  3.6 0.7 %copy-start.2 = (s32[1,3]{1,0:T(1,128)S(1)}, s32[1,3]{1,0:T(1,128)}, u32[]{:S(2)}) copy-start(s32[1,3]{1,0:T(1,128)} %active_in.1) | copy-start | bytes 40
  4.2 1.0 %copy-start = (bf16[32,1,3,2048]{3,0,2,1:T(8,128)(2,1)S(1)}, bf16[32,1,3,2048]{3,0,2,1:T(8,128)(2,1)}, u32[]{:S(2)}) copy-start(bf16[32,1,3,2048]{3,0,2,1:T(8,128)(2,1)} %param.6) | copy-start | bytes 1179652
  6.1 3.8 %collective-permute-start.3 = (bf16[144,128]{1,0:T(8,128)(2,1)S(1)}, bf16[144,128]{1,0:T(8,128)(2,1)S(1)}, u32[]{:S(2)}, u32[]{:S(2)}) collective-permute-start(bf16[144,128]{1,0:T(8,128)(2,1)S(1)} %pad_maximum_fusion), channel_id=1, source_target_pairs={{0,2},{1,3},{2,0},{3,1},{4,6},{5,7},{6,4},{7,5},{8,10},{9,11},{10,... | collective-permute-start | bytes 110600 | tf_op jit(solution)/shard_map/ppermute | solution.py:394
  8.5 5.4 %collective-permute-start.2 = (bf16[3,16,2176]{2,1,0:T(8,128)(2,1)S(1)}, bf16[3,16,2176]{2,1,0:T(8,128)(2,1)S(1)}, u32[]{:S(2)}, u32[]{:S(2)}) collective-permute-start(bf16[3,16,2176]{2,1,0:T(8,128)(2,1)S(1)} %get-tuple-element.16), channel_id=1, source_target_pairs={{0,8},{1,9},{2,10},{3,11},{4,12},{5,13},{6,14},{7,15},{8,0},{9,1},... | collective-permute-start | bytes 626696 | tf_op jit(solution)/shard_map/ppermute | solution.py:394
  9.9 3.7 %collective-permute-start.4 = (bf16[288,128]{1,0:T(8,128)(2,1)S(1)}, bf16[288,128]{1,0:T(8,128)(2,1)S(1)}, u32[]{:S(2)}, u32[]{:S(2)}) collective-permute-start(bf16[288,128]{1,0:T(8,128)(2,1)S(1)} %constant_dynamic-update-slice_fusion.near), channel_id=1, source_target_pairs={{0,1},{1,0},{2,3},{3,2},{4,5},{5,4},{6,7},{7,6},{8,9},{9,8},{10,11... | collective-permute-start | bytes 221192 | tf_op jit(solution)/shard_map/ppermute | solution.py:394
  11.2 5.8 %collective-permute-start = (bf16[3,16,2176]{2,1,0:T(8,128)(2,1)S(1)}, bf16[3,16,2176]{2,1,0:T(8,128)(2,1)S(1)}, u32[]{:S(2)}, u32[]{:S(2)}) collective-permute-start(bf16[3,16,2176]{2,1,0:T(8,128)(2,1)S(1)} %get-tuple-element.14.own.t0), channel_id=1, source_target_pairs={{0,4},{1,5},{2,6},{3,7},{4,0},{5,1},{6,2},{7,3},{8,12},{9,13},{10,... | collective-permute-start | bytes 626696 | tf_op jit(solution)/shard_map/ppermute | solution.py:394
  13.9 4.5 %collective-permute-start.5 = (bf16[3,16,2176]{2,1,0:T(8,128)(2,1)S(1)}, bf16[3,16,2176]{2,1,0:T(8,128)(2,1)S(1)}, u32[]{:S(2)}, u32[]{:S(2)}) collective-permute-start(bf16[3,16,2176]{2,1,0:T(8,128)(2,1)S(1)} %collective-permute-done.2.told.t2), channel_id=1, source_target_pairs={{0,4},{1,5},{2,6},{3,7},{4,0},{5,1},{6,2},{7,3},{8,12},{9,13},{10,... | collective-permute-start | bytes 626696 | tf_op jit(solution)/shard_map/ppermute | solution.py:394
  17.0 1.4 %copy-start.1 = (s32[128,4]{0,1:T(4,128)S(1)}, s32[128,4]{0,1:T(4,128)}, u32[]{:S(2)}) copy-start(s32[128,4]{0,1:T(4,128)} %param.7) | copy-start | bytes 6148
  17.0 1.4 %collective-permute-start.6 = (bf16[6,72,128]{2,1,0:T(8,128)(2,1)S(1)}, bf16[6,72,128]{2,1,0:T(8,128)(2,1)S(1)}, u32[]{:S(2)}, u32[]{:S(2)}) collective-permute-start(bf16[6,72,128]{2,1,0:T(8,128)(2,1)S(1)} %get-tuple-element.20), channel_id=1, source_target_pairs={{0,4},{1,5},{2,6},{3,7},{4,0},{5,1},{6,2},{7,3},{8,12},{9,13},{10,... | collective-permute-start | bytes 331784 | tf_op jit(solution)/shard_map/ppermute | solution.py:394
  27.1 7.4 %collective-permute-start.7 = (s16[16,3200]{1,0:T(8,128)(2,1)S(1)}, s16[16,3200]{1,0:T(8,128)(2,1)S(1)}, u32[]{:S(2)}, u32[]{:S(2)}) collective-permute-start(s16[16,3200]{1,0:T(8,128)(2,1)S(1)} %get-tuple-element.21), channel_id=1, source_target_pairs={{0,0},{1,4},{2,8},{3,12},{4,2},{5,6},{6,10},{7,14},{8,1},{9,5},{10... | collective-permute-start | bytes 307208 | tf_op jit(solution)/shard_map/ppermute | solution.py:399
  31.4 6.1 %collective-permute-start.8 = (s16[16,3200]{1,0:T(8,128)(2,1)S(1)}, s16[16,3200]{1,0:T(8,128)(2,1)S(1)}, u32[]{:S(2)}, u32[]{:S(2)}) collective-permute-start(s16[16,3200]{1,0:T(8,128)(2,1)S(1)} %get-tuple-element.22), channel_id=1, source_target_pairs={{0,1},{1,5},{2,9},{3,13},{4,3},{5,7},{6,11},{7,15},{8,0},{9,4},{10... | collective-permute-start | bytes 307208 | tf_op jit(solution)/shard_map/ppermute | solution.py:399

commit v10 on v9

--- a/solution.py
+++ b/solution.py
@@ -404,7 +404,6 @@
     nb = data.shape[2] // 128
     panel = templates[:, 0].transpose(1, 0, 2)
     keep, send = split(offsets, active, panel)
-    panel_c = swapped(keep, 1, 0)
     pieces = data.reshape(3 * nb, 128)
     pieces_y, send = lax.optimization_barrier((swapped(pieces, 2, 0), send))
     pair = jnp.concatenate([pieces, pieces_y], axis=0)
@@ -413,7 +412,8 @@
     far = swapped(near, 0, 1)
     mine, mate = make_series(keep, panel_y, near, far, nb, 2 * nb + span // 128 + 8)
     mate = swapped(mate, 1, 0)
-    panel_late, _ = lax.optimization_barrier((panel_y, far))
+    keep_late, panel_late, _ = lax.optimization_barrier((keep, panel_y, far))
+    panel_c = swapped(keep_late, 1, 0)
     panel_yc = swapped(panel_late, 1, 0)
     first, second = correlate_stations(
         (keep, panel_c, panel_y, panel_yc), (mine, mate), masks.T, span, nb

time: 38.9 us -> 39.3 us (1.010)
  waiting for transfers between devices: 7.54 us -> 9.59 us
  starting transfers between devices: 16.7 us -> 15 us
    ppermute x7, waiting for transfers between devices: 2.73 us -> 4.79 us  [swapped(): return lax.ppermute(value, ('loop', 'tgrp'), pairs)]
    ppermute x7, starting transfers between devices: 11.1 us -> 9.17 us  [swapped(): return lax.ppermute(value, ('loop', 'tgrp'), pairs)]
  transfers between devices with their start and end apart: 9 -> 9, of which waited for: 5 -> 6; matrix products, arithmetic and copies ran while one was open for 0% -> 0% of each run, Pallas kernels for 4% -> 4%
where the time goes in v10:
time: 39.3 us; the launch traced here: 38.9 us
  starting transfers between devices  15 us (38%)
  Pallas kernels  11.1 us (28%)
  waiting for transfers between devices  9.59 us (24%)
  local copies, waits for them, and re-layouts  2.43 us (6%)
  between operations  0.73 us (2%)
    ppermute x7, starting transfers between devices, swapped(): return lax.ppermute(value, ('loop', 'tgrp'), pairs)  9.17 us
    pallas_call x1, Pallas kernels, correlate_stations(): pl.pallas_call(functools.partial(correlate_kernel, span, nb), out_shape=(...  8.75 us
    ppermute x2, starting transfers between devices, to_owner(): return lax.ppermute(value, ('loop', 'tgrp'), pairs)  5.83 us
    ppermute x2, waiting for transfers between devices, to_owner(): return lax.ppermute(value, ('loop', 'tgrp'), pairs)  4.8 us
    ppermute x7, waiting for transfers between devices, swapped(): return lax.ppermute(value, ('loop', 'tgrp'), pairs)  4.79 us
    unnamed x8, local copies, waits for them, and re-layouts  1.66 us
    pallas_call x1, Pallas kernels, decode(): pl.pallas_call(decode_kernel, out_shape=jax.ShapeDtypeStruct((2 * ROWS, f...  0.98 us
    pallas_call x1, Pallas kernels, split(): pl.pallas_call(split_kernel, out_shape=(half, half), in_specs=[pl.BlockSp...  0.84 us
  transfers between devices with their start and end apart: 9, of which 6 were waited for; matrix products, arithmetic and copies ran while one was open for 0% of the time, Pallas kernels for 4%

profile of v10, /device:TPU:1, one launch (start us, length us, event | category | flops | bytes accessed | tf_op | source)
XLA Modules:
  0.0 38.9 jit_solution(10985548825527686578)
XLA Ops:
  0.0 0.8 %reshape.3 = bf16[72,128]{1,0:T(8,128)(2,1)S(1)} reshape(bf16[1,3,3072]{2,1,0:T(4,128)(2,1)} %param.5) | data formatting | bytes 36864 | tf_op jit(solution)/shard_map/reshape | solution.py:407
  0.8 2.1 %collective-permute-start = (bf16[72,128]{1,0:T(8,128)(2,1)S(1)}, bf16[72,128]{1,0:T(8,128)(2,1)S(1)}, u32[]{:S(2)}, u32[]{:S(2)}) collective-permute-start(bf16[72,128]{1,0:T(8,128)(2,1)S(1)} %reshape.3), channel_id=1, source_target_pairs={{0,8},{1,9},{2,10},{3,11},{4,12},{5,13},{6,14},{7,15},{8,0},{9,1},... | collective-permute-start | bytes 55304 | tf_op jit(solution)/shard_map/ppermute | solution.py:394
  3.6 0.0 copy-start.2
  3.6 0.6 %copy-done.2 = s32[1,3]{1,0:T(1,128)S(1)} copy-done((s32[1,3]{1,0:T(1,128)S(1)}, s32[1,3]{1,0:T(1,128)}, u32[]{:S(2)}) %copy-start.2) | copy-done | bytes 36
  4.2 1.0 %copy-done = bf16[32,1,3,2048]{3,0,2,1:T(8,128)(2,1)S(1)} copy-done((bf16[32,1,3,2048]{3,0,2,1:T(8,128)(2,1)S(1)}, bf16[32,1,3,2048]{3,0,2,1:T(8,128)(2,1)}, u32[]{:S(2)}) %copy-start) | copy-done | bytes 393240
  5.2 0.8 %split.1 = (bf16[3,16,2176]{2,1,0:T(8,128)(2,1)S(1)}, bf16[3,16,2176]{2,1,0:T(8,128)(2,1)S(1)}) custom-call(s32[1]{0:T(128)S(6)} %copy.8.offset_in, s32[1,3]{1,0:T(1,128)S(1)} %copy-done.2, bf16[3,32,2048]{2,1,0:T(8,128)(2,1)S(1)} %bitcast.4), custom_call_target="tpu_custom_call" | custom-call | tf_op jit(solution)/shard_map/split/pallas_call | solution.py:137
  6.1 2.4 %collective-permute-start.2 = (bf16[144,128]{1,0:T(8,128)(2,1)S(1)}, bf16[144,128]{1,0:T(8,128)(2,1)S(1)}, u32[]{:S(2)}, u32[]{:S(2)}) collective-permute-start(bf16[144,128]{1,0:T(8,128)(2,1)S(1)} %pad_maximum_fusion), channel_id=1, source_target_pairs={{0,2},{1,3},{2,0},{3,1},{4,6},{5,7},{6,4},{7,5},{8,10},{9,11},{10,... | collective-permute-start | bytes 110600 | tf_op jit(solution)/shard_map/ppermute | solution.py:394
  8.5 0.2 collective-permute-start.1
  8.7 1.2 %collective-permute-done.2 = bf16[144,128]{1,0:T(8,128)(2,1)S(1)} collective-permute-done((bf16[144,128]{1,0:T(8,128)(2,1)S(1)}, bf16[144,128]{1,0:T(8,128)(2,1)S(1)}, u32[]{:S(2)}, u32[]{:S(2)}) %collective-permute-start.2) | collective-permute-done | bytes 36896 | tf_op jit(solution)/shard_map/ppermute | solution.py:394
  9.9 1.4 %collective-permute-start.3 = (bf16[288,128]{1,0:T(8,128)(2,1)S(1)}, bf16[288,128]{1,0:T(8,128)(2,1)S(1)}, u32[]{:S(2)}, u32[]{:S(2)}) collective-permute-start(bf16[288,128]{1,0:T(8,128)(2,1)S(1)} %constant_dynamic-update-slice_fusion.near), channel_id=1, source_target_pairs={{0,1},{1,0},{2,3},{3,2},{4,5},{5,4},{6,7},{7,6},{8,9},{9,8},{10,11... | collective-permute-start | bytes 221192 | tf_op jit(solution)/shard_map/ppermute | solution.py:394
  11.2 2.2 %collective-permute-done.3.far = bf16[288,128]{1,0:T(8,128)(2,1)S(1)} collective-permute-done((bf16[288,128]{1,0:T(8,128)(2,1)S(1)}, bf16[288,128]{1,0:T(8,128)(2,1)S(1)}, u32[]{:S(2)}, u32[]{:S(2)}) %collective-permute-start.3) | collective-permute-done | bytes 73760 | tf_op jit(solution)/shard_map/ppermute | solution.py:394
  13.4 0.5 %collective-permute-done.1.told.t2 = bf16[3,16,2176]{2,1,0:T(8,128)(2,1)S(1)} collective-permute-done((bf16[3,16,2176]{2,1,0:T(8,128)(2,1)S(1)}, bf16[3,16,2176]{2,1,0:T(8,128)(2,1)S(1)}, u32[]{:S(2)}, u32[]{:S(2)}) %collective-permute-start.1) | collective-permute-done | bytes 208928 | tf_op jit(solution)/shard_map/ppermute | solution.py:394
  13.9 2.5 %collective-permute-start.4 = (bf16[3,16,2176]{2,1,0:T(8,128)(2,1)S(1)}, bf16[3,16,2176]{2,1,0:T(8,128)(2,1)S(1)}, u32[]{:S(2)}, u32[]{:S(2)}) collective-permute-start(bf16[3,16,2176]{2,1,0:T(8,128)(2,1)S(1)} %get-tuple-element.19.own.t0), channel_id=1, source_target_pairs={{0,4},{1,5},{2,6},{3,7},{4,0},{5,1},{6,2},{7,3},{8,12},{9,13},{10,... | collective-permute-start | bytes 626696 | tf_op jit(solution)/shard_map/ppermute | solution.py:394
  16.4 0.0 collective-permute-start.5
  16.4 0.6 %series.1 = (bf16[6,72,128]{2,1,0:T(8,128)(2,1)S(1)}, bf16[6,72,128]{2,1,0:T(8,128)(2,1)S(1)}) custom-call(bf16[3,16,2176]{2,1,0:T(8,128)(2,1)S(1)} %get-tuple-element.19.own.t0, bf16[3,16,2176]{2,1,0:T(8,128)(2,1)S(1)} %collective-permute-done.1.told.t2, bf16[288,128]{1,0:T(8,128)(2,1)S(1)} %constant_dynamic-update-slice_fusion.near, ...), custom_call_target="tpu_custom_call" | custom-call | tf_op jit(solution)/shard_map/series/pallas_call | solution.py:185
  17.0 0.0 copy-start.1
  17.0 0.6 %collective-permute-start.6 = (bf16[6,72,128]{2,1,0:T(8,128)(2,1)S(1)}, bf16[6,72,128]{2,1,0:T(8,128)(2,1)S(1)}, u32[]{:S(2)}, u32[]{:S(2)}) collective-permute-start(bf16[6,72,128]{2,1,0:T(8,128)(2,1)S(1)} %get-tuple-element.22), channel_id=1, source_target_pairs={{0,4},{1,5},{2,6},{3,7},{4,0},{5,1},{6,2},{7,3},{8,12},{9,13},{10,... | collective-permute-start | bytes 331784 | tf_op jit(solution)/shard_map/ppermute | solution.py:394
  17.6 1.0 %collective-permute-done.6.mate = bf16[6,72,128]{2,1,0:T(8,128)(2,1)S(1)} collective-permute-done((bf16[6,72,128]{2,1,0:T(8,128)(2,1)S(1)}, bf16[6,72,128]{2,1,0:T(8,128)(2,1)S(1)}, u32[]{:S(2)}, u32[]{:S(2)}) %collective-permute-start.6) | collective-permute-done | bytes 110624 | tf_op jit(solution)/shard_map/ppermute | solution.py:394
  18.5 8.8 %correlate.1 = (s16[16,3200]{1,0:T(8,128)(2,1)S(1)}, s16[16,3200]{1,0:T(8,128)(2,1)S(1)}) custom-call(bf16[3,16,2176]{2,1,0:T(8,128)(2,1)S(1)} %get-tuple-element.19.own.t0, bf16[3,16,2176]{2,1,0:T(8,128)(2,1)S(1)} %collective-permute-done.4.t1, bf16[3,16,2176]{2,1,0:T(8,128)(2,1)S(1)} %collective-permute-done.1.told.t2, ...), custom_call_target="tpu_custom_call" | custom-call | tf_op jit(solution)/shard_map/correlate/pallas_call | solution.py:370
  27.3 4.5 %collective-permute-start.7 = (s16[16,3200]{1,0:T(8,128)(2,1)S(1)}, s16[16,3200]{1,0:T(8,128)(2,1)S(1)}, u32[]{:S(2)}, u32[]{:S(2)}) collective-permute-start(s16[16,3200]{1,0:T(8,128)(2,1)S(1)} %get-tuple-element.23), channel_id=1, source_target_pairs={{0,0},{1,4},{2,8},{3,12},{4,2},{5,6},{6,10},{7,14},{8,1},{9,5},{10... | collective-permute-start | bytes 307208 | tf_op jit(solution)/shard_map/ppermute | solution.py:399
  31.8 1.3 %collective-permute-start.8 = (s16[16,3200]{1,0:T(8,128)(2,1)S(1)}, s16[16,3200]{1,0:T(8,128)(2,1)S(1)}, u32[]{:S(2)}, u32[]{:S(2)}) collective-permute-start(s16[16,3200]{1,0:T(8,128)(2,1)S(1)} %get-tuple-element.24), channel_id=1, source_target_pairs={{0,1},{1,5},{2,9},{3,13},{4,3},{5,7},{6,11},{7,15},{8,0},{9,4},{10... | collective-permute-start | bytes 307208 | tf_op jit(solution)/shard_map/ppermute | solution.py:399
  33.1 1.2 %collective-permute-done.7.a_ref = s16[16,3200]{1,0:T(8,128)(2,1)S(1)} collective-permute-done((s16[16,3200]{1,0:T(8,128)(2,1)S(1)}, s16[16,3200]{1,0:T(8,128)(2,1)S(1)}, u32[]{:S(2)}, u32[]{:S(2)}) %collective-permute-start.7) | collective-permute-done | bytes 102432 | tf_op jit(solution)/shard_map/ppermute | solution.py:399
  34.3 3.6 %collective-permute-done.8.b_ref = s16[16,3200]{1,0:T(8,128)(2,1)S(1)} collective-permute-done((s16[16,3200]{1,0:T(8,128)(2,1)S(1)}, s16[16,3200]{1,0:T(8,128)(2,1)S(1)}, u32[]{:S(2)}, u32[]{:S(2)}) %collective-permute-start.8) | collective-permute-done | bytes 102432 | tf_op jit(solution)/shard_map/ppermute | solution.py:399
  37.9 1.0 %decode.1 = f32[32,3072]{1,0:T(8,128)} custom-call(s16[16,3200]{1,0:T(8,128)(2,1)S(1)} %collective-permute-done.7.a_ref, s16[16,3200]{1,0:T(8,128)(2,1)S(1)} %collective-permute-done.8.b_ref), custom_call_target="tpu_custom_call" | custom-call | tf_op jit(solution)/shard_map/decode/pallas_call | solution.py:355
  (9 shorter events, 0.0 us)
Async XLA Ops:
  0.8 5.3 %collective-permute-start = (bf16[72,128]{1,0:T(8,128)(2,1)S(1)}, bf16[72,128]{1,0:T(8,128)(2,1)S(1)}, u32[]{:S(2)}, u32[]{:S(2)}) collective-permute-start(bf16[72,128]{1,0:T(8,128)(2,1)S(1)} %reshape.3), channel_id=1, source_target_pairs={{0,8},{1,9},{2,10},{3,11},{4,12},{5,13},{6,14},{7,15},{8,0},{9,1},... | collective-permute-start | bytes 55304 | tf_op jit(solution)/shard_map/ppermute | solution.py:394
  3.6 0.7 %copy-start.2 = (s32[1,3]{1,0:T(1,128)S(1)}, s32[1,3]{1,0:T(1,128)}, u32[]{:S(2)}) copy-start(s32[1,3]{1,0:T(1,128)} %active_in.1) | copy-start | bytes 40
  4.2 1.0 %copy-start = (bf16[32,1,3,2048]{3,0,2,1:T(8,128)(2,1)S(1)}, bf16[32,1,3,2048]{3,0,2,1:T(8,128)(2,1)}, u32[]{:S(2)}) copy-start(bf16[32,1,3,2048]{3,0,2,1:T(8,128)(2,1)} %param.6) | copy-start | bytes 1179652
  6.1 3.8 %collective-permute-start.2 = (bf16[144,128]{1,0:T(8,128)(2,1)S(1)}, bf16[144,128]{1,0:T(8,128)(2,1)S(1)}, u32[]{:S(2)}, u32[]{:S(2)}) collective-permute-start(bf16[144,128]{1,0:T(8,128)(2,1)S(1)} %pad_maximum_fusion), channel_id=1, source_target_pairs={{0,2},{1,3},{2,0},{3,1},{4,6},{5,7},{6,4},{7,5},{8,10},{9,11},{10,... | collective-permute-start | bytes 110600 | tf_op jit(solution)/shard_map/ppermute | solution.py:394
  8.5 5.4 %collective-permute-start.1 = (bf16[3,16,2176]{2,1,0:T(8,128)(2,1)S(1)}, bf16[3,16,2176]{2,1,0:T(8,128)(2,1)S(1)}, u32[]{:S(2)}, u32[]{:S(2)}) collective-permute-start(bf16[3,16,2176]{2,1,0:T(8,128)(2,1)S(1)} %get-tuple-element.17), channel_id=1, source_target_pairs={{0,8},{1,9},{2,10},{3,11},{4,12},{5,13},{6,14},{7,15},{8,0},{9,1},... | collective-permute-start | bytes 626696 | tf_op jit(solution)/shard_map/ppermute | solution.py:394
  9.9 3.6 %collective-permute-start.3 = (bf16[288,128]{1,0:T(8,128)(2,1)S(1)}, bf16[288,128]{1,0:T(8,128)(2,1)S(1)}, u32[]{:S(2)}, u32[]{:S(2)}) collective-permute-start(bf16[288,128]{1,0:T(8,128)(2,1)S(1)} %constant_dynamic-update-slice_fusion.near), channel_id=1, source_target_pairs={{0,1},{1,0},{2,3},{3,2},{4,5},{5,4},{6,7},{7,6},{8,9},{9,8},{10,11... | collective-permute-start | bytes 221192 | tf_op jit(solution)/shard_map/ppermute | solution.py:394
  13.9 4.6 %collective-permute-start.4 = (bf16[3,16,2176]{2,1,0:T(8,128)(2,1)S(1)}, bf16[3,16,2176]{2,1,0:T(8,128)(2,1)S(1)}, u32[]{:S(2)}, u32[]{:S(2)}) collective-permute-start(bf16[3,16,2176]{2,1,0:T(8,128)(2,1)S(1)} %get-tuple-element.19.own.t0), channel_id=1, source_target_pairs={{0,4},{1,5},{2,6},{3,7},{4,0},{5,1},{6,2},{7,3},{8,12},{9,13},{10,... | collective-permute-start | bytes 626696 | tf_op jit(solution)/shard_map/ppermute | solution.py:394
  16.4 2.1 %collective-permute-start.5 = (bf16[3,16,2176]{2,1,0:T(8,128)(2,1)S(1)}, bf16[3,16,2176]{2,1,0:T(8,128)(2,1)S(1)}, u32[]{:S(2)}, u32[]{:S(2)}) collective-permute-start(bf16[3,16,2176]{2,1,0:T(8,128)(2,1)S(1)} %collective-permute-done.1.told.t2), channel_id=1, source_target_pairs={{0,4},{1,5},{2,6},{3,7},{4,0},{5,1},{6,2},{7,3},{8,12},{9,13},{10,... | collective-permute-start | bytes 626696 | tf_op jit(solution)/shard_map/ppermute | solution.py:394
  17.0 1.6 %copy-start.1 = (s32[128,4]{0,1:T(4,128)S(1)}, s32[128,4]{0,1:T(4,128)}, u32[]{:S(2)}) copy-start(s32[128,4]{0,1:T(4,128)} %param.7) | copy-start | bytes 6148
  17.0 1.5 %collective-permute-start.6 = (bf16[6,72,128]{2,1,0:T(8,128)(2,1)S(1)}, bf16[6,72,128]{2,1,0:T(8,128)(2,1)S(1)}, u32[]{:S(2)}, u32[]{:S(2)}) collective-permute-start(bf16[6,72,128]{2,1,0:T(8,128)(2,1)S(1)} %get-tuple-element.22), channel_id=1, source_target_pairs={{0,4},{1,5},{2,6},{3,7},{4,0},{5,1},{6,2},{7,3},{8,12},{9,13},{10,... | collective-permute-start | bytes 331784 | tf_op jit(solution)/shard_map/ppermute | solution.py:394
  27.3 7.0 %collective-permute-start.7 = (s16[16,3200]{1,0:T(8,128)(2,1)S(1)}, s16[16,3200]{1,0:T(8,128)(2,1)S(1)}, u32[]{:S(2)}, u32[]{:S(2)}) collective-permute-start(s16[16,3200]{1,0:T(8,128)(2,1)S(1)} %get-tuple-element.23), channel_id=1, source_target_pairs={{0,0},{1,4},{2,8},{3,12},{4,2},{5,6},{6,10},{7,14},{8,1},{9,5},{10... | collective-permute-start | bytes 307208 | tf_op jit(solution)/shard_map/ppermute | solution.py:399
  31.8 6.1 %collective-permute-start.8 = (s16[16,3200]{1,0:T(8,128)(2,1)S(1)}, s16[16,3200]{1,0:T(8,128)(2,1)S(1)}, u32[]{:S(2)}, u32[]{:S(2)}) collective-permute-start(s16[16,3200]{1,0:T(8,128)(2,1)S(1)} %get-tuple-element.24), channel_id=1, source_target_pairs={{0,1},{1,5},{2,9},{3,13},{4,3},{5,7},{6,11},{7,15},{8,0},{9,4},{10... | collective-permute-start | bytes 307208 | tf_op jit(solution)/shard_map/ppermute | solution.py:399

commit v11 on v9

--- a/solution.py
+++ b/solution.py
@@ -339,27 +339,33 @@
         out[:, 128 * nb :] = jnp.concatenate(levels, axis=0).astype(jnp.int32).astype(jnp.int16)
 
 
-def decode_kernel(a_ref, b_ref, out_ref):
-    odd = lax.axis_index("tgrp") % 2
-    nb = out_ref.shape[1] // 128
-    for ref, half in ((a_ref, odd), (b_ref, 1 - odd)):
-        at = pl.multiple_of(ROWS * half, ROWS)
-        step = jnp.exp2(ref[:, 128 * nb :].astype(jnp.float32) * (1.0 / LEVELS)) * (1.0 / STEPS)
-        for j in range(nb):
-            value = ref[:, 128 * j : 128 * j + 128].astype(jnp.float32)
-            out_ref[pl.ds(at, ROWS), 128 * j : 128 * j + 128] = value * step[:, j : j + 1]
-
-
-def decode(first, second):
-    vmem = pl.BlockSpec(memory_space=pltpu.VMEM)
+def place_kernel(flip, part_ref, *refs):
+    out_ref, block, sem = refs[-3:]
+    half = (lax.axis_index("tgrp") + flip) % 2
+    nb = block.shape[1] // 128
+    step = jnp.exp2(part_ref[:, 128 * nb :].astype(jnp.float32) * (1.0 / LEVELS)) * (1.0 / STEPS)
+    for j in range(nb):
+        value = part_ref[:, 128 * j : 128 * j + 128].astype(jnp.float32)
+        block[:, 128 * j : 128 * j + 128] = value * step[:, j : j + 1]
+    rows = pl.ds(pl.multiple_of(ROWS * half, ROWS), ROWS)
+    copy = pltpu.make_async_copy(block, out_ref.at[rows, :], sem)
+    copy.start()
+    copy.wait()
+
+
+def place(part, flip, *earlier):
+    width = part.shape[1] - 128
+    unread = pl.BlockSpec(memory_space=pl.ANY)
     return pl.pallas_call(
-        decode_kernel,
-        out_shape=jax.ShapeDtypeStruct((2 * ROWS, first.shape[1] - 128), jnp.float32),
-        in_specs=[vmem, vmem],
-        out_specs=vmem,
+        functools.partial(place_kernel, flip),
+        out_shape=jax.ShapeDtypeStruct((2 * ROWS, width), jnp.float32),
+        in_specs=[pl.BlockSpec(memory_space=pltpu.VMEM)] + [unread] * len(earlier),
+        out_specs=unread,
+        scratch_shapes=[pltpu.VMEM((ROWS, width), jnp.float32), pltpu.SemaphoreType.DMA],
+        input_output_aliases={1: 0} if earlier else {},
         compiler_params=pltpu.CompilerParams(vmem_limit_bytes=4 << 20),
-        name="decode",
-    )(first, second)
+        name="place",
+    )(part, *earlier)
 
 
 def correlate_stations(panels, series, masks, span, nb):
@@ -418,7 +424,8 @@
     first, second = correlate_stations(
         (keep, panel_c, panel_y, panel_yc), (mine, mate), masks.T, span, nb
     )
-    return decode(to_owner(first, 0), to_owner(second, 1))
+    first, second = to_owner(first, 0), to_owner(second, 1)
+    return place(second, 1, place(first, 0))
 
 
 def solution(mesh):

time: 38.9 us -> 38.8 us (level)
  waiting for transfers between devices: 7.54 us -> 6.69 us
  Pallas kernels: 11.1 us -> 11.8 us
    ppermute x2, waiting for transfers between devices: 4.8 us -> 3.95 us  [to_owner(): return lax.ppermute(value, ('loop', 'tgrp'), pairs)]
    pallas_call x1 -> x2, Pallas kernels: 0.98 us -> 1.68 us  [place(): pl.pallas_call(functools.partial(place_kernel, flip), out_shape=jax.Shape...]
  transfers between devices with their start and end apart: 9 -> 9, of which waited for: 5 -> 5; matrix products, arithmetic and copies ran while one was open for 0% -> 0% of each run, Pallas kernels for 4% -> 6%
where the time goes in v11:
time: 38.8 us; the launch traced here: 38.4 us
  starting transfers between devices  16.7 us (43%)
  Pallas kernels  11.8 us (30%)
  waiting for transfers between devices  6.69 us (17%)
  local copies, waits for them, and re-layouts  2.43 us (6%)
  between operations  0.75 us (2%)
    ppermute x7, starting transfers between devices, swapped(): return lax.ppermute(value, ('loop', 'tgrp'), pairs)  11.1 us
    pallas_call x1, Pallas kernels, correlate_stations(): pl.pallas_call(functools.partial(correlate_kernel, span, nb), out_shape=(...  8.73 us
    ppermute x2, starting transfers between devices, to_owner(): return lax.ppermute(value, ('loop', 'tgrp'), pairs)  5.61 us
    ppermute x2, waiting for transfers between devices, to_owner(): return lax.ppermute(value, ('loop', 'tgrp'), pairs)  3.95 us
    ppermute x7, waiting for transfers between devices, swapped(): return lax.ppermute(value, ('loop', 'tgrp'), pairs)  2.73 us
    pallas_call x2, Pallas kernels, place(): pl.pallas_call(functools.partial(place_kernel, flip), out_shape=jax.Shape...  1.68 us
    unnamed x8, local copies, waits for them, and re-layouts  1.66 us
    pallas_call x1, Pallas kernels, split(): pl.pallas_call(split_kernel, out_shape=(half, half), in_specs=[pl.BlockSp...  0.84 us
  transfers between devices with their start and end apart: 9, of which 5 were waited for; matrix products, arithmetic and copies ran while one was open for 0% of the time, Pallas kernels for 6%

profile of v11, /device:TPU:1, one launch (start us, length us, event | category | flops | bytes accessed | tf_op | source)
XLA Modules:
  0.0 38.4 jit_solution(10989005575595538542)
XLA Ops:
  0.0 0.8 %reshape.3 = bf16[72,128]{1,0:T(8,128)(2,1)S(1)} reshape(bf16[1,3,3072]{2,1,0:T(4,128)(2,1)} %param.5) | data formatting | bytes 36864 | tf_op jit(solution)/shard_map/reshape | solution.py:414
  0.8 2.1 %collective-permute-start.1 = (bf16[72,128]{1,0:T(8,128)(2,1)S(1)}, bf16[72,128]{1,0:T(8,128)(2,1)S(1)}, u32[]{:S(2)}, u32[]{:S(2)}) collective-permute-start(bf16[72,128]{1,0:T(8,128)(2,1)S(1)} %reshape.3), channel_id=1, source_target_pairs={{0,8},{1,9},{2,10},{3,11},{4,12},{5,13},{6,14},{7,15},{8,0},{9,1},... | collective-permute-start | bytes 55304 | tf_op jit(solution)/shard_map/ppermute | solution.py:400
  3.6 0.0 copy-start.2
  3.6 0.6 %copy-done.2 = s32[1,3]{1,0:T(1,128)S(1)} copy-done((s32[1,3]{1,0:T(1,128)S(1)}, s32[1,3]{1,0:T(1,128)}, u32[]{:S(2)}) %copy-start.2) | copy-done | bytes 36
  4.2 1.0 %copy-done = bf16[32,1,3,2048]{3,0,2,1:T(8,128)(2,1)S(1)} copy-done((bf16[32,1,3,2048]{3,0,2,1:T(8,128)(2,1)S(1)}, bf16[32,1,3,2048]{3,0,2,1:T(8,128)(2,1)}, u32[]{:S(2)}) %copy-start) | copy-done | bytes 393240
  5.2 0.8 %split.1 = (bf16[3,16,2176]{2,1,0:T(8,128)(2,1)S(1)}, bf16[3,16,2176]{2,1,0:T(8,128)(2,1)S(1)}) custom-call(s32[1]{0:T(128)S(6)} %copy.10.offset_in, s32[1,3]{1,0:T(1,128)S(1)} %copy-done.2, bf16[3,32,2048]{2,1,0:T(8,128)(2,1)S(1)} %bitcast.4), custom_call_target="tpu_custom_call" | custom-call | tf_op jit(solution)/shard_map/split/pallas_call | solution.py:137
  6.1 2.4 %collective-permute-start.3 = (bf16[144,128]{1,0:T(8,128)(2,1)S(1)}, bf16[144,128]{1,0:T(8,128)(2,1)S(1)}, u32[]{:S(2)}, u32[]{:S(2)}) collective-permute-start(bf16[144,128]{1,0:T(8,128)(2,1)S(1)} %pad_maximum_fusion), channel_id=1, source_target_pairs={{0,2},{1,3},{2,0},{3,1},{4,6},{5,7},{6,4},{7,5},{8,10},{9,11},{10,... | collective-permute-start | bytes 110600 | tf_op jit(solution)/shard_map/ppermute | solution.py:400
  8.5 0.2 collective-permute-start.2
  8.7 1.2 %collective-permute-done.3 = bf16[144,128]{1,0:T(8,128)(2,1)S(1)} collective-permute-done((bf16[144,128]{1,0:T(8,128)(2,1)S(1)}, bf16[144,128]{1,0:T(8,128)(2,1)S(1)}, u32[]{:S(2)}, u32[]{:S(2)}) %collective-permute-start.3) | collective-permute-done | bytes 36896 | tf_op jit(solution)/shard_map/ppermute | solution.py:400
  9.9 1.4 %collective-permute-start.4 = (bf16[288,128]{1,0:T(8,128)(2,1)S(1)}, bf16[288,128]{1,0:T(8,128)(2,1)S(1)}, u32[]{:S(2)}, u32[]{:S(2)}) collective-permute-start(bf16[288,128]{1,0:T(8,128)(2,1)S(1)} %constant_dynamic-update-slice_fusion.near), channel_id=1, source_target_pairs={{0,1},{1,0},{2,3},{3,2},{4,5},{5,4},{6,7},{7,6},{8,9},{9,8},{10,11... | collective-permute-start | bytes 221192 | tf_op jit(solution)/shard_map/ppermute | solution.py:400
  11.2 2.4 %collective-permute-start = (bf16[3,16,2176]{2,1,0:T(8,128)(2,1)S(1)}, bf16[3,16,2176]{2,1,0:T(8,128)(2,1)S(1)}, u32[]{:S(2)}, u32[]{:S(2)}) collective-permute-start(bf16[3,16,2176]{2,1,0:T(8,128)(2,1)S(1)} %get-tuple-element.14.own.t0), channel_id=1, source_target_pairs={{0,4},{1,5},{2,6},{3,7},{4,0},{5,1},{6,2},{7,3},{8,12},{9,13},{10,... | collective-permute-start | bytes 626696 | tf_op jit(solution)/shard_map/ppermute | solution.py:400
  13.6 0.3 collective-permute-done.2.told.t2
  13.9 2.5 %collective-permute-start.5 = (bf16[3,16,2176]{2,1,0:T(8,128)(2,1)S(1)}, bf16[3,16,2176]{2,1,0:T(8,128)(2,1)S(1)}, u32[]{:S(2)}, u32[]{:S(2)}) collective-permute-start(bf16[3,16,2176]{2,1,0:T(8,128)(2,1)S(1)} %collective-permute-done.2.told.t2), channel_id=1, source_target_pairs={{0,4},{1,5},{2,6},{3,7},{4,0},{5,1},{6,2},{7,3},{8,12},{9,13},{10,... | collective-permute-start | bytes 626696 | tf_op jit(solution)/shard_map/ppermute | solution.py:400
  16.4 0.6 %series.1 = (bf16[6,72,128]{2,1,0:T(8,128)(2,1)S(1)}, bf16[6,72,128]{2,1,0:T(8,128)(2,1)S(1)}) custom-call(bf16[3,16,2176]{2,1,0:T(8,128)(2,1)S(1)} %get-tuple-element.14.own.t0, bf16[3,16,2176]{2,1,0:T(8,128)(2,1)S(1)} %collective-permute-done.2.told.t2, bf16[288,128]{1,0:T(8,128)(2,1)S(1)} %constant_dynamic-update-slice_fusion.near, ...), custom_call_target="tpu_custom_call" | custom-call | tf_op jit(solution)/shard_map/series/pallas_call | solution.py:185
  17.0 0.0 copy-start.1
  17.0 0.1 collective-permute-start.6
  17.1 1.3 %collective-permute-done.6.mate = bf16[6,72,128]{2,1,0:T(8,128)(2,1)S(1)} collective-permute-done((bf16[6,72,128]{2,1,0:T(8,128)(2,1)S(1)}, bf16[6,72,128]{2,1,0:T(8,128)(2,1)S(1)}, u32[]{:S(2)}, u32[]{:S(2)}) %collective-permute-start.6) | collective-permute-done | bytes 110624 | tf_op jit(solution)/shard_map/ppermute | solution.py:400
  18.4 8.7 %correlate.1 = (s16[16,3200]{1,0:T(8,128)(2,1)S(1)}, s16[16,3200]{1,0:T(8,128)(2,1)S(1)}) custom-call(bf16[3,16,2176]{2,1,0:T(8,128)(2,1)S(1)} %get-tuple-element.14.own.t0, bf16[3,16,2176]{2,1,0:T(8,128)(2,1)S(1)} %collective-permute-done.t1, bf16[3,16,2176]{2,1,0:T(8,128)(2,1)S(1)} %collective-permute-done.2.told.t2, ...), custom_call_target="tpu_custom_call" | custom-call | tf_op jit(solution)/shard_map/correlate/pallas_call | solution.py:376
  27.1 4.3 %collective-permute-start.8 = (s16[16,3200]{1,0:T(8,128)(2,1)S(1)}, s16[16,3200]{1,0:T(8,128)(2,1)S(1)}, u32[]{:S(2)}, u32[]{:S(2)}) collective-permute-start(s16[16,3200]{1,0:T(8,128)(2,1)S(1)} %get-tuple-element.22), channel_id=1, source_target_pairs={{0,0},{1,4},{2,8},{3,12},{4,2},{5,6},{6,10},{7,14},{8,1},{9,5},{10... | collective-permute-start | bytes 307208 | tf_op jit(solution)/shard_map/ppermute | solution.py:405
  31.4 1.3 %collective-permute-start.7 = (s16[16,3200]{1,0:T(8,128)(2,1)S(1)}, s16[16,3200]{1,0:T(8,128)(2,1)S(1)}, u32[]{:S(2)}, u32[]{:S(2)}) collective-permute-start(s16[16,3200]{1,0:T(8,128)(2,1)S(1)} %get-tuple-element.21), channel_id=1, source_target_pairs={{0,1},{1,5},{2,9},{3,13},{4,3},{5,7},{6,11},{7,15},{8,0},{9,4},{10... | collective-permute-start | bytes 307208 | tf_op jit(solution)/shard_map/ppermute | solution.py:405
  32.7 1.8 %collective-permute-done.8.part_ref = s16[16,3200]{1,0:T(8,128)(2,1)S(1)} collective-permute-done((s16[16,3200]{1,0:T(8,128)(2,1)S(1)}, s16[16,3200]{1,0:T(8,128)(2,1)S(1)}, u32[]{:S(2)}, u32[]{:S(2)}) %collective-permute-start.8) | collective-permute-done | bytes 102432 | tf_op jit(solution)/shard_map/ppermute | solution.py:405
  34.5 0.8 %place.2.refs_0_ = f32[32,3072]{1,0:T(8,128)} custom-call(s16[16,3200]{1,0:T(8,128)(2,1)S(1)} %collective-permute-done.8.part_ref), custom_call_target="tpu_custom_call" | custom-call | tf_op jit(solution)/shard_map/place/pallas_call | solution.py:359
  35.4 2.2 %collective-permute-done.7.part_ref = s16[16,3200]{1,0:T(8,128)(2,1)S(1)} collective-permute-done((s16[16,3200]{1,0:T(8,128)(2,1)S(1)}, s16[16,3200]{1,0:T(8,128)(2,1)S(1)}, u32[]{:S(2)}, u32[]{:S(2)}) %collective-permute-start.7) | collective-permute-done | bytes 102432 | tf_op jit(solution)/shard_map/ppermute | solution.py:405
  37.5 0.8 %place.3 = f32[32,3072]{1,0:T(8,128)} custom-call(s16[16,3200]{1,0:T(8,128)(2,1)S(1)} %collective-permute-done.7.part_ref, f32[32,3072]{1,0:T(8,128)} %place.2.refs_0_), custom_call_target="tpu_custom_call", output_to_operand_aliasing={{}: (1, {})} | custom-call | tf_op jit(solution)/shard_map/place/pallas_call | solution.py:359
  (10 shorter events, 0.0 us)
Async XLA Ops:
  0.8 5.3 %collective-permute-start.1 = (bf16[72,128]{1,0:T(8,128)(2,1)S(1)}, bf16[72,128]{1,0:T(8,128)(2,1)S(1)}, u32[]{:S(2)}, u32[]{:S(2)}) collective-permute-start(bf16[72,128]{1,0:T(8,128)(2,1)S(1)} %reshape.3), channel_id=1, source_target_pairs={{0,8},{1,9},{2,10},{3,11},{4,12},{5,13},{6,14},{7,15},{8,0},{9,1},... | collective-permute-start | bytes 55304 | tf_op jit(solution)/shard_map/ppermute | solution.py:400
  3.6 0.7 %copy-start.2 = (s32[1,3]{1,0:T(1,128)S(1)}, s32[1,3]{1,0:T(1,128)}, u32[]{:S(2)}) copy-start(s32[1,3]{1,0:T(1,128)} %active_in.1) | copy-start | bytes 40
  4.2 1.0 %copy-start = (bf16[32,1,3,2048]{3,0,2,1:T(8,128)(2,1)S(1)}, bf16[32,1,3,2048]{3,0,2,1:T(8,128)(2,1)}, u32[]{:S(2)}) copy-start(bf16[32,1,3,2048]{3,0,2,1:T(8,128)(2,1)} %param.6) | copy-start | bytes 1179652
  6.1 3.8 %collective-permute-start.3 = (bf16[144,128]{1,0:T(8,128)(2,1)S(1)}, bf16[144,128]{1,0:T(8,128)(2,1)S(1)}, u32[]{:S(2)}, u32[]{:S(2)}) collective-permute-start(bf16[144,128]{1,0:T(8,128)(2,1)S(1)} %pad_maximum_fusion), channel_id=1, source_target_pairs={{0,2},{1,3},{2,0},{3,1},{4,6},{5,7},{6,4},{7,5},{8,10},{9,11},{10,... | collective-permute-start | bytes 110600 | tf_op jit(solution)/shard_map/ppermute | solution.py:400
  8.5 5.4 %collective-permute-start.2 = (bf16[3,16,2176]{2,1,0:T(8,128)(2,1)S(1)}, bf16[3,16,2176]{2,1,0:T(8,128)(2,1)S(1)}, u32[]{:S(2)}, u32[]{:S(2)}) collective-permute-start(bf16[3,16,2176]{2,1,0:T(8,128)(2,1)S(1)} %get-tuple-element.16), channel_id=1, source_target_pairs={{0,8},{1,9},{2,10},{3,11},{4,12},{5,13},{6,14},{7,15},{8,0},{9,1},... | collective-permute-start | bytes 626696 | tf_op jit(solution)/shard_map/ppermute | solution.py:400
  9.9 3.7 %collective-permute-start.4 = (bf16[288,128]{1,0:T(8,128)(2,1)S(1)}, bf16[288,128]{1,0:T(8,128)(2,1)S(1)}, u32[]{:S(2)}, u32[]{:S(2)}) collective-permute-start(bf16[288,128]{1,0:T(8,128)(2,1)S(1)} %constant_dynamic-update-slice_fusion.near), channel_id=1, source_target_pairs={{0,1},{1,0},{2,3},{3,2},{4,5},{5,4},{6,7},{7,6},{8,9},{9,8},{10,11... | collective-permute-start | bytes 221192 | tf_op jit(solution)/shard_map/ppermute | solution.py:400
  11.2 5.8 %collective-permute-start = (bf16[3,16,2176]{2,1,0:T(8,128)(2,1)S(1)}, bf16[3,16,2176]{2,1,0:T(8,128)(2,1)S(1)}, u32[]{:S(2)}, u32[]{:S(2)}) collective-permute-start(bf16[3,16,2176]{2,1,0:T(8,128)(2,1)S(1)} %get-tuple-element.14.own.t0), channel_id=1, source_target_pairs={{0,4},{1,5},{2,6},{3,7},{4,0},{5,1},{6,2},{7,3},{8,12},{9,13},{10,... | collective-permute-start | bytes 626696 | tf_op jit(solution)/shard_map/ppermute | solution.py:400
  13.9 4.5 %collective-permute-start.5 = (bf16[3,16,2176]{2,1,0:T(8,128)(2,1)S(1)}, bf16[3,16,2176]{2,1,0:T(8,128)(2,1)S(1)}, u32[]{:S(2)}, u32[]{:S(2)}) collective-permute-start(bf16[3,16,2176]{2,1,0:T(8,128)(2,1)S(1)} %collective-permute-done.2.told.t2), channel_id=1, source_target_pairs={{0,4},{1,5},{2,6},{3,7},{4,0},{5,1},{6,2},{7,3},{8,12},{9,13},{10,... | collective-permute-start | bytes 626696 | tf_op jit(solution)/shard_map/ppermute | solution.py:400
  17.0 1.4 %copy-start.1 = (s32[128,4]{0,1:T(4,128)S(1)}, s32[128,4]{0,1:T(4,128)}, u32[]{:S(2)}) copy-start(s32[128,4]{0,1:T(4,128)} %param.7) | copy-start | bytes 6148
  17.0 1.4 %collective-permute-start.6 = (bf16[6,72,128]{2,1,0:T(8,128)(2,1)S(1)}, bf16[6,72,128]{2,1,0:T(8,128)(2,1)S(1)}, u32[]{:S(2)}, u32[]{:S(2)}) collective-permute-start(bf16[6,72,128]{2,1,0:T(8,128)(2,1)S(1)} %get-tuple-element.20), channel_id=1, source_target_pairs={{0,4},{1,5},{2,6},{3,7},{4,0},{5,1},{6,2},{7,3},{8,12},{9,13},{10,... | collective-permute-start | bytes 331784 | tf_op jit(solution)/shard_map/ppermute | solution.py:400
  27.1 7.4 %collective-permute-start.8 = (s16[16,3200]{1,0:T(8,128)(2,1)S(1)}, s16[16,3200]{1,0:T(8,128)(2,1)S(1)}, u32[]{:S(2)}, u32[]{:S(2)}) collective-permute-start(s16[16,3200]{1,0:T(8,128)(2,1)S(1)} %get-tuple-element.22), channel_id=1, source_target_pairs={{0,0},{1,4},{2,8},{3,12},{4,2},{5,6},{6,10},{7,14},{8,1},{9,5},{10... | collective-permute-start | bytes 307208 | tf_op jit(solution)/shard_map/ppermute | solution.py:405
  31.4 6.1 %collective-permute-start.7 = (s16[16,3200]{1,0:T(8,128)(2,1)S(1)}, s16[16,3200]{1,0:T(8,128)(2,1)S(1)}, u32[]{:S(2)}, u32[]{:S(2)}) collective-permute-start(s16[16,3200]{1,0:T(8,128)(2,1)S(1)} %get-tuple-element.21), channel_id=1, source_target_pairs={{0,1},{1,5},{2,9},{3,13},{4,3},{5,7},{6,11},{7,15},{8,0},{9,4},{10... | collective-permute-start | bytes 307208 | tf_op jit(solution)/shard_map/ppermute | solution.py:405

commit v12 on v11

--- a/solution.py
+++ b/solution.py
@@ -161,7 +161,7 @@
     for b in range(4):
         at = pl.multiple_of(blocks * (z ^ b), 8)
         for i in range(6):
-            first = 6 * blocks * (b // 2) + i * blocks
+            first = blocks * (6 * (i // 3) + 3 * (b // 2) + i % 3)
             whole[i, pl.ds(at, blocks), :] = wide[b % 2][first : first + blocks]
     for station in range(2):
         words = (own, told)[station]
@@ -412,10 +412,10 @@
     keep, send = split(offsets, active, panel)
     panel_c = swapped(keep, 1, 0)
     pieces = data.reshape(3 * nb, 128)
-    pieces_y, send = lax.optimization_barrier((swapped(pieces, 2, 0), send))
-    pair = jnp.concatenate([pieces, pieces_y], axis=0)
+    pieces_z, send = lax.optimization_barrier((swapped(pieces, 0, 2), send))
+    pair = jnp.concatenate([pieces, pieces_z], axis=0)
     panel_y = swapped(send, 2, 0)
-    near = jnp.concatenate([pair, swapped(pair, 0, 2)], axis=0)
+    near = jnp.concatenate([pair, swapped(pair, 2, 0)], axis=0)
     far = swapped(near, 0, 1)
     mine, mate = make_series(keep, panel_y, near, far, nb, 2 * nb + span // 128 + 8)
     mate = swapped(mate, 1, 0)

time: 38.8 us -> 38.8 us (level)
  the two profiles are of different devices: /device:TPU:1 before, /device:TPU:4 now
where the time goes in v12:
time: 38.8 us; the launch traced here: 38.6 us
  waiting for transfers between devices  13.2 us (34%)
  Pallas kernels  11.8 us (30%)
  starting transfers between devices  10.4 us (27%)
  local copies, waits for them, and re-layouts  2.43 us (6%)
  between operations  0.75 us (2%)
    pallas_call x1, Pallas kernels, correlate_stations(): pl.pallas_call(functools.partial(correlate_kernel, span, nb), out_shape=(...  8.73 us
    ppermute x2, waiting for transfers between devices, to_owner(): return lax.ppermute(value, ('loop', 'tgrp'), pairs)  7.1 us
    ppermute x7, starting transfers between devices, swapped(): return lax.ppermute(value, ('loop', 'tgrp'), pairs)  6.96 us
    ppermute x7, waiting for transfers between devices, swapped(): return lax.ppermute(value, ('loop', 'tgrp'), pairs)  6.11 us
    ppermute x2, starting transfers between devices, to_owner(): return lax.ppermute(value, ('loop', 'tgrp'), pairs)  3.44 us
    pallas_call x2, Pallas kernels, place(): pl.pallas_call(functools.partial(place_kernel, flip), out_shape=jax.Shape...  1.68 us
    unnamed x8, local copies, waits for them, and re-layouts  1.66 us
    pallas_call x1, Pallas kernels, split(): pl.pallas_call(split_kernel, out_shape=(half, half), in_specs=[pl.BlockSp...  0.84 us
  transfers between devices with their start and end apart: 9, of which 4 were waited for; matrix products, arithmetic and copies ran while one was open for 0% of the time, Pallas kernels for 6%

profile of v12, /device:TPU:4, one launch (start us, length us, event | category | flops | bytes accessed | tf_op | source)
XLA Modules:
  0.0 38.6 jit_solution(16911038543435414341)
XLA Ops:
  0.0 0.8 %reshape.3 = bf16[72,128]{1,0:T(8,128)(2,1)S(1)} reshape(bf16[1,3,3072]{2,1,0:T(4,128)(2,1)} %param.5) | data formatting | bytes 36864 | tf_op jit(solution)/shard_map/reshape | solution.py:414
  0.8 2.7 %collective-permute-start.1 = (bf16[72,128]{1,0:T(8,128)(2,1)S(1)}, bf16[72,128]{1,0:T(8,128)(2,1)S(1)}, u32[]{:S(2)}, u32[]{:S(2)}) collective-permute-start(bf16[72,128]{1,0:T(8,128)(2,1)S(1)} %reshape.3), channel_id=1, source_target_pairs={{0,2},{1,3},{2,0},{3,1},{4,6},{5,7},{6,4},{7,5},{8,10},{9,11},{10,... | collective-permute-start | bytes 55304 | tf_op jit(solution)/shard_map/ppermute | solution.py:400
  4.1 0.0 copy-start.2
  4.1 0.6 %copy-done.2 = s32[1,3]{1,0:T(1,128)S(1)} copy-done((s32[1,3]{1,0:T(1,128)S(1)}, s32[1,3]{1,0:T(1,128)}, u32[]{:S(2)}) %copy-start.2) | copy-done | bytes 36
  4.7 1.0 %copy-done = bf16[32,1,3,2048]{3,0,2,1:T(8,128)(2,1)S(1)} copy-done((bf16[32,1,3,2048]{3,0,2,1:T(8,128)(2,1)S(1)}, bf16[32,1,3,2048]{3,0,2,1:T(8,128)(2,1)}, u32[]{:S(2)}) %copy-start) | copy-done | bytes 393240
  5.7 0.8 %split.1 = (bf16[3,16,2176]{2,1,0:T(8,128)(2,1)S(1)}, bf16[3,16,2176]{2,1,0:T(8,128)(2,1)S(1)}) custom-call(s32[1]{0:T(128)S(6)} %copy.10.offset_in, s32[1,3]{1,0:T(1,128)S(1)} %copy-done.2, bf16[3,32,2048]{2,1,0:T(8,128)(2,1)S(1)} %bitcast.4), custom_call_target="tpu_custom_call" | custom-call | tf_op jit(solution)/shard_map/split/pallas_call | solution.py:137
  6.6 0.6 %collective-permute-start.3 = (bf16[144,128]{1,0:T(8,128)(2,1)S(1)}, bf16[144,128]{1,0:T(8,128)(2,1)S(1)}, u32[]{:S(2)}, u32[]{:S(2)}) collective-permute-start(bf16[144,128]{1,0:T(8,128)(2,1)S(1)} %pad_maximum_fusion), channel_id=1, source_target_pairs={{0,8},{1,9},{2,10},{3,11},{4,12},{5,13},{6,14},{7,15},{8,0},{9,1},... | collective-permute-start | bytes 110600 | tf_op jit(solution)/shard_map/ppermute | solution.py:400
  7.2 1.5 %collective-permute-start.2 = (bf16[3,16,2176]{2,1,0:T(8,128)(2,1)S(1)}, bf16[3,16,2176]{2,1,0:T(8,128)(2,1)S(1)}, u32[]{:S(2)}, u32[]{:S(2)}) collective-permute-start(bf16[3,16,2176]{2,1,0:T(8,128)(2,1)S(1)} %get-tuple-element.16), channel_id=1, source_target_pairs={{0,8},{1,9},{2,10},{3,11},{4,12},{5,13},{6,14},{7,15},{8,0},{9,1},... | collective-permute-start | bytes 626696 | tf_op jit(solution)/shard_map/ppermute | solution.py:400
  8.7 2.4 %collective-permute-done.3 = bf16[144,128]{1,0:T(8,128)(2,1)S(1)} collective-permute-done((bf16[144,128]{1,0:T(8,128)(2,1)S(1)}, bf16[144,128]{1,0:T(8,128)(2,1)S(1)}, u32[]{:S(2)}, u32[]{:S(2)}) %collective-permute-start.3) | collective-permute-done | bytes 36896 | tf_op jit(solution)/shard_map/ppermute | solution.py:400
  11.1 1.6 %collective-permute-start.4 = (bf16[288,128]{1,0:T(8,128)(2,1)S(1)}, bf16[288,128]{1,0:T(8,128)(2,1)S(1)}, u32[]{:S(2)}, u32[]{:S(2)}) collective-permute-start(bf16[288,128]{1,0:T(8,128)(2,1)S(1)} %constant_dynamic-update-slice_fusion.near), channel_id=1, source_target_pairs={{0,1},{1,0},{2,3},{3,2},{4,5},{5,4},{6,7},{7,6},{8,9},{9,8},{10,11... | collective-permute-start | bytes 221192 | tf_op jit(solution)/shard_map/ppermute | solution.py:400
  12.7 0.0 collective-permute-start
  12.7 2.8 %collective-permute-done.4.far = bf16[288,128]{1,0:T(8,128)(2,1)S(1)} collective-permute-done((bf16[288,128]{1,0:T(8,128)(2,1)S(1)}, bf16[288,128]{1,0:T(8,128)(2,1)S(1)}, u32[]{:S(2)}, u32[]{:S(2)}) %collective-permute-start.4) | collective-permute-done | bytes 73760 | tf_op jit(solution)/shard_map/ppermute | solution.py:400
  15.5 0.0 collective-permute-done.2.told.t2
  15.5 0.0 collective-permute-start.5
  15.5 0.6 %series.1 = (bf16[6,72,128]{2,1,0:T(8,128)(2,1)S(1)}, bf16[6,72,128]{2,1,0:T(8,128)(2,1)S(1)}) custom-call(bf16[3,16,2176]{2,1,0:T(8,128)(2,1)S(1)} %get-tuple-element.14.own.t0, bf16[3,16,2176]{2,1,0:T(8,128)(2,1)S(1)} %collective-permute-done.2.told.t2, bf16[288,128]{1,0:T(8,128)(2,1)S(1)} %constant_dynamic-update-slice_fusion.near, ...), custom_call_target="tpu_custom_call" | custom-call | tf_op jit(solution)/shard_map/series/pallas_call | solution.py:185
  16.1 0.0 copy-start.1
  16.1 0.6 %collective-permute-start.6 = (bf16[6,72,128]{2,1,0:T(8,128)(2,1)S(1)}, bf16[6,72,128]{2,1,0:T(8,128)(2,1)S(1)}, u32[]{:S(2)}, u32[]{:S(2)}) collective-permute-start(bf16[6,72,128]{2,1,0:T(8,128)(2,1)S(1)} %get-tuple-element.20), channel_id=1, source_target_pairs={{0,4},{1,5},{2,6},{3,7},{4,0},{5,1},{6,2},{7,3},{8,12},{9,13},{10,... | collective-permute-start | bytes 331784 | tf_op jit(solution)/shard_map/ppermute | solution.py:400
  16.7 1.0 %collective-permute-done.6.mate = bf16[6,72,128]{2,1,0:T(8,128)(2,1)S(1)} collective-permute-done((bf16[6,72,128]{2,1,0:T(8,128)(2,1)S(1)}, bf16[6,72,128]{2,1,0:T(8,128)(2,1)S(1)}, u32[]{:S(2)}, u32[]{:S(2)}) %collective-permute-start.6) | collective-permute-done | bytes 110624 | tf_op jit(solution)/shard_map/ppermute | solution.py:400
  17.6 8.7 %correlate.1 = (s16[16,3200]{1,0:T(8,128)(2,1)S(1)}, s16[16,3200]{1,0:T(8,128)(2,1)S(1)}) custom-call(bf16[3,16,2176]{2,1,0:T(8,128)(2,1)S(1)} %get-tuple-element.14.own.t0, bf16[3,16,2176]{2,1,0:T(8,128)(2,1)S(1)} %collective-permute-done.t1, bf16[3,16,2176]{2,1,0:T(8,128)(2,1)S(1)} %collective-permute-done.2.told.t2, ...), custom_call_target="tpu_custom_call" | custom-call | tf_op jit(solution)/shard_map/correlate/pallas_call | solution.py:376
  26.4 3.4 %collective-permute-start.8 = (s16[16,3200]{1,0:T(8,128)(2,1)S(1)}, s16[16,3200]{1,0:T(8,128)(2,1)S(1)}, u32[]{:S(2)}, u32[]{:S(2)}) collective-permute-start(s16[16,3200]{1,0:T(8,128)(2,1)S(1)} %get-tuple-element.22), channel_id=1, source_target_pairs={{0,0},{1,4},{2,8},{3,12},{4,2},{5,6},{6,10},{7,14},{8,1},{9,5},{10... | collective-permute-start | bytes 307208 | tf_op jit(solution)/shard_map/ppermute | solution.py:405
  29.7 0.1 collective-permute-start.7
  29.8 7.1 %collective-permute-done.8.part_ref = s16[16,3200]{1,0:T(8,128)(2,1)S(1)} collective-permute-done((s16[16,3200]{1,0:T(8,128)(2,1)S(1)}, s16[16,3200]{1,0:T(8,128)(2,1)S(1)}, u32[]{:S(2)}, u32[]{:S(2)}) %collective-permute-start.8) | collective-permute-done | bytes 102432 | tf_op jit(solution)/shard_map/ppermute | solution.py:405
  36.9 0.8 %place.2.refs_0_ = f32[32,3072]{1,0:T(8,128)} custom-call(s16[16,3200]{1,0:T(8,128)(2,1)S(1)} %collective-permute-done.8.part_ref), custom_call_target="tpu_custom_call" | custom-call | tf_op jit(solution)/shard_map/place/pallas_call | solution.py:359
  37.8 0.8 %place.3 = f32[32,3072]{1,0:T(8,128)} custom-call(s16[16,3200]{1,0:T(8,128)(2,1)S(1)} %collective-permute-done.7.part_ref, f32[32,3072]{1,0:T(8,128)} %place.2.refs_0_), custom_call_target="tpu_custom_call", output_to_operand_aliasing={{}: (1, {})} | custom-call | tf_op jit(solution)/shard_map/place/pallas_call | solution.py:359
  (10 shorter events, 0.0 us)
Async XLA Ops:
  0.8 5.8 %collective-permute-start.1 = (bf16[72,128]{1,0:T(8,128)(2,1)S(1)}, bf16[72,128]{1,0:T(8,128)(2,1)S(1)}, u32[]{:S(2)}, u32[]{:S(2)}) collective-permute-start(bf16[72,128]{1,0:T(8,128)(2,1)S(1)} %reshape.3), channel_id=1, source_target_pairs={{0,2},{1,3},{2,0},{3,1},{4,6},{5,7},{6,4},{7,5},{8,10},{9,11},{10,... | collective-permute-start | bytes 55304 | tf_op jit(solution)/shard_map/ppermute | solution.py:400
  4.1 0.7 %copy-start.2 = (s32[1,3]{1,0:T(1,128)S(1)}, s32[1,3]{1,0:T(1,128)}, u32[]{:S(2)}) copy-start(s32[1,3]{1,0:T(1,128)} %active_in.1) | copy-start | bytes 40
  4.7 1.0 %copy-start = (bf16[32,1,3,2048]{3,0,2,1:T(8,128)(2,1)S(1)}, bf16[32,1,3,2048]{3,0,2,1:T(8,128)(2,1)}, u32[]{:S(2)}) copy-start(bf16[32,1,3,2048]{3,0,2,1:T(8,128)(2,1)} %param.6) | copy-start | bytes 1179652
  6.6 4.5 %collective-permute-start.3 = (bf16[144,128]{1,0:T(8,128)(2,1)S(1)}, bf16[144,128]{1,0:T(8,128)(2,1)S(1)}, u32[]{:S(2)}, u32[]{:S(2)}) collective-permute-start(bf16[144,128]{1,0:T(8,128)(2,1)S(1)} %pad_maximum_fusion), channel_id=1, source_target_pairs={{0,8},{1,9},{2,10},{3,11},{4,12},{5,13},{6,14},{7,15},{8,0},{9,1},... | collective-permute-start | bytes 110600 | tf_op jit(solution)/shard_map/ppermute | solution.py:400
  7.2 8.3 %collective-permute-start.2 = (bf16[3,16,2176]{2,1,0:T(8,128)(2,1)S(1)}, bf16[3,16,2176]{2,1,0:T(8,128)(2,1)S(1)}, u32[]{:S(2)}, u32[]{:S(2)}) collective-permute-start(bf16[3,16,2176]{2,1,0:T(8,128)(2,1)S(1)} %get-tuple-element.16), channel_id=1, source_target_pairs={{0,8},{1,9},{2,10},{3,11},{4,12},{5,13},{6,14},{7,15},{8,0},{9,1},... | collective-permute-start | bytes 626696 | tf_op jit(solution)/shard_map/ppermute | solution.py:400
  11.1 4.4 %collective-permute-start.4 = (bf16[288,128]{1,0:T(8,128)(2,1)S(1)}, bf16[288,128]{1,0:T(8,128)(2,1)S(1)}, u32[]{:S(2)}, u32[]{:S(2)}) collective-permute-start(bf16[288,128]{1,0:T(8,128)(2,1)S(1)} %constant_dynamic-update-slice_fusion.near), channel_id=1, source_target_pairs={{0,1},{1,0},{2,3},{3,2},{4,5},{5,4},{6,7},{7,6},{8,9},{9,8},{10,11... | collective-permute-start | bytes 221192 | tf_op jit(solution)/shard_map/ppermute | solution.py:400
  12.7 3.9 %collective-permute-start = (bf16[3,16,2176]{2,1,0:T(8,128)(2,1)S(1)}, bf16[3,16,2176]{2,1,0:T(8,128)(2,1)S(1)}, u32[]{:S(2)}, u32[]{:S(2)}) collective-permute-start(bf16[3,16,2176]{2,1,0:T(8,128)(2,1)S(1)} %get-tuple-element.14.own.t0), channel_id=1, source_target_pairs={{0,4},{1,5},{2,6},{3,7},{4,0},{5,1},{6,2},{7,3},{8,12},{9,13},{10,... | collective-permute-start | bytes 626696 | tf_op jit(solution)/shard_map/ppermute | solution.py:400
  15.5 2.1 %collective-permute-start.5 = (bf16[3,16,2176]{2,1,0:T(8,128)(2,1)S(1)}, bf16[3,16,2176]{2,1,0:T(8,128)(2,1)S(1)}, u32[]{:S(2)}, u32[]{:S(2)}) collective-permute-start(bf16[3,16,2176]{2,1,0:T(8,128)(2,1)S(1)} %collective-permute-done.2.told.t2), channel_id=1, source_target_pairs={{0,4},{1,5},{2,6},{3,7},{4,0},{5,1},{6,2},{7,3},{8,12},{9,13},{10,... | collective-permute-start | bytes 626696 | tf_op jit(solution)/shard_map/ppermute | solution.py:400
  16.1 1.6 %copy-start.1 = (s32[128,4]{0,1:T(4,128)S(1)}, s32[128,4]{0,1:T(4,128)}, u32[]{:S(2)}) copy-start(s32[128,4]{0,1:T(4,128)} %param.7) | copy-start | bytes 6148
  16.1 1.5 %collective-permute-start.6 = (bf16[6,72,128]{2,1,0:T(8,128)(2,1)S(1)}, bf16[6,72,128]{2,1,0:T(8,128)(2,1)S(1)}, u32[]{:S(2)}, u32[]{:S(2)}) collective-permute-start(bf16[6,72,128]{2,1,0:T(8,128)(2,1)S(1)} %get-tuple-element.20), channel_id=1, source_target_pairs={{0,4},{1,5},{2,6},{3,7},{4,0},{5,1},{6,2},{7,3},{8,12},{9,13},{10,... | collective-permute-start | bytes 331784 | tf_op jit(solution)/shard_map/ppermute | solution.py:400
  26.4 10.5 %collective-permute-start.8 = (s16[16,3200]{1,0:T(8,128)(2,1)S(1)}, s16[16,3200]{1,0:T(8,128)(2,1)S(1)}, u32[]{:S(2)}, u32[]{:S(2)}) collective-permute-start(s16[16,3200]{1,0:T(8,128)(2,1)S(1)} %get-tuple-element.22), channel_id=1, source_target_pairs={{0,0},{1,4},{2,8},{3,12},{4,2},{5,6},{6,10},{7,14},{8,1},{9,5},{10... | collective-permute-start | bytes 307208 | tf_op jit(solution)/shard_map/ppermute | solution.py:405
  29.7 8.0 %collective-permute-start.7 = (s16[16,3200]{1,0:T(8,128)(2,1)S(1)}, s16[16,3200]{1,0:T(8,128)(2,1)S(1)}, u32[]{:S(2)}, u32[]{:S(2)}) collective-permute-start(s16[16,3200]{1,0:T(8,128)(2,1)S(1)} %get-tuple-element.21), channel_id=1, source_target_pairs={{0,1},{1,5},{2,9},{3,13},{4,3},{5,7},{6,11},{7,15},{8,0},{9,4},{10... | collective-permute-start | bytes 307208 | tf_op jit(solution)/shard_map/ppermute | solution.py:405

commit v13 on v11

--- a/solution.py
+++ b/solution.py
@@ -424,8 +424,8 @@
     first, second = correlate_stations(
         (keep, panel_c, panel_y, panel_yc), (mine, mate), masks.T, span, nb
     )
-    first, second = to_owner(first, 0), to_owner(second, 1)
-    return place(second, 1, place(first, 0))
+    second, first = to_owner(second, 1), to_owner(first, 0)
+    return place(first, 0, place(second, 1))
 
 
 def solution(mesh):

time: 38.8 us -> 38.4 us (0.990)
  the two profiles are of different devices: /device:TPU:1 before, /device:TPU:7 now
where the time goes in v13:
time: 38.4 us; the launch traced here: 38.1 us
  starting transfers between devices  16.8 us (44%)
  Pallas kernels  11.8 us (31%)
  waiting for transfers between devices  6.33 us (16%)
  local copies, waits for them, and re-layouts  2.43 us (6%)
  between operations  0.75 us (2%)
    ppermute x7, starting transfers between devices, swapped(): return lax.ppermute(value, ('loop', 'tgrp'), pairs)  10.2 us
    pallas_call x1, Pallas kernels, correlate_stations(): pl.pallas_call(functools.partial(correlate_kernel, span, nb), out_shape=(...  8.73 us
    ppermute x2, starting transfers between devices, to_owner(): return lax.ppermute(value, ('loop', 'tgrp'), pairs)  6.56 us
    ppermute x2, waiting for transfers between devices, to_owner(): return lax.ppermute(value, ('loop', 'tgrp'), pairs)  4.62 us
    ppermute x7, waiting for transfers between devices, swapped(): return lax.ppermute(value, ('loop', 'tgrp'), pairs)  1.71 us
    pallas_call x2, Pallas kernels, place(): pl.pallas_call(functools.partial(place_kernel, flip), out_shape=jax.Shape...  1.68 us
    unnamed x8, local copies, waits for them, and re-layouts  1.66 us
    pallas_call x1, Pallas kernels, split(): pl.pallas_call(split_kernel, out_shape=(half, half), in_specs=[pl.BlockSp...  0.84 us
  transfers between devices with their start and end apart: 9, of which 5 were waited for; matrix products, arithmetic and copies ran while one was open for 0% of the time, Pallas kernels for 6%

profile of v13, /device:TPU:7, one launch (start us, length us, event | category | flops | bytes accessed | tf_op | source)
XLA Modules:
  0.0 38.1 jit_solution(14275192978012599193)
XLA Ops:
  0.0 0.8 %reshape.3 = bf16[72,128]{1,0:T(8,128)(2,1)S(1)} reshape(bf16[1,3,3072]{2,1,0:T(4,128)(2,1)} %param.5) | data formatting | bytes 36864 | tf_op jit(solution)/shard_map/reshape | solution.py:414
  0.8 0.3 collective-permute-start.1
  1.7 0.0 copy-start.2
  1.7 0.6 %copy-done.2 = s32[1,3]{1,0:T(1,128)S(1)} copy-done((s32[1,3]{1,0:T(1,128)S(1)}, s32[1,3]{1,0:T(1,128)}, u32[]{:S(2)}) %copy-start.2) | copy-done | bytes 36
  2.4 1.0 %copy-done = bf16[32,1,3,2048]{3,0,2,1:T(8,128)(2,1)S(1)} copy-done((bf16[32,1,3,2048]{3,0,2,1:T(8,128)(2,1)S(1)}, bf16[32,1,3,2048]{3,0,2,1:T(8,128)(2,1)}, u32[]{:S(2)}) %copy-start) | copy-done | bytes 393240
  3.4 0.8 %split.1 = (bf16[3,16,2176]{2,1,0:T(8,128)(2,1)S(1)}, bf16[3,16,2176]{2,1,0:T(8,128)(2,1)S(1)}) custom-call(s32[1]{0:T(128)S(6)} %copy.10.offset_in, s32[1,3]{1,0:T(1,128)S(1)} %copy-done.2, bf16[3,32,2048]{2,1,0:T(8,128)(2,1)S(1)} %bitcast.4), custom_call_target="tpu_custom_call" | custom-call | tf_op jit(solution)/shard_map/split/pallas_call | solution.py:137
  4.2 2.4 %collective-permute-start.3 = (bf16[144,128]{1,0:T(8,128)(2,1)S(1)}, bf16[144,128]{1,0:T(8,128)(2,1)S(1)}, u32[]{:S(2)}, u32[]{:S(2)}) collective-permute-start(bf16[144,128]{1,0:T(8,128)(2,1)S(1)} %pad_maximum_fusion), channel_id=1, source_target_pairs={{0,2},{1,3},{2,0},{3,1},{4,6},{5,7},{6,4},{7,5},{8,10},{9,11},{10,... | collective-permute-start | bytes 110600 | tf_op jit(solution)/shard_map/ppermute | solution.py:400
  6.6 1.2 %collective-permute-start.2 = (bf16[3,16,2176]{2,1,0:T(8,128)(2,1)S(1)}, bf16[3,16,2176]{2,1,0:T(8,128)(2,1)S(1)}, u32[]{:S(2)}, u32[]{:S(2)}) collective-permute-start(bf16[3,16,2176]{2,1,0:T(8,128)(2,1)S(1)} %get-tuple-element.16), channel_id=1, source_target_pairs={{0,8},{1,9},{2,10},{3,11},{4,12},{5,13},{6,14},{7,15},{8,0},{9,1},... | collective-permute-start | bytes 626696 | tf_op jit(solution)/shard_map/ppermute | solution.py:400
  7.9 0.1 collective-permute-done.3
  8.0 1.4 %collective-permute-start.4 = (bf16[288,128]{1,0:T(8,128)(2,1)S(1)}, bf16[288,128]{1,0:T(8,128)(2,1)S(1)}, u32[]{:S(2)}, u32[]{:S(2)}) collective-permute-start(bf16[288,128]{1,0:T(8,128)(2,1)S(1)} %constant_dynamic-update-slice_fusion.near), channel_id=1, source_target_pairs={{0,1},{1,0},{2,3},{3,2},{4,5},{5,4},{6,7},{7,6},{8,9},{9,8},{10,11... | collective-permute-start | bytes 221192 | tf_op jit(solution)/shard_map/ppermute | solution.py:400
  9.4 2.4 %collective-permute-start = (bf16[3,16,2176]{2,1,0:T(8,128)(2,1)S(1)}, bf16[3,16,2176]{2,1,0:T(8,128)(2,1)S(1)}, u32[]{:S(2)}, u32[]{:S(2)}) collective-permute-start(bf16[3,16,2176]{2,1,0:T(8,128)(2,1)S(1)} %get-tuple-element.14.own.t0), channel_id=1, source_target_pairs={{0,4},{1,5},{2,6},{3,7},{4,0},{5,1},{6,2},{7,3},{8,12},{9,13},{10,... | collective-permute-start | bytes 626696 | tf_op jit(solution)/shard_map/ppermute | solution.py:400
  11.8 0.3 collective-permute-done.2.told.t2
  12.0 2.5 %collective-permute-start.5 = (bf16[3,16,2176]{2,1,0:T(8,128)(2,1)S(1)}, bf16[3,16,2176]{2,1,0:T(8,128)(2,1)S(1)}, u32[]{:S(2)}, u32[]{:S(2)}) collective-permute-start(bf16[3,16,2176]{2,1,0:T(8,128)(2,1)S(1)} %collective-permute-done.2.told.t2), channel_id=1, source_target_pairs={{0,4},{1,5},{2,6},{3,7},{4,0},{5,1},{6,2},{7,3},{8,12},{9,13},{10,... | collective-permute-start | bytes 626696 | tf_op jit(solution)/shard_map/ppermute | solution.py:400
  14.6 0.6 %series.1 = (bf16[6,72,128]{2,1,0:T(8,128)(2,1)S(1)}, bf16[6,72,128]{2,1,0:T(8,128)(2,1)S(1)}) custom-call(bf16[3,16,2176]{2,1,0:T(8,128)(2,1)S(1)} %get-tuple-element.14.own.t0, bf16[3,16,2176]{2,1,0:T(8,128)(2,1)S(1)} %collective-permute-done.2.told.t2, bf16[288,128]{1,0:T(8,128)(2,1)S(1)} %constant_dynamic-update-slice_fusion.near, ...), custom_call_target="tpu_custom_call" | custom-call | tf_op jit(solution)/shard_map/series/pallas_call | solution.py:185
  15.1 0.0 copy-start.1
  15.1 0.1 collective-permute-start.6
  15.2 1.3 %collective-permute-done.6.mate = bf16[6,72,128]{2,1,0:T(8,128)(2,1)S(1)} collective-permute-done((bf16[6,72,128]{2,1,0:T(8,128)(2,1)S(1)}, bf16[6,72,128]{2,1,0:T(8,128)(2,1)S(1)}, u32[]{:S(2)}, u32[]{:S(2)}) %collective-permute-start.6) | collective-permute-done | bytes 110624 | tf_op jit(solution)/shard_map/ppermute | solution.py:400
  16.5 8.7 %correlate.1 = (s16[16,3200]{1,0:T(8,128)(2,1)S(1)}, s16[16,3200]{1,0:T(8,128)(2,1)S(1)}) custom-call(bf16[3,16,2176]{2,1,0:T(8,128)(2,1)S(1)} %get-tuple-element.14.own.t0, bf16[3,16,2176]{2,1,0:T(8,128)(2,1)S(1)} %collective-permute-done.t1, bf16[3,16,2176]{2,1,0:T(8,128)(2,1)S(1)} %collective-permute-done.2.told.t2, ...), custom_call_target="tpu_custom_call" | custom-call | tf_op jit(solution)/shard_map/correlate/pallas_call | solution.py:376
  25.3 3.4 %collective-permute-start.8 = (s16[16,3200]{1,0:T(8,128)(2,1)S(1)}, s16[16,3200]{1,0:T(8,128)(2,1)S(1)}, u32[]{:S(2)}, u32[]{:S(2)}) collective-permute-start(s16[16,3200]{1,0:T(8,128)(2,1)S(1)} %get-tuple-element.22), channel_id=1, source_target_pairs={{0,1},{1,5},{2,9},{3,13},{4,3},{5,7},{6,11},{7,15},{8,0},{9,4},{10... | collective-permute-start | bytes 307208 | tf_op jit(solution)/shard_map/ppermute | solution.py:405
  28.6 3.2 %collective-permute-start.7 = (s16[16,3200]{1,0:T(8,128)(2,1)S(1)}, s16[16,3200]{1,0:T(8,128)(2,1)S(1)}, u32[]{:S(2)}, u32[]{:S(2)}) collective-permute-start(s16[16,3200]{1,0:T(8,128)(2,1)S(1)} %get-tuple-element.21), channel_id=1, source_target_pairs={{0,0},{1,4},{2,8},{3,12},{4,2},{5,6},{6,10},{7,14},{8,1},{9,5},{10... | collective-permute-start | bytes 307208 | tf_op jit(solution)/shard_map/ppermute | solution.py:405
  31.8 0.2 collective-permute-done.8.part_ref
  32.1 0.8 %place.2.refs_0_ = f32[32,3072]{1,0:T(8,128)} custom-call(s16[16,3200]{1,0:T(8,128)(2,1)S(1)} %collective-permute-done.8.part_ref), custom_call_target="tpu_custom_call" | custom-call | tf_op jit(solution)/shard_map/place/pallas_call | solution.py:359
  32.9 4.4 %collective-permute-done.7.part_ref = s16[16,3200]{1,0:T(8,128)(2,1)S(1)} collective-permute-done((s16[16,3200]{1,0:T(8,128)(2,1)S(1)}, s16[16,3200]{1,0:T(8,128)(2,1)S(1)}, u32[]{:S(2)}, u32[]{:S(2)}) %collective-permute-start.7) | collective-permute-done | bytes 102432 | tf_op jit(solution)/shard_map/ppermute | solution.py:405
  37.3 0.8 %place.3 = f32[32,3072]{1,0:T(8,128)} custom-call(s16[16,3200]{1,0:T(8,128)(2,1)S(1)} %collective-permute-done.7.part_ref, f32[32,3072]{1,0:T(8,128)} %place.2.refs_0_), custom_call_target="tpu_custom_call", output_to_operand_aliasing={{}: (1, {})} | custom-call | tf_op jit(solution)/shard_map/place/pallas_call | solution.py:359
  (10 shorter events, 0.0 us)
Async XLA Ops:
  0.8 3.5 %collective-permute-start.1 = (bf16[72,128]{1,0:T(8,128)(2,1)S(1)}, bf16[72,128]{1,0:T(8,128)(2,1)S(1)}, u32[]{:S(2)}, u32[]{:S(2)}) collective-permute-start(bf16[72,128]{1,0:T(8,128)(2,1)S(1)} %reshape.3), channel_id=1, source_target_pairs={{0,8},{1,9},{2,10},{3,11},{4,12},{5,13},{6,14},{7,15},{8,0},{9,1},... | collective-permute-start | bytes 55304 | tf_op jit(solution)/shard_map/ppermute | solution.py:400
  1.7 0.7 %copy-start.2 = (s32[1,3]{1,0:T(1,128)S(1)}, s32[1,3]{1,0:T(1,128)}, u32[]{:S(2)}) copy-start(s32[1,3]{1,0:T(1,128)} %active_in.1) | copy-start | bytes 40
  2.4 1.0 %copy-start = (bf16[32,1,3,2048]{3,0,2,1:T(8,128)(2,1)S(1)}, bf16[32,1,3,2048]{3,0,2,1:T(8,128)(2,1)}, u32[]{:S(2)}) copy-start(bf16[32,1,3,2048]{3,0,2,1:T(8,128)(2,1)} %param.6) | copy-start | bytes 1179652
  4.2 3.8 %collective-permute-start.3 = (bf16[144,128]{1,0:T(8,128)(2,1)S(1)}, bf16[144,128]{1,0:T(8,128)(2,1)S(1)}, u32[]{:S(2)}, u32[]{:S(2)}) collective-permute-start(bf16[144,128]{1,0:T(8,128)(2,1)S(1)} %pad_maximum_fusion), channel_id=1, source_target_pairs={{0,2},{1,3},{2,0},{3,1},{4,6},{5,7},{6,4},{7,5},{8,10},{9,11},{10,... | collective-permute-start | bytes 110600 | tf_op jit(solution)/shard_map/ppermute | solution.py:400
  6.6 5.4 %collective-permute-start.2 = (bf16[3,16,2176]{2,1,0:T(8,128)(2,1)S(1)}, bf16[3,16,2176]{2,1,0:T(8,128)(2,1)S(1)}, u32[]{:S(2)}, u32[]{:S(2)}) collective-permute-start(bf16[3,16,2176]{2,1,0:T(8,128)(2,1)S(1)} %get-tuple-element.16), channel_id=1, source_target_pairs={{0,8},{1,9},{2,10},{3,11},{4,12},{5,13},{6,14},{7,15},{8,0},{9,1},... | collective-permute-start | bytes 626696 | tf_op jit(solution)/shard_map/ppermute | solution.py:400
  8.0 3.8 %collective-permute-start.4 = (bf16[288,128]{1,0:T(8,128)(2,1)S(1)}, bf16[288,128]{1,0:T(8,128)(2,1)S(1)}, u32[]{:S(2)}, u32[]{:S(2)}) collective-permute-start(bf16[288,128]{1,0:T(8,128)(2,1)S(1)} %constant_dynamic-update-slice_fusion.near), channel_id=1, source_target_pairs={{0,1},{1,0},{2,3},{3,2},{4,5},{5,4},{6,7},{7,6},{8,9},{9,8},{10,11... | collective-permute-start | bytes 221192 | tf_op jit(solution)/shard_map/ppermute | solution.py:400
  9.4 5.8 %collective-permute-start = (bf16[3,16,2176]{2,1,0:T(8,128)(2,1)S(1)}, bf16[3,16,2176]{2,1,0:T(8,128)(2,1)S(1)}, u32[]{:S(2)}, u32[]{:S(2)}) collective-permute-start(bf16[3,16,2176]{2,1,0:T(8,128)(2,1)S(1)} %get-tuple-element.14.own.t0), channel_id=1, source_target_pairs={{0,4},{1,5},{2,6},{3,7},{4,0},{5,1},{6,2},{7,3},{8,12},{9,13},{10,... | collective-permute-start | bytes 626696 | tf_op jit(solution)/shard_map/ppermute | solution.py:400
  12.0 4.5 %collective-permute-start.5 = (bf16[3,16,2176]{2,1,0:T(8,128)(2,1)S(1)}, bf16[3,16,2176]{2,1,0:T(8,128)(2,1)S(1)}, u32[]{:S(2)}, u32[]{:S(2)}) collective-permute-start(bf16[3,16,2176]{2,1,0:T(8,128)(2,1)S(1)} %collective-permute-done.2.told.t2), channel_id=1, source_target_pairs={{0,4},{1,5},{2,6},{3,7},{4,0},{5,1},{6,2},{7,3},{8,12},{9,13},{10,... | collective-permute-start | bytes 626696 | tf_op jit(solution)/shard_map/ppermute | solution.py:400
  15.1 1.4 %copy-start.1 = (s32[128,4]{0,1:T(4,128)S(1)}, s32[128,4]{0,1:T(4,128)}, u32[]{:S(2)}) copy-start(s32[128,4]{0,1:T(4,128)} %param.7) | copy-start | bytes 6148
  15.1 1.4 %collective-permute-start.6 = (bf16[6,72,128]{2,1,0:T(8,128)(2,1)S(1)}, bf16[6,72,128]{2,1,0:T(8,128)(2,1)S(1)}, u32[]{:S(2)}, u32[]{:S(2)}) collective-permute-start(bf16[6,72,128]{2,1,0:T(8,128)(2,1)S(1)} %get-tuple-element.20), channel_id=1, source_target_pairs={{0,4},{1,5},{2,6},{3,7},{4,0},{5,1},{6,2},{7,3},{8,12},{9,13},{10,... | collective-permute-start | bytes 331784 | tf_op jit(solution)/shard_map/ppermute | solution.py:400
  25.3 6.8 %collective-permute-start.8 = (s16[16,3200]{1,0:T(8,128)(2,1)S(1)}, s16[16,3200]{1,0:T(8,128)(2,1)S(1)}, u32[]{:S(2)}, u32[]{:S(2)}) collective-permute-start(s16[16,3200]{1,0:T(8,128)(2,1)S(1)} %get-tuple-element.22), channel_id=1, source_target_pairs={{0,1},{1,5},{2,9},{3,13},{4,3},{5,7},{6,11},{7,15},{8,0},{9,4},{10... | collective-permute-start | bytes 307208 | tf_op jit(solution)/shard_map/ppermute | solution.py:405
  28.6 8.7 %collective-permute-start.7 = (s16[16,3200]{1,0:T(8,128)(2,1)S(1)}, s16[16,3200]{1,0:T(8,128)(2,1)S(1)}, u32[]{:S(2)}, u32[]{:S(2)}) collective-permute-start(s16[16,3200]{1,0:T(8,128)(2,1)S(1)} %get-tuple-element.21), channel_id=1, source_target_pairs={{0,0},{1,4},{2,8},{3,12},{4,2},{5,6},{6,10},{7,14},{8,1},{9,5},{10... | collective-permute-start | bytes 307208 | tf_op jit(solution)/shard_map/ppermute | solution.py:405

commit v14 on v13

--- a/solution.py
+++ b/solution.py
@@ -340,17 +340,21 @@
 
 
 def place_kernel(flip, part_ref, *refs):
-    out_ref, block, sem = refs[-3:]
+    out_ref, block, sems = refs[-3:]
     half = (lax.axis_index("tgrp") + flip) % 2
     nb = block.shape[1] // 128
     step = jnp.exp2(part_ref[:, 128 * nb :].astype(jnp.float32) * (1.0 / LEVELS)) * (1.0 / STEPS)
-    for j in range(nb):
-        value = part_ref[:, 128 * j : 128 * j + 128].astype(jnp.float32)
-        block[:, 128 * j : 128 * j + 128] = value * step[:, j : j + 1]
     rows = pl.ds(pl.multiple_of(ROWS * half, ROWS), ROWS)
-    copy = pltpu.make_async_copy(block, out_ref.at[rows, :], sem)
-    copy.start()
-    copy.wait()
+    copies = []
+    for chunk, (low, high) in enumerate(((0, nb // 2), (nb // 2, nb))):
+        for j in range(low, high):
+            value = part_ref[:, 128 * j : 128 * j + 128].astype(jnp.float32)
+            block[:, 128 * j : 128 * j + 128] = value * step[:, j : j + 1]
+        columns = pl.ds(128 * low, 128 * (high - low))
+        copies.append(pltpu.make_async_copy(block.at[:, columns], out_ref.at[rows, columns], sems.at[chunk]))
+        copies[-1].start()
+    for copy in copies:
+        copy.wait()
 
 
 def place(part, flip, *earlier):
@@ -361,7 +365,7 @@
         out_shape=jax.ShapeDtypeStruct((2 * ROWS, width), jnp.float32),
         in_specs=[pl.BlockSpec(memory_space=pltpu.VMEM)] + [unread] * len(earlier),
         out_specs=unread,
-        scratch_shapes=[pltpu.VMEM((ROWS, width), jnp.float32), pltpu.SemaphoreType.DMA],
+        scratch_shapes=[pltpu.VMEM((ROWS, width), jnp.float32), pltpu.SemaphoreType.DMA((2,))],
         input_output_aliases={1: 0} if earlier else {},
         compiler_params=pltpu.CompilerParams(vmem_limit_bytes=4 << 20),
         name="place",

time: 38.4 us -> 38.4 us (level)
  no operation moved by 1% of the time
where the time goes in v14:
time: 38.4 us; the launch traced here: 38.1 us
  starting transfers between devices  16.8 us (44%)
  Pallas kernels  11.8 us (31%)
  waiting for transfers between devices  6.35 us (17%)
  local copies, waits for them, and re-layouts  2.43 us (6%)
  between operations  0.75 us (2%)
    ppermute x7, starting transfers between devices, swapped(): return lax.ppermute(value, ('loop', 'tgrp'), pairs)  10.2 us
    pallas_call x1, Pallas kernels, correlate_stations(): pl.pallas_call(functools.partial(correlate_kernel, span, nb), out_shape=(...  8.73 us
    ppermute x2, starting transfers between devices, to_owner(): return lax.ppermute(value, ('loop', 'tgrp'), pairs)  6.56 us
    ppermute x2, waiting for transfers between devices, to_owner(): return lax.ppermute(value, ('loop', 'tgrp'), pairs)  4.65 us
    ppermute x7, waiting for transfers between devices, swapped(): return lax.ppermute(value, ('loop', 'tgrp'), pairs)  1.71 us
    unnamed x8, local copies, waits for them, and re-layouts  1.66 us
    pallas_call x2, Pallas kernels, place(): pl.pallas_call(functools.partial(place_kernel, flip), out_shape=jax.Shape...  1.62 us
    pallas_call x1, Pallas kernels, split(): pl.pallas_call(split_kernel, out_shape=(half, half), in_specs=[pl.BlockSp...  0.84 us
  transfers between devices with their start and end apart: 9, of which 5 were waited for; matrix products, arithmetic and copies ran while one was open for 0% of the time, Pallas kernels for 6%

profile of v14, /device:TPU:7, one launch (start us, length us, event | category | flops | bytes accessed | tf_op | source)
XLA Modules:
  0.0 38.1 jit_solution(16530257334613064136)
XLA Ops:
  0.0 0.8 %reshape.3 = bf16[72,128]{1,0:T(8,128)(2,1)S(1)} reshape(bf16[1,3,3072]{2,1,0:T(4,128)(2,1)} %param.5) | data formatting | bytes 36864 | tf_op jit(solution)/shard_map/reshape | solution.py:418
  0.8 0.3 collective-permute-start.1
  1.7 0.0 copy-start.2
  1.7 0.6 %copy-done.2 = s32[1,3]{1,0:T(1,128)S(1)} copy-done((s32[1,3]{1,0:T(1,128)S(1)}, s32[1,3]{1,0:T(1,128)}, u32[]{:S(2)}) %copy-start.2) | copy-done | bytes 36
  2.4 1.0 %copy-done = bf16[32,1,3,2048]{3,0,2,1:T(8,128)(2,1)S(1)} copy-done((bf16[32,1,3,2048]{3,0,2,1:T(8,128)(2,1)S(1)}, bf16[32,1,3,2048]{3,0,2,1:T(8,128)(2,1)}, u32[]{:S(2)}) %copy-start) | copy-done | bytes 393240
  3.4 0.8 %split.1 = (bf16[3,16,2176]{2,1,0:T(8,128)(2,1)S(1)}, bf16[3,16,2176]{2,1,0:T(8,128)(2,1)S(1)}) custom-call(s32[1]{0:T(128)S(6)} %copy.10.offset_in, s32[1,3]{1,0:T(1,128)S(1)} %copy-done.2, bf16[3,32,2048]{2,1,0:T(8,128)(2,1)S(1)} %bitcast.4), custom_call_target="tpu_custom_call" | custom-call | tf_op jit(solution)/shard_map/split/pallas_call | solution.py:137
  4.2 2.4 %collective-permute-start.3 = (bf16[144,128]{1,0:T(8,128)(2,1)S(1)}, bf16[144,128]{1,0:T(8,128)(2,1)S(1)}, u32[]{:S(2)}, u32[]{:S(2)}) collective-permute-start(bf16[144,128]{1,0:T(8,128)(2,1)S(1)} %pad_maximum_fusion), channel_id=1, source_target_pairs={{0,2},{1,3},{2,0},{3,1},{4,6},{5,7},{6,4},{7,5},{8,10},{9,11},{10,... | collective-permute-start | bytes 110600 | tf_op jit(solution)/shard_map/ppermute | solution.py:404
  6.6 1.2 %collective-permute-start.2 = (bf16[3,16,2176]{2,1,0:T(8,128)(2,1)S(1)}, bf16[3,16,2176]{2,1,0:T(8,128)(2,1)S(1)}, u32[]{:S(2)}, u32[]{:S(2)}) collective-permute-start(bf16[3,16,2176]{2,1,0:T(8,128)(2,1)S(1)} %get-tuple-element.16), channel_id=1, source_target_pairs={{0,8},{1,9},{2,10},{3,11},{4,12},{5,13},{6,14},{7,15},{8,0},{9,1},... | collective-permute-start | bytes 626696 | tf_op jit(solution)/shard_map/ppermute | solution.py:404
  7.9 0.1 collective-permute-done.3
  8.0 1.4 %collective-permute-start.4 = (bf16[288,128]{1,0:T(8,128)(2,1)S(1)}, bf16[288,128]{1,0:T(8,128)(2,1)S(1)}, u32[]{:S(2)}, u32[]{:S(2)}) collective-permute-start(bf16[288,128]{1,0:T(8,128)(2,1)S(1)} %constant_dynamic-update-slice_fusion.near), channel_id=1, source_target_pairs={{0,1},{1,0},{2,3},{3,2},{4,5},{5,4},{6,7},{7,6},{8,9},{9,8},{10,11... | collective-permute-start | bytes 221192 | tf_op jit(solution)/shard_map/ppermute | solution.py:404
  9.4 2.4 %collective-permute-start = (bf16[3,16,2176]{2,1,0:T(8,128)(2,1)S(1)}, bf16[3,16,2176]{2,1,0:T(8,128)(2,1)S(1)}, u32[]{:S(2)}, u32[]{:S(2)}) collective-permute-start(bf16[3,16,2176]{2,1,0:T(8,128)(2,1)S(1)} %get-tuple-element.14.own.t0), channel_id=1, source_target_pairs={{0,4},{1,5},{2,6},{3,7},{4,0},{5,1},{6,2},{7,3},{8,12},{9,13},{10,... | collective-permute-start | bytes 626696 | tf_op jit(solution)/shard_map/ppermute | solution.py:404
  11.8 0.3 collective-permute-done.2.told.t2
  12.0 2.5 %collective-permute-start.5 = (bf16[3,16,2176]{2,1,0:T(8,128)(2,1)S(1)}, bf16[3,16,2176]{2,1,0:T(8,128)(2,1)S(1)}, u32[]{:S(2)}, u32[]{:S(2)}) collective-permute-start(bf16[3,16,2176]{2,1,0:T(8,128)(2,1)S(1)} %collective-permute-done.2.told.t2), channel_id=1, source_target_pairs={{0,4},{1,5},{2,6},{3,7},{4,0},{5,1},{6,2},{7,3},{8,12},{9,13},{10,... | collective-permute-start | bytes 626696 | tf_op jit(solution)/shard_map/ppermute | solution.py:404
  14.6 0.6 %series.1 = (bf16[6,72,128]{2,1,0:T(8,128)(2,1)S(1)}, bf16[6,72,128]{2,1,0:T(8,128)(2,1)S(1)}) custom-call(bf16[3,16,2176]{2,1,0:T(8,128)(2,1)S(1)} %get-tuple-element.14.own.t0, bf16[3,16,2176]{2,1,0:T(8,128)(2,1)S(1)} %collective-permute-done.2.told.t2, bf16[288,128]{1,0:T(8,128)(2,1)S(1)} %constant_dynamic-update-slice_fusion.near, ...), custom_call_target="tpu_custom_call" | custom-call | tf_op jit(solution)/shard_map/series/pallas_call | solution.py:185
  15.1 0.0 copy-start.1
  15.1 0.1 collective-permute-start.6
  15.2 1.3 %collective-permute-done.6.mate = bf16[6,72,128]{2,1,0:T(8,128)(2,1)S(1)} collective-permute-done((bf16[6,72,128]{2,1,0:T(8,128)(2,1)S(1)}, bf16[6,72,128]{2,1,0:T(8,128)(2,1)S(1)}, u32[]{:S(2)}, u32[]{:S(2)}) %collective-permute-start.6) | collective-permute-done | bytes 110624 | tf_op jit(solution)/shard_map/ppermute | solution.py:404
  16.5 8.7 %correlate.1 = (s16[16,3200]{1,0:T(8,128)(2,1)S(1)}, s16[16,3200]{1,0:T(8,128)(2,1)S(1)}) custom-call(bf16[3,16,2176]{2,1,0:T(8,128)(2,1)S(1)} %get-tuple-element.14.own.t0, bf16[3,16,2176]{2,1,0:T(8,128)(2,1)S(1)} %collective-permute-done.t1, bf16[3,16,2176]{2,1,0:T(8,128)(2,1)S(1)} %collective-permute-done.2.told.t2, ...), custom_call_target="tpu_custom_call" | custom-call | tf_op jit(solution)/shard_map/correlate/pallas_call | solution.py:380
  25.3 3.4 %collective-permute-start.8 = (s16[16,3200]{1,0:T(8,128)(2,1)S(1)}, s16[16,3200]{1,0:T(8,128)(2,1)S(1)}, u32[]{:S(2)}, u32[]{:S(2)}) collective-permute-start(s16[16,3200]{1,0:T(8,128)(2,1)S(1)} %get-tuple-element.22), channel_id=1, source_target_pairs={{0,1},{1,5},{2,9},{3,13},{4,3},{5,7},{6,11},{7,15},{8,0},{9,4},{10... | collective-permute-start | bytes 307208 | tf_op jit(solution)/shard_map/ppermute | solution.py:409
  28.6 3.2 %collective-permute-start.7 = (s16[16,3200]{1,0:T(8,128)(2,1)S(1)}, s16[16,3200]{1,0:T(8,128)(2,1)S(1)}, u32[]{:S(2)}, u32[]{:S(2)}) collective-permute-start(s16[16,3200]{1,0:T(8,128)(2,1)S(1)} %get-tuple-element.21), channel_id=1, source_target_pairs={{0,0},{1,4},{2,8},{3,12},{4,2},{5,6},{6,10},{7,14},{8,1},{9,5},{10... | collective-permute-start | bytes 307208 | tf_op jit(solution)/shard_map/ppermute | solution.py:409
  31.8 0.2 collective-permute-done.8.part_ref
  32.1 0.8 %place.2.refs_0_ = f32[32,3072]{1,0:T(8,128)} custom-call(s16[16,3200]{1,0:T(8,128)(2,1)S(1)} %collective-permute-done.8.part_ref), custom_call_target="tpu_custom_call" | custom-call | tf_op jit(solution)/shard_map/place/pallas_call | solution.py:363
  32.9 4.4 %collective-permute-done.7.part_ref = s16[16,3200]{1,0:T(8,128)(2,1)S(1)} collective-permute-done((s16[16,3200]{1,0:T(8,128)(2,1)S(1)}, s16[16,3200]{1,0:T(8,128)(2,1)S(1)}, u32[]{:S(2)}, u32[]{:S(2)}) %collective-permute-start.7) | collective-permute-done | bytes 102432 | tf_op jit(solution)/shard_map/ppermute | solution.py:409
  37.3 0.8 %place.3 = f32[32,3072]{1,0:T(8,128)} custom-call(s16[16,3200]{1,0:T(8,128)(2,1)S(1)} %collective-permute-done.7.part_ref, f32[32,3072]{1,0:T(8,128)} %place.2.refs_0_), custom_call_target="tpu_custom_call", output_to_operand_aliasing={{}: (1, {})} | custom-call | tf_op jit(solution)/shard_map/place/pallas_call | solution.py:363
  (10 shorter events, 0.0 us)
Async XLA Ops:
  0.8 3.5 %collective-permute-start.1 = (bf16[72,128]{1,0:T(8,128)(2,1)S(1)}, bf16[72,128]{1,0:T(8,128)(2,1)S(1)}, u32[]{:S(2)}, u32[]{:S(2)}) collective-permute-start(bf16[72,128]{1,0:T(8,128)(2,1)S(1)} %reshape.3), channel_id=1, source_target_pairs={{0,8},{1,9},{2,10},{3,11},{4,12},{5,13},{6,14},{7,15},{8,0},{9,1},... | collective-permute-start | bytes 55304 | tf_op jit(solution)/shard_map/ppermute | solution.py:404
  1.7 0.7 %copy-start.2 = (s32[1,3]{1,0:T(1,128)S(1)}, s32[1,3]{1,0:T(1,128)}, u32[]{:S(2)}) copy-start(s32[1,3]{1,0:T(1,128)} %active_in.1) | copy-start | bytes 40
  2.4 1.0 %copy-start = (bf16[32,1,3,2048]{3,0,2,1:T(8,128)(2,1)S(1)}, bf16[32,1,3,2048]{3,0,2,1:T(8,128)(2,1)}, u32[]{:S(2)}) copy-start(bf16[32,1,3,2048]{3,0,2,1:T(8,128)(2,1)} %param.6) | copy-start | bytes 1179652
  4.2 3.8 %collective-permute-start.3 = (bf16[144,128]{1,0:T(8,128)(2,1)S(1)}, bf16[144,128]{1,0:T(8,128)(2,1)S(1)}, u32[]{:S(2)}, u32[]{:S(2)}) collective-permute-start(bf16[144,128]{1,0:T(8,128)(2,1)S(1)} %pad_maximum_fusion), channel_id=1, source_target_pairs={{0,2},{1,3},{2,0},{3,1},{4,6},{5,7},{6,4},{7,5},{8,10},{9,11},{10,... | collective-permute-start | bytes 110600 | tf_op jit(solution)/shard_map/ppermute | solution.py:404
  6.6 5.4 %collective-permute-start.2 = (bf16[3,16,2176]{2,1,0:T(8,128)(2,1)S(1)}, bf16[3,16,2176]{2,1,0:T(8,128)(2,1)S(1)}, u32[]{:S(2)}, u32[]{:S(2)}) collective-permute-start(bf16[3,16,2176]{2,1,0:T(8,128)(2,1)S(1)} %get-tuple-element.16), channel_id=1, source_target_pairs={{0,8},{1,9},{2,10},{3,11},{4,12},{5,13},{6,14},{7,15},{8,0},{9,1},... | collective-permute-start | bytes 626696 | tf_op jit(solution)/shard_map/ppermute | solution.py:404
  8.0 3.8 %collective-permute-start.4 = (bf16[288,128]{1,0:T(8,128)(2,1)S(1)}, bf16[288,128]{1,0:T(8,128)(2,1)S(1)}, u32[]{:S(2)}, u32[]{:S(2)}) collective-permute-start(bf16[288,128]{1,0:T(8,128)(2,1)S(1)} %constant_dynamic-update-slice_fusion.near), channel_id=1, source_target_pairs={{0,1},{1,0},{2,3},{3,2},{4,5},{5,4},{6,7},{7,6},{8,9},{9,8},{10,11... | collective-permute-start | bytes 221192 | tf_op jit(solution)/shard_map/ppermute | solution.py:404
  9.4 5.8 %collective-permute-start = (bf16[3,16,2176]{2,1,0:T(8,128)(2,1)S(1)}, bf16[3,16,2176]{2,1,0:T(8,128)(2,1)S(1)}, u32[]{:S(2)}, u32[]{:S(2)}) collective-permute-start(bf16[3,16,2176]{2,1,0:T(8,128)(2,1)S(1)} %get-tuple-element.14.own.t0), channel_id=1, source_target_pairs={{0,4},{1,5},{2,6},{3,7},{4,0},{5,1},{6,2},{7,3},{8,12},{9,13},{10,... | collective-permute-start | bytes 626696 | tf_op jit(solution)/shard_map/ppermute | solution.py:404
  12.0 4.5 %collective-permute-start.5 = (bf16[3,16,2176]{2,1,0:T(8,128)(2,1)S(1)}, bf16[3,16,2176]{2,1,0:T(8,128)(2,1)S(1)}, u32[]{:S(2)}, u32[]{:S(2)}) collective-permute-start(bf16[3,16,2176]{2,1,0:T(8,128)(2,1)S(1)} %collective-permute-done.2.told.t2), channel_id=1, source_target_pairs={{0,4},{1,5},{2,6},{3,7},{4,0},{5,1},{6,2},{7,3},{8,12},{9,13},{10,... | collective-permute-start | bytes 626696 | tf_op jit(solution)/shard_map/ppermute | solution.py:404
  15.1 1.4 %copy-start.1 = (s32[128,4]{0,1:T(4,128)S(1)}, s32[128,4]{0,1:T(4,128)}, u32[]{:S(2)}) copy-start(s32[128,4]{0,1:T(4,128)} %param.7) | copy-start | bytes 6148
  15.1 1.4 %collective-permute-start.6 = (bf16[6,72,128]{2,1,0:T(8,128)(2,1)S(1)}, bf16[6,72,128]{2,1,0:T(8,128)(2,1)S(1)}, u32[]{:S(2)}, u32[]{:S(2)}) collective-permute-start(bf16[6,72,128]{2,1,0:T(8,128)(2,1)S(1)} %get-tuple-element.20), channel_id=1, source_target_pairs={{0,4},{1,5},{2,6},{3,7},{4,0},{5,1},{6,2},{7,3},{8,12},{9,13},{10,... | collective-permute-start | bytes 331784 | tf_op jit(solution)/shard_map/ppermute | solution.py:404
  25.3 6.8 %collective-permute-start.8 = (s16[16,3200]{1,0:T(8,128)(2,1)S(1)}, s16[16,3200]{1,0:T(8,128)(2,1)S(1)}, u32[]{:S(2)}, u32[]{:S(2)}) collective-permute-start(s16[16,3200]{1,0:T(8,128)(2,1)S(1)} %get-tuple-element.22), channel_id=1, source_target_pairs={{0,1},{1,5},{2,9},{3,13},{4,3},{5,7},{6,11},{7,15},{8,0},{9,4},{10... | collective-permute-start | bytes 307208 | tf_op jit(solution)/shard_map/ppermute | solution.py:409
  28.6 8.7 %collective-permute-start.7 = (s16[16,3200]{1,0:T(8,128)(2,1)S(1)}, s16[16,3200]{1,0:T(8,128)(2,1)S(1)}, u32[]{:S(2)}, u32[]{:S(2)}) collective-permute-start(s16[16,3200]{1,0:T(8,128)(2,1)S(1)} %get-tuple-element.21), channel_id=1, source_target_pairs={{0,0},{1,4},{2,8},{3,12},{4,2},{5,6},{6,10},{7,14},{8,1},{9,5},{10... | collective-permute-start | bytes 307208 | tf_op jit(solution)/shard_map/ppermute | solution.py:409
